TPU v7x, 256 devices: a whole 4x4x8 slice. The times are simulated.
256 devices in a mesh: tm: 16 (over z, core), block: 16 (over x, y).
Axes of the slice: x: 4, y: 4, z: 8, core: 2. Of those that a mesh axis runs over, the one named last changes fastest.
Arguments:
- state: float32 [16, 4, 256, 2048], P('tm', None, None, 'block'), may hold values from -6 to 6
- far_field: float32 [16, 4, 2048], P('tm', None, 'block'), may hold values from -6 to 6
- face_index: int32 [16, 2048], P('tm', 'block'), may hold values from 0 to 1023, as said below
- face_weight: float32 [16, 4, 2048], P('tm', None, 'block'), may hold values from 0.05 to 0.45
- mean_flow: float32 [2, 2], replicated, may hold values from -0.6 to 0.6
Outputs:
- new_state: float32 [16, 4, 256, 2048], P('tm', None, None, 'block')
Inputs may be any that keep to these rules, and one draw needn't show every extreme that they name: `face_index`: each face's index points into the opposite row's 8 * 128 interface faces laid end to end; the 4 faces read wrap around that cycle. At each level, the faces of one blade row take distinct first indices, every face of the opposite row exactly once.
All inputs are finite; a program needn't handle non-finite values.
Results may differ from a plain program's by a relative error of at most 0.00016.
Values sent between devices are 32-bit elements; how exact they have to be, the bound alone decides.
No kernel may reach another device: no remote copies, remote signals or barrier semaphores. Data moves between devices by JAX's collectives and lax.ppermute only.
A program may use at most 64 MiB of HBM per device.

v0:
```python
import jax
import jax.numpy as jnp
from jax import lax
from jax.sharding import PartitionSpec as P

SECTION_FACTORS = (0.075, 0.05, 0.1125, 0.15, 0.3)
OMEGA = 1.0
DISSIPATION = 0.2


def joined_along(pieces, dim):
    pieces = jnp.moveaxis(pieces, 0, dim)
    lengths = pieces.shape
    return pieces.reshape(*lengths[:dim], lengths[dim] * lengths[dim + 1], *lengths[dim + 2 :])


def gather_together(arrays, axis, dims):
    flat = jnp.concatenate([a.reshape(-1) for a in arrays])
    lines, at, done = (lax.all_gather(flat, axis), 0, [])
    for a, dim in zip(arrays, dims):
        pieces = lines[:, at : at + a.size].reshape(-1, *a.shape)
        done.append(joined_along(pieces, dim))
        at += a.size
    return tuple(done)


def derivative_matrix(count):
    index = jnp.arange(count)
    offsets = index[:, None] - index[None, :]
    angle = jnp.pi * offsets.astype(jnp.float32) / count
    parity_sign = 1.0 - 2.0 * (offsets % 2).astype(jnp.float32)
    safe_angle = jnp.where(offsets == 0, 0.5 * jnp.pi, angle)
    cotangent = jnp.cos(safe_angle) / jnp.sin(safe_angle)
    return jnp.where(offsets == 0, 0.0, 0.5 * parity_sign * cotangent)


def interface_ghost(faces, table, weight, row_side, width):
    level_count = faces.shape[0]
    cycle_size = faces.shape[2] // 2
    grid = faces.reshape(level_count, 4, 2, cycle_size)
    other = jnp.take(grid, 1 - row_side, axis=2)
    shape = (level_count, 4, width)
    total = jnp.zeros(shape, jnp.float32)
    for offset in range(weight.shape[1]):
        source = (table + offset) % cycle_size
        picked = jnp.take_along_axis(other, jnp.broadcast_to(source[:, None, :], shape), axis=2)
        total = total + weight[:, offset][:, None, :] * picked
    return total


def pitch_neighbours(last_all, first_all):
    half_count = lax.axis_size("block") // 2
    place = lax.axis_index("block")
    row_start = place // half_count * half_count
    in_row = place % half_count
    lower_place = row_start + (in_row + half_count - 1) % half_count
    upper_place = row_start + (in_row + 1) % half_count
    lower_col = lax.dynamic_slice_in_dim(last_all, lower_place, 1, 3)
    upper_col = lax.dynamic_slice_in_dim(first_all, upper_place, 1, 3)
    return (lower_col, upper_col)


def residual(field, lower_ghost, upper_ghost, lower_col, upper_col, speeds):
    speed_u = speeds[0]
    speed_v = speeds[1]
    padded_i = jnp.concatenate([lower_ghost[:, :, None], field, upper_ghost[:, :, None]], axis=2)
    padded_j = jnp.concatenate([lower_col, field, upper_col], axis=3)
    diff_i = padded_i[:, :, 2:] - padded_i[:, :, :-2]
    diff_j = padded_j[..., 2:] - padded_j[..., :-2]
    laplace = (
        padded_i[:, :, 2:]
        - 2.0 * field
        + padded_i[:, :, :-2]
        + (padded_j[..., 2:] - 2.0 * field + padded_j[..., :-2])
    )
    flux_i = jnp.stack(
        [
            speed_u * diff_i[:, 0] + diff_i[:, 1],
            speed_u * diff_i[:, 1] + diff_i[:, 3],
            speed_u * diff_i[:, 2],
            speed_u * diff_i[:, 3] + diff_i[:, 1],
        ],
        axis=1,
    )
    flux_j = jnp.stack(
        [
            speed_v * diff_j[:, 0] + diff_j[:, 2],
            speed_v * diff_j[:, 1],
            speed_v * diff_j[:, 2] + diff_j[:, 3],
            speed_v * diff_j[:, 3] + diff_j[:, 2],
        ],
        axis=1,
    )
    return 0.5 * (flux_i + flux_j) - DISSIPATION * laplace


def shards(state, far_field, face_index, face_weight, mean_flow):
    tm_count = lax.axis_size("tm")
    row_side = lax.axis_index("block") // (lax.axis_size("block") // 2)
    level_here = state.shape[0]
    row_count = state.shape[2]
    width = state.shape[3]
    spectral = derivative_matrix(level_here * tm_count)
    speeds = jnp.take(mean_flow, row_side, axis=0)
    field = state
    for factor in SECTION_FACTORS:
        sent = jnp.where(row_side == 0, field[:, :, row_count - 1], field[:, :, 0])
        face_gathered, last_all, first_all = gather_together(
            (sent[:, :, None, :], field[..., -1:], field[..., :1]), "block", (3, 3, 3)
        )
        faces = face_gathered.reshape(level_here, 4, -1)
        lower_col, upper_col = pitch_neighbours(last_all, first_all)
        ghost = interface_ghost(faces, face_index, face_weight, row_side, width)
        lower_ghost = jnp.where(row_side == 0, far_field, ghost)
        upper_ghost = jnp.where(row_side == 0, ghost, far_field)
        flux = residual(field, lower_ghost, upper_ghost, lower_col, upper_col, speeds)
        applied = jnp.einsum(
            "nm,mvij->nvij",
            spectral,
            lax.all_to_all(field, "tm", split_axis=2, concat_axis=0, tiled=True),
            precision=lax.Precision.HIGHEST,
        )
        deriv = lax.all_to_all(applied, "tm", split_axis=0, concat_axis=2, tiled=True)
        field = state - factor * (flux + OMEGA * deriv)
    return field


def solution(mesh):
    in_specs = (
        P("tm", None, None, "block"),
        P("tm", None, "block"),
        P("tm", "block"),
        P("tm", None, "block"),
        P(),
    )
    out_specs = P("tm", None, None, "block")
    return jax.shard_map(shards, mesh=mesh, in_specs=in_specs, out_specs=out_specs, check_vma=False)
```

profile of v0, /device:TPU:1, one launch (start us, length us, event | category | flops | bytes accessed | tf_op | source)
XLA Modules:
  0.0 387.8 jit_solution(15861849240728194838)
XLA Ops:
  2.2 10.1 %all-to-all-start = ((f32[1,4,256,128]{3,1,0,2:T(4,128)}), f32[1,4,256,128]{3,1,0,2:T(4,128)S(1)}, u32[]{:S(2)}, u32[]{:S(2)}) async-start(f32[1,4,256,128]{3,1,0,2:T(4,128)} %copy.96), calls=%async_computation | async-start | bytes 1048576 | tf_op jit(solution)/shard_map/all_to_all | solution.py:120
  12.9 19.8 %all-gather.5 = f32[16,1,2560]{2,1,0:T(1,128)S(1)} all-gather(f32[1,1,2560]{2,1,0:T(1,128)S(1)} %reshape.1411), channel_id=2, replica_groups=mesh['tm'=16,'block'=16] {'block'}, dimensions={0}, use_global_device_ids=true | all-gather | bytes 174080 | tf_op jit(solution)/shard_map/all_gather | solution.py:19
  33.5 4.8 %gather_fusion.3 = f32[512]{0:T(512)S(1)} fusion(f32[4,1024]{1,0:T(4,128)S(1)} %select_bitcast_fusion.4, s32[512]{0:T(512)S(1)} %get-tuple-element.136), kind=kCustom, calls=%fused_computation.3.clone | custom fusion | bytes 8192 | tf_op jit(solution)/shard_map/jit(take_along_axis)/gather | solution.py:46
  38.4 4.8 %gather_fusion.2 = f32[512]{0:T(512)S(1)} fusion(f32[4,1024]{1,0:T(4,128)S(1)} %select_bitcast_fusion.4, s32[512]{0:T(512)S(1)} %get-tuple-element.135), kind=kCustom, calls=%fused_computation.2.clone | custom fusion | bytes 8192 | tf_op jit(solution)/shard_map/jit(take_along_axis)/gather | solution.py:46
  43.3 4.8 %gather_fusion.1 = f32[512]{0:T(512)S(1)} fusion(f32[4,1024]{1,0:T(4,128)S(1)} %select_bitcast_fusion.4, s32[512]{0:T(512)S(1)} %get-tuple-element.134), kind=kCustom, calls=%fused_computation.1.clone | custom fusion | bytes 8192 | tf_op jit(solution)/shard_map/jit(take_along_axis)/gather | solution.py:46
  48.1 4.8 %gather_fusion = f32[512]{0:T(512)S(1)} fusion(f32[4,1024]{1,0:T(4,128)S(1)} %select_bitcast_fusion.4, s32[512]{0:T(512)S(1)} %get-tuple-element.133), kind=kCustom, calls=%fused_computation.clone | custom fusion | bytes 8192 | tf_op jit(solution)/shard_map/jit(take_along_axis)/gather | solution.py:46
  56.2 11.6 %all-to-all-start.1 = ((f32[16,4,16,128]{3,2,1,0:T(8,128)}), f32[16,4,16,128]{3,2,1,0:T(8,128)S(1)}, u32[]{:S(2)}, u32[]{:S(2)}) async-start(f32[16,4,16,128]{3,2,1,0:T(8,128)} %copy.99), calls=%async_computation.1 | async-start | bytes 1048576 | tf_op jit(solution)/shard_map/all_to_all | solution.py:123
  71.5 13.6 %all-to-all-done.1 = f32[16,4,16,128]{3,2,1,0:T(8,128)S(1)} async-done(((f32[16,4,16,128]{3,2,1,0:T(8,128)}), f32[16,4,16,128]{3,2,1,0:T(8,128)S(1)}, u32[]{:S(2)}, u32[]{:S(2)}) %all-to-all-start.1) | async-done | bytes 524320 | tf_op jit(solution)/shard_map/all_to_all | solution.py:123
  91.8 18.6 %all-gather.6 = f32[16,1,2560]{2,1,0:T(1,128)S(1)} all-gather(f32[1,1,2560]{2,1,0:T(1,128)S(1)} %reshape.1413), channel_id=3, replica_groups=mesh['tm'=16,'block'=16] {'block'}, dimensions={0}, use_global_device_ids=true | all-gather | bytes 174080 | tf_op jit(solution)/shard_map/all_gather | solution.py:19
  110.5 4.8 %gather_fusion.7 = f32[512]{0:T(512)S(1)} fusion(f32[4,1024]{1,0:T(4,128)S(1)} %select_bitcast_fusion.3, s32[512]{0:T(512)S(1)} %get-tuple-element.136), kind=kCustom, calls=%fused_computation.7.clone | custom fusion | bytes 8192 | tf_op jit(solution)/shard_map/jit(take_along_axis)/gather | solution.py:46
  115.4 4.8 %gather_fusion.6 = f32[512]{0:T(512)S(1)} fusion(f32[4,1024]{1,0:T(4,128)S(1)} %select_bitcast_fusion.3, s32[512]{0:T(512)S(1)} %get-tuple-element.135), kind=kCustom, calls=%fused_computation.6.clone | custom fusion | bytes 8192 | tf_op jit(solution)/shard_map/jit(take_along_axis)/gather | solution.py:46
  120.2 4.8 %gather_fusion.5 = f32[512]{0:T(512)S(1)} fusion(f32[4,1024]{1,0:T(4,128)S(1)} %select_bitcast_fusion.3, s32[512]{0:T(512)S(1)} %get-tuple-element.134), kind=kCustom, calls=%fused_computation.5.clone | custom fusion | bytes 8192 | tf_op jit(solution)/shard_map/jit(take_along_axis)/gather | solution.py:46
  125.1 4.8 %gather_fusion.4 = f32[512]{0:T(512)S(1)} fusion(f32[4,1024]{1,0:T(4,128)S(1)} %select_bitcast_fusion.3, s32[512]{0:T(512)S(1)} %get-tuple-element.133), kind=kCustom, calls=%fused_computation.4.clone | custom fusion | bytes 8192 | tf_op jit(solution)/shard_map/jit(take_along_axis)/gather | solution.py:46
  132.3 11.1 %all-to-all-start.3 = ((f32[16,4,16,128]{3,2,1,0:T(8,128)}), f32[16,4,16,128]{3,2,1,0:T(8,128)S(1)}, u32[]{:S(2)}, u32[]{:S(2)}) async-start(f32[16,4,16,128]{3,2,1,0:T(8,128)} %copy.112), calls=%async_computation.3 | async-start | bytes 1048576 | tf_op jit(solution)/shard_map/all_to_all | solution.py:123
  146.9 13.9 %all-to-all-done.3 = f32[16,4,16,128]{3,2,1,0:T(8,128)S(1)} async-done(((f32[16,4,16,128]{3,2,1,0:T(8,128)}), f32[16,4,16,128]{3,2,1,0:T(8,128)S(1)}, u32[]{:S(2)}, u32[]{:S(2)}) %all-to-all-start.3) | async-done | bytes 524320 | tf_op jit(solution)/shard_map/all_to_all | solution.py:123
  167.7 17.1 %all-gather.7 = f32[16,1,2560]{2,1,0:T(1,128)S(1)} all-gather(f32[1,1,2560]{2,1,0:T(1,128)S(1)} %reshape.1415), channel_id=4, replica_groups=mesh['tm'=16,'block'=16] {'block'}, dimensions={0}, use_global_device_ids=true | all-gather | bytes 174080 | tf_op jit(solution)/shard_map/all_gather | solution.py:19
  184.9 4.8 %gather_fusion.11 = f32[512]{0:T(512)S(1)} fusion(f32[4,1024]{1,0:T(4,128)S(1)} %select_bitcast_fusion.2, s32[512]{0:T(512)S(1)} %get-tuple-element.136), kind=kCustom, calls=%fused_computation.11.clone | custom fusion | bytes 8192 | tf_op jit(solution)/shard_map/jit(take_along_axis)/gather | solution.py:46
  189.8 4.8 %gather_fusion.10 = f32[512]{0:T(512)S(1)} fusion(f32[4,1024]{1,0:T(4,128)S(1)} %select_bitcast_fusion.2, s32[512]{0:T(512)S(1)} %get-tuple-element.135), kind=kCustom, calls=%fused_computation.10.clone | custom fusion | bytes 8192 | tf_op jit(solution)/shard_map/jit(take_along_axis)/gather | solution.py:46
  194.6 4.8 %gather_fusion.9 = f32[512]{0:T(512)S(1)} fusion(f32[4,1024]{1,0:T(4,128)S(1)} %select_bitcast_fusion.2, s32[512]{0:T(512)S(1)} %get-tuple-element.134), kind=kCustom, calls=%fused_computation.9.clone | custom fusion | bytes 8192 | tf_op jit(solution)/shard_map/jit(take_along_axis)/gather | solution.py:46
  199.5 4.8 %gather_fusion.8 = f32[512]{0:T(512)S(1)} fusion(f32[4,1024]{1,0:T(4,128)S(1)} %select_bitcast_fusion.2, s32[512]{0:T(512)S(1)} %get-tuple-element.133), kind=kCustom, calls=%fused_computation.8.clone | custom fusion | bytes 8192 | tf_op jit(solution)/shard_map/jit(take_along_axis)/gather | solution.py:46
  206.7 11.1 %all-to-all-start.5 = ((f32[16,4,16,128]{3,2,1,0:T(8,128)}), f32[16,4,16,128]{3,2,1,0:T(8,128)S(1)}, u32[]{:S(2)}, u32[]{:S(2)}) async-start(f32[16,4,16,128]{3,2,1,0:T(8,128)} %copy.125), calls=%async_computation.5 | async-start | bytes 1048576 | tf_op jit(solution)/shard_map/all_to_all | solution.py:123
  221.2 13.9 %all-to-all-done.5 = f32[16,4,16,128]{3,2,1,0:T(8,128)S(1)} async-done(((f32[16,4,16,128]{3,2,1,0:T(8,128)}), f32[16,4,16,128]{3,2,1,0:T(8,128)S(1)}, u32[]{:S(2)}, u32[]{:S(2)}) %all-to-all-start.5) | async-done | bytes 524320 | tf_op jit(solution)/shard_map/all_to_all | solution.py:123
  242.1 18.8 %all-gather.8 = f32[16,1,2560]{2,1,0:T(1,128)S(1)} all-gather(f32[1,1,2560]{2,1,0:T(1,128)S(1)} %reshape.1417), channel_id=5, replica_groups=mesh['tm'=16,'block'=16] {'block'}, dimensions={0}, use_global_device_ids=true | all-gather | bytes 174080 | tf_op jit(solution)/shard_map/all_gather | solution.py:19
  260.9 4.8 %gather_fusion.15 = f32[512]{0:T(512)S(1)} fusion(f32[4,1024]{1,0:T(4,128)S(1)} %select_bitcast_fusion.1, s32[512]{0:T(512)S(1)} %get-tuple-element.136), kind=kCustom, calls=%fused_computation.15.clone | custom fusion | bytes 8192 | tf_op jit(solution)/shard_map/jit(take_along_axis)/gather | solution.py:46
  265.8 4.8 %gather_fusion.14 = f32[512]{0:T(512)S(1)} fusion(f32[4,1024]{1,0:T(4,128)S(1)} %select_bitcast_fusion.1, s32[512]{0:T(512)S(1)} %get-tuple-element.135), kind=kCustom, calls=%fused_computation.14.clone | custom fusion | bytes 8192 | tf_op jit(solution)/shard_map/jit(take_along_axis)/gather | solution.py:46
  270.6 4.8 %gather_fusion.13 = f32[512]{0:T(512)S(1)} fusion(f32[4,1024]{1,0:T(4,128)S(1)} %select_bitcast_fusion.1, s32[512]{0:T(512)S(1)} %get-tuple-element.134), kind=kCustom, calls=%fused_computation.13.clone | custom fusion | bytes 8192 | tf_op jit(solution)/shard_map/jit(take_along_axis)/gather | solution.py:46
  275.5 4.8 %gather_fusion.12 = f32[512]{0:T(512)S(1)} fusion(f32[4,1024]{1,0:T(4,128)S(1)} %select_bitcast_fusion.1, s32[512]{0:T(512)S(1)} %get-tuple-element.133), kind=kCustom, calls=%fused_computation.12.clone | custom fusion | bytes 8192 | tf_op jit(solution)/shard_map/jit(take_along_axis)/gather | solution.py:46
  282.8 11.1 %all-to-all-start.7 = ((f32[16,4,16,128]{3,2,1,0:T(8,128)}), f32[16,4,16,128]{3,2,1,0:T(8,128)S(1)}, u32[]{:S(2)}, u32[]{:S(2)}) async-start(f32[16,4,16,128]{3,2,1,0:T(8,128)} %copy.138), calls=%async_computation.7 | async-start | bytes 1048576 | tf_op jit(solution)/shard_map/all_to_all | solution.py:123
  297.3 13.9 %all-to-all-done.7 = f32[16,4,16,128]{3,2,1,0:T(8,128)S(1)} async-done(((f32[16,4,16,128]{3,2,1,0:T(8,128)}), f32[16,4,16,128]{3,2,1,0:T(8,128)S(1)}, u32[]{:S(2)}, u32[]{:S(2)}) %all-to-all-start.7) | async-done | bytes 524320 | tf_op jit(solution)/shard_map/all_to_all | solution.py:123
  318.1 17.1 %all-gather.9 = f32[16,1,2560]{2,1,0:T(1,128)S(1)} all-gather(f32[1,1,2560]{2,1,0:T(1,128)S(1)} %reshape.1419), channel_id=6, replica_groups=mesh['tm'=16,'block'=16] {'block'}, dimensions={0}, use_global_device_ids=true | all-gather | bytes 174080 | tf_op jit(solution)/shard_map/all_gather | solution.py:19
  357.1 11.1 %all-to-all-start.9 = ((f32[16,4,16,128]{3,2,1,0:T(8,128)}), f32[16,4,16,128]{3,2,1,0:T(8,128)S(1)}, u32[]{:S(2)}, u32[]{:S(2)}) async-start(f32[16,4,16,128]{3,2,1,0:T(8,128)} %copy.150), calls=%async_computation.9 | async-start | bytes 1048576 | tf_op jit(solution)/shard_map/all_to_all | solution.py:123
  370.9 14.7 %all-to-all-done.9 = f32[16,4,16,128]{3,2,1,0:T(8,128)S(1)} async-done(((f32[16,4,16,128]{3,2,1,0:T(8,128)}), f32[16,4,16,128]{3,2,1,0:T(8,128)S(1)}, u32[]{:S(2)}, u32[]{:S(2)}) %all-to-all-start.9) | async-done | bytes 524320 | tf_op jit(solution)/shard_map/all_to_all | solution.py:123
  (212 shorter events, 81.5 us)
Async XLA Ops:
  2.2 10.1 %copy-start = (f32[1,4,256,128]{3,2,1,0:T(8,128)S(1)}, f32[1,4,256,128]{3,2,1,0:T(8,128)}, u32[]{:S(2)}) copy-start(f32[1,4,256,128]{3,2,1,0:T(8,128)} %param.9) | copy-start | bytes 1572868
  2.2 52.3 %all-to-all-start = ((f32[1,4,256,128]{3,1,0,2:T(4,128)}), f32[1,4,256,128]{3,1,0,2:T(4,128)S(1)}, u32[]{:S(2)}, u32[]{:S(2)}) async-start(f32[1,4,256,128]{3,1,0,2:T(4,128)} %copy.96), calls=%async_computation | async-start | bytes 1048576 | tf_op jit(solution)/shard_map/all_to_all | solution.py:120
  56.2 11.6 %copy-start.26 = (f32[2,2]{1,0:T(2,128)S(1)}, f32[2,2]{1,0:T(2,128)}, u32[]{:S(2)}) copy-start(f32[2,2]{1,0:T(2,128)} %param.13) | copy-start | bytes 52
  56.2 28.9 %all-to-all-start.1 = ((f32[16,4,16,128]{3,2,1,0:T(8,128)}), f32[16,4,16,128]{3,2,1,0:T(8,128)S(1)}, u32[]{:S(2)}, u32[]{:S(2)}) async-start(f32[16,4,16,128]{3,2,1,0:T(8,128)} %copy.99), calls=%async_computation.1 | async-start | bytes 1048576 | tf_op jit(solution)/shard_map/all_to_all | solution.py:123
  85.2 0.9 copy-start.21
  85.2 1.0 copy-start.22
  87.8 42.8 %all-to-all-start.2 = ((f32[1,4,256,128]{3,1,0,2:T(4,128)}), f32[1,4,256,128]{3,1,0,2:T(4,128)S(1)}, u32[]{:S(2)}, u32[]{:S(2)}) async-start(f32[1,4,256,128]{3,1,0,2:T(4,128)} %copy.109), calls=%async_computation.2 | async-start | bytes 1048576 | tf_op jit(solution)/shard_map/all_to_all | solution.py:120
  132.3 28.4 %all-to-all-start.3 = ((f32[16,4,16,128]{3,2,1,0:T(8,128)}), f32[16,4,16,128]{3,2,1,0:T(8,128)S(1)}, u32[]{:S(2)}, u32[]{:S(2)}) async-start(f32[16,4,16,128]{3,2,1,0:T(8,128)} %copy.112), calls=%async_computation.3 | async-start | bytes 1048576 | tf_op jit(solution)/shard_map/all_to_all | solution.py:123
  160.8 0.9 copy-start.1
  160.8 1.0 copy-start.2
  160.8 1.0 copy-start.9
  160.8 1.1 copy-start.10
  160.8 1.2 copy-start.11
  160.8 1.2 copy-start.12
  163.7 41.2 %all-to-all-start.4 = ((f32[1,4,256,128]{3,1,0,2:T(4,128)}), f32[1,4,256,128]{3,1,0,2:T(4,128)S(1)}, u32[]{:S(2)}, u32[]{:S(2)}) async-start(f32[1,4,256,128]{3,1,0,2:T(4,128)} %copy.122), calls=%async_computation.4 | async-start | bytes 1048576 | tf_op jit(solution)/shard_map/all_to_all | solution.py:120
  206.7 28.4 %all-to-all-start.5 = ((f32[16,4,16,128]{3,2,1,0:T(8,128)}), f32[16,4,16,128]{3,2,1,0:T(8,128)S(1)}, u32[]{:S(2)}, u32[]{:S(2)}) async-start(f32[16,4,16,128]{3,2,1,0:T(8,128)} %copy.125), calls=%async_computation.5 | async-start | bytes 1048576 | tf_op jit(solution)/shard_map/all_to_all | solution.py:123
  235.1 0.9 copy-start.3
  235.1 1.0 copy-start.4
  235.1 1.0 copy-start.13
  235.1 1.1 copy-start.14
  235.1 1.2 copy-start.15
  235.1 1.2 copy-start.16
  238.0 43.0 %all-to-all-start.6 = ((f32[1,4,256,128]{3,1,0,2:T(4,128)}), f32[1,4,256,128]{3,1,0,2:T(4,128)S(1)}, u32[]{:S(2)}, u32[]{:S(2)}) async-start(f32[1,4,256,128]{3,1,0,2:T(4,128)} %copy.135), calls=%async_computation.6 | async-start | bytes 1048576 | tf_op jit(solution)/shard_map/all_to_all | solution.py:120
  282.8 28.4 %all-to-all-start.7 = ((f32[16,4,16,128]{3,2,1,0:T(8,128)}), f32[16,4,16,128]{3,2,1,0:T(8,128)S(1)}, u32[]{:S(2)}, u32[]{:S(2)}) async-start(f32[16,4,16,128]{3,2,1,0:T(8,128)} %copy.138), calls=%async_computation.7 | async-start | bytes 1048576 | tf_op jit(solution)/shard_map/all_to_all | solution.py:123
  311.2 1.0 copy-start.6
  311.2 1.0 copy-start.17
  311.2 1.1 copy-start.18
  311.2 1.2 copy-start.19
  311.2 1.2 copy-start.20
  314.1 41.2 %all-to-all-start.8 = ((f32[1,4,256,128]{3,1,0,2:T(4,128)}), f32[1,4,256,128]{3,1,0,2:T(4,128)S(1)}, u32[]{:S(2)}, u32[]{:S(2)}) async-start(f32[1,4,256,128]{3,1,0,2:T(4,128)} %copy.147), calls=%async_computation.8 | async-start | bytes 1048576 | tf_op jit(solution)/shard_map/all_to_all | solution.py:120
  357.1 28.4 %all-to-all-start.9 = ((f32[16,4,16,128]{3,2,1,0:T(8,128)}), f32[16,4,16,128]{3,2,1,0:T(8,128)S(1)}, u32[]{:S(2)}, u32[]{:S(2)}) async-start(f32[16,4,16,128]{3,2,1,0:T(8,128)} %copy.150), calls=%async_computation.9 | async-start | bytes 1048576 | tf_op jit(solution)/shard_map/all_to_all | solution.py:123
  385.6 1.0 copy-start.8
  (5 other events, 3.8 us)
where the time goes:
time: 389 us; the launch traced here: 388 us
  local copies, waits for them, and re-layouts  122 us (31%)
  blocking collectives  91.4 us (23%)
  starting transfers between devices  80 us (21%)
  waiting for transfers between devices  70.1 us (18%)
  other arithmetic  19 us (5%)
  matrix products  4.24 us (1%)
    gather x20, local copies, waits for them, and re-layouts, interface_ghost(): jnp.take_along_axis(other, jnp.broadcast_to(source[:, None, :], shape), a...  96.8 us
    all_gather x5, blocking collectives, gather_together(): lines, at, done = (lax.all_gather(flat, axis), 0, [])  91.4 us
    all_to_all x5, waiting for transfers between devices, shards(): lax.all_to_all(applied, 'tm', split_axis=0, concat_axis=2, tiled=True)  70.1 us
    all_to_all x5, starting transfers between devices, shards(): lax.all_to_all(applied, 'tm', split_axis=0, concat_axis=2, tiled=True)  56 us
    all_to_all x5, starting transfers between devices, shards(): lax.all_to_all(field, 'tm', split_axis=2, concat_axis=0, tiled=True)  24 us
    unnamed x75, local copies, waits for them, and re-layouts  9.53 us
  transfers between devices with their start and end apart: 10, of which 5 were waited for; matrix products, arithmetic and copies ran while one was open for 31% of the time, Pallas kernels for 0%

commit v1 on v0

v1 whole, which is shorter than its diff:
```python
import functools

import jax
import jax.numpy as jnp
import numpy as np
from jax import lax
from jax.experimental import pallas as pl
from jax.experimental.pallas import tpu as pltpu
from jax.sharding import PartitionSpec as P

SECTION_FACTORS = (0.075, 0.05, 0.1125, 0.15, 0.3)
OMEGA = 1.0
DISSIPATION = 0.2

NT = 16
NV = 4
CHUNK = 16
HALO = 5
LINES = CHUNK + 2 * HALO
W = 128
HALF = 8
BLOCKS = 16
NR = 112
BEFORE, AFTER, TABLE = 64, 84, 104
ZONE = 25
HALF_ZONE = 13
EDGE_PACKS = 7
VMEM = pl.BlockSpec(memory_space=pltpu.VMEM)
SMEM = pl.BlockSpec(memory_space=pltpu.SMEM)


def level_matrix():
    offsets = np.arange(NT)[:, None] - np.arange(NT)[None, :]
    angle = np.pi * offsets / NT
    safe = np.where(offsets == 0, 0.5 * np.pi, angle)
    cot = np.cos(safe) / np.sin(safe)
    matrix = np.where(offsets == 0, 0.0, 0.5 * (1.0 - 2.0 * (offsets % 2)) * cot)
    matrix = OMEGA * matrix + 4.0 * DISSIPATION * np.eye(NT)
    return np.kron(np.eye(NV), matrix).astype(np.float32)


def params(mib):
    return pltpu.CompilerParams(vmem_limit_bytes=mib << 20)


def place():
    return lax.axis_index("tm"), lax.axis_index("block")


def line_address(side, r, v):
    if r < 0:
        rotor, stator = BEFORE + v * HALO + r + HALO, AFTER + v * HALO - 1 - r
    elif r < CHUNK:
        rotor, stator = v * CHUNK + r, v * CHUNK + CHUNK - 1 - r
    else:
        rotor, stator = AFTER + v * HALO + r - CHUNK, BEFORE + v * HALO + 20 - r
    return jnp.where(side == 0, rotor, stator)


def pack_kernel(state, far, index, weight, out):
    _, block = place()
    side = block // HALF
    rotor = side == 0
    table = jnp.concatenate([index[...].astype(jnp.float32), weight[...], jnp.zeros((3, W), jnp.float32)], axis=0)
    for t in range(NT):
        chunk = jnp.where(rotor, t, NT - 1 - t)
        start = pl.multiple_of(chunk * CHUNK, CHUNK)
        low = pl.multiple_of(jnp.maximum(start - 8, 0), 8)
        high = pl.multiple_of(jnp.minimum(start + CHUNK, 248), 8)
        for v in range(NV):
            out[t, v * CHUNK : (v + 1) * CHUNK] = state[v, pl.ds(start, CHUNK)]
            before = state[v, pl.ds(low, 8)][3:8]
            after = state[v, pl.ds(high, 8)][0:5]
            if t == 0:
                ghost = jnp.broadcast_to(far[v : v + 1], (HALO, W))
                before = jnp.where(rotor, ghost, before)
                after = jnp.where(rotor, after, ghost)
            out[t, BEFORE + v * HALO : BEFORE + (v + 1) * HALO] = before
            out[t, AFTER + v * HALO : AFTER + (v + 1) * HALO] = after
        out[t, TABLE:NR] = table


def zone_kernel(lines, low, high, left, right):
    _, block = place()
    side = block // HALF
    for k in range(ZONE):
        if k < 20:
            address = line_address(side, CHUNK - 1 - k // NV, k % NV)
        else:
            address = TABLE + k - 20
        tile = lines[pl.ds(address, NT, stride=NR), :]
        if k < HALF_ZONE:
            low[k * NT : (k + 1) * NT] = tile
        else:
            high[(k - HALF_ZONE) * NT : (k - HALF_ZONE + 1) * NT] = tile
    high[(HALF_ZONE - 1) * NT :] = jnp.zeros((NT, W), jnp.float32)
    part = lax.broadcasted_iota(jnp.int32, (NT, W), 1) // 8
    for p in range(EDGE_PACKS):
        left_pack = jnp.zeros((NT, W), jnp.float32)
        right_pack = jnp.zeros((NT, W), jnp.float32)
        for k in range(16):
            m = p * 16 + k
            if m >= LINES * NV:
                break
            tile = lines[pl.ds(line_address(side, m // NV - HALO, m % NV), NT, stride=NR), :]
            moved = tile if k == 0 else pltpu.roll(tile, 8 * k, 1)
            left_pack = jnp.where(part == k, moved, left_pack)
            moved = tile if k == 15 else pltpu.roll(tile, 8 * k + 8, 1)
            right_pack = jnp.where(part == k, moved, right_pack)
        left[p * NT : (p + 1) * NT] = left_pack
        right[p * NT : (p + 1) * NT] = right_pack


def coefficients(flow, side):
    sign = jnp.where(side == 0, 0.5, -0.5)
    along = sign * flow[side, 0]
    across = 0.5 * flow[side, 1]
    return sign, along - DISSIPATION, -along - DISSIPATION, across - DISSIPATION, -across - DISSIPATION


def rates(coefs, up, down, nxt, prv, timed):
    sign, cu, cd, cn, cp = coefs
    plain = [timed[v] + (cu * up[v] + cd * down[v]) + (cn * nxt[v] + cp * prv[v]) for v in range(NV)]
    mixed = sign * (up[1] - down[1]) + 0.5 * (nxt[2] - prv[2])
    pressure_up = sign * (up[3] - down[3])
    pressure_next = 0.5 * (nxt[3] - prv[3])
    return [plain[0] + mixed, plain[1] + pressure_up, plain[2] + pressure_next, plain[3] + mixed]


def level_product(matrix, values):
    return jnp.dot(matrix, values, precision=lax.Precision.HIGHEST, preferred_element_type=jnp.float32)


def chain_kernel(low, high, matrix, flow, out, cur, ghosts):
    _, block = place()
    own_side, own = block // HALF, block % HALF
    lane = lax.broadcasted_iota(jnp.int32, (NT, W), 1)

    def tile(side, j, k):
        source, k = (low, k) if k < HALF_ZONE else (high, k - HALF_ZONE)
        return source[HALF * side + j, k * NT : (k + 1) * NT, :]

    def value(section, side, line, v, j):
        if section == 0:
            return tile(side, j, line * NV + v)
        return cur[section % 2, side, line, v, j]

    def interpolate(section, side, j):
        first = tile(side, j, 20).astype(jnp.int32)
        totals = [jnp.zeros((NT, W), jnp.float32)] * NV
        for k in range(4):
            source = (first + k) & (HALF * W - 1)
            within, which = source & (W - 1), source >> 7
            weight = tile(side, j, 21 + k)
            picked = [None] * NV
            for m in range(HALF):
                here = which == m
                for v in range(NV):
                    got = jnp.take_along_axis(value(section, 1 - side, 0, v, m), within, axis=1, mode="promise_in_bounds")
                    picked[v] = got if m == 0 else jnp.where(here, got, picked[v])
            totals = [totals[v] + weight * picked[v] for v in range(NV)]
        return totals

    for s in range(5):

        def ghost_step(step, _, s=s):
            side, j = step // HALF, step % HALF
            got = interpolate(s, side, j)
            for v in range(NV):
                ghosts[side, v, j] = got[v]
            return 0

        if s < 4:
            lax.fori_loop(0, 2 * HALF, ghost_step, 0)
            for v in range(NV):
                out[s, v, 0] = ghosts[own_side, v, own]
                after = ghosts[own_side, v, (own + 1) % HALF]
                before = ghosts[own_side, v, (own + HALF - 1) % HALF]
                out[s, v, 1] = jnp.where(lane < W // 2, after, before)
        else:
            got = interpolate(s, own_side, own)
            for v in range(NV):
                out[s, v, 0] = got[v]
                out[s, v, 1] = got[v]
            break

        def line_step(step, _, s=s):
            side, j = step // HALF, step % HALF
            after, before = (j + 1) % HALF, (j + HALF - 1) % HALF
            coefs = coefficients(flow, side)
            for line in range(4 - s):
                here = [value(s, side, line, v, j) for v in range(NV)]
                up = [ghosts[side, v, j] if line == 0 else value(s, side, line - 1, v, j) for v in range(NV)]
                down = [value(s, side, line + 1, v, j) for v in range(NV)]
                nxt = [
                    jnp.where(
                        lane == W - 1,
                        pltpu.roll(value(s, side, line, v, after), W - 1, 1),
                        pltpu.roll(here[v], W - 1, 1),
                    )
                    for v in range(NV)
                ]
                prv = [
                    jnp.where(
                        lane == 0, pltpu.roll(value(s, side, line, v, before), 1, 1), pltpu.roll(here[v], 1, 1)
                    )
                    for v in range(NV)
                ]
                product = level_product(matrix[...], jnp.concatenate(here, axis=0))
                timed = [product[v * NT : (v + 1) * NT] for v in range(NV)]
                rate = rates(coefs, up, down, nxt, prv, timed)
                for v in range(NV):
                    cur[(s + 1) % 2, side, line, v, j] = value(0, side, line, v, j) - SECTION_FACTORS[s] * rate[v]
            return 0

        lax.fori_loop(0, 2 * HALF, line_step, 0)


def bulk_kernel(lines, from_left, from_right, ghosts, matrix, flow, out, start, even, odd):
    t, block = place()
    side = block // HALF
    lane = lax.broadcasted_iota(jnp.int32, (NT, W), 1)
    for m in range(LINES * NV):
        r, v = m // NV - HALO, m % NV
        at = slice(v * NT, (v + 1) * NT)
        start[m // NV, at, :W] = lines[pl.ds(line_address(side, r, v), NT, stride=NR), :]
        p, k = m // 16, m % 16
        after = from_right[p * NT : (p + 1) * NT]
        after = after if k == 0 else pltpu.roll(after, W - 8 * k, 1)
        before = from_left[p * NT : (p + 1) * NT]
        before = before if k == 15 else pltpu.roll(before, 120 - 8 * k, 1)
        start[m // NV, at, W:] = jnp.where(lane < W // 2, after, before)
    coefs = coefficients(flow, side)
    for s in range(5):
        now = start if s == 0 else (even if s % 2 == 0 else odd)
        new = odd if s % 2 == 0 else even

        @pl.when(t == NT - 1)
        def _(now=now, s=s):
            for v in range(NV):
                at = slice(v * NT, (v + 1) * NT)
                now[HALO + CHUNK, at, :W] = ghosts[s, v, 0]
                now[HALO + CHUNK, at, W:] = ghosts[s, v, 1]

        if s > 0:

            @pl.when(t == 0)
            def _(now=now):
                now[HALO - 1] = start[HALO - 1]

        def line_step(i, _, now=now, new=new, s=s):
            here = now[i]
            split = lambda x: [x[v * NT : (v + 1) * NT] for v in range(NV)]
            nxt = pltpu.roll(here, 2 * W - 1, 1)
            prv = pltpu.roll(here, 1, 1)
            timed = level_product(matrix[...], here)
            rate = rates(coefs, split(now[i + 1]), split(now[i - 1]), split(nxt), split(prv), split(timed))
            base = split(start[i])
            for v in range(NV):
                result = base[v] - SECTION_FACTORS[s] * rate[v]
                if s < 4:
                    new[i, v * NT : (v + 1) * NT] = result
                else:
                    cell = jnp.where(side == 0, i - HALO, CHUNK - 1 + HALO - i)
                    out[pl.ds(v * CHUNK + cell, NT, stride=NV * CHUNK), :] = result[:, :W]
            return 0

        lax.fori_loop(s + 1, LINES - 1 - s, line_step, 0)


def unpack_kernel(shares, out):
    _, block = place()
    for t in range(NT):
        chunk = jnp.where(block < HALF, t, NT - 1 - t)
        start = pl.multiple_of(chunk * CHUNK, CHUNK)
        for v in range(NV):
            out[v, pl.ds(start, CHUNK)] = shares[t, v * CHUNK : (v + 1) * CHUNK]


def f32(*shape):
    return jax.ShapeDtypeStruct(shape, jnp.float32)


def shards(state, far_field, face_index, face_weight, mean_flow):
    matrix = jnp.asarray(level_matrix())
    t = lax.axis_index("tm")
    shares = pl.pallas_call(
        pack_kernel, out_shape=f32(NT, NR, W), in_specs=[VMEM] * 4, out_specs=VMEM, compiler_params=params(16), name="pack"
    )(state[0], far_field[0], face_index, face_weight[0])
    lines = lax.all_to_all(shares, "tm", 0, 0, tiled=True).reshape(NT * NR, W)
    low, high, left, right = pl.pallas_call(
        zone_kernel,
        out_shape=[f32(HALF_ZONE * NT, W)] * 2 + [f32(EDGE_PACKS * NT, W)] * 2,
        in_specs=[VMEM],
        out_specs=[VMEM] * 4,
        compiler_params=params(16),
        name="zone",
    )(lines)
    last = NT - 1
    given = lax.ppermute(low, "tm", [(last, last - 1)])
    offered = jnp.where(t == last - 1, given, high)
    rights = [(b, b // HALF * HALF + (b + 1) % HALF) for b in range(BLOCKS)]
    from_left = lax.ppermute(right, "block", rights)
    from_right = lax.ppermute(left, "block", [(b, a) for a, b in rights])
    zone_high = lax.all_to_all(jnp.broadcast_to(offered, (BLOCKS, HALF_ZONE * NT, W)), "block", 0, 0, tiled=True)
    zone_low = lax.ppermute(zone_high, "tm", [(last - 1, last)])
    ghosts = pl.pallas_call(
        chain_kernel,
        out_shape=f32(5, NV, 2, NT, W),
        in_specs=[VMEM] * 3 + [SMEM],
        out_specs=VMEM,
        scratch_shapes=[pltpu.VMEM((2, 2, 4, NV, HALF, NT, W), jnp.float32), pltpu.VMEM((2, NV, HALF, NT, W), jnp.float32)],
        compiler_params=params(32),
        name="chain",
    )(zone_low, zone_high, matrix, mean_flow)
    grid = pltpu.VMEM((LINES, NV * NT, 2 * W), jnp.float32)
    done = pl.pallas_call(
        bulk_kernel,
        out_shape=f32(NT * NV * CHUNK, W),
        in_specs=[VMEM] * 5 + [SMEM],
        out_specs=VMEM,
        scratch_shapes=[grid, grid, grid],
        compiler_params=params(32),
        name="bulk",
    )(lines, from_left, from_right, ghosts, matrix, mean_flow)
    done = lax.all_to_all(done.reshape(NT, NV * CHUNK, W), "tm", 0, 0, tiled=True)
    result = pl.pallas_call(
        unpack_kernel, out_shape=f32(NV, NT * CHUNK, W), in_specs=[VMEM], out_specs=VMEM, compiler_params=params(16), name="unpack"
    )(done)
    return result[None]


def solution(mesh):
    in_specs = (
        P("tm", None, None, "block"),
        P("tm", None, "block"),
        P("tm", "block"),
        P("tm", None, "block"),
        P(),
    )
    out_specs = P("tm", None, None, "block")
    return jax.shard_map(shards, mesh=mesh, in_specs=in_specs, out_specs=out_specs, check_vma=False)
```

time: 389 us -> 175 us (0.45)
  local copies, waits for them, and re-layouts: 122 us -> 3.18 us
  Pallas kernels: 0 us -> 78.2 us
  starting transfers between devices: 80 us -> 5.07 us
  waiting for transfers between devices: 70.1 us -> 0.01 us
  other arithmetic: 19 us -> 0.01 us
  matrix products: 4.24 us -> 0 us
    gather x20 -> x0, local copies, waits for them, and re-layouts: 96.8 us -> none  [interface_ghost(): jnp.take_along_axis(other, jnp.broadcast_to(source[:, None, :], shape), a...]
    all_gather x5 -> x0, blocking collectives: 91.4 us -> none  [gather_together(): lines, at, done = (lax.all_gather(flat, axis), 0, [])]
    all_to_all x0 -> x3, blocking collectives: none -> 87.8 us  [the longest x1 35.5 us: shards(): lines = lax.all_to_all(shares, 'tm', 0, 0, tiled=True).reshape(NT * NR, W)]
    all_to_all x10 -> x0, starting transfers between devices: 80 us -> none  [the longest x5 56 us: shards(): lax.all_to_all(applied, 'tm', split_axis=0, concat_axis=2, tiled=True)]
    pallas_call x0 -> x5, Pallas kernels: none -> 78.2 us  [the longest x1 54.7 us: shards(): pl.pallas_call(chain_kernel, out_shape=f32(5, NV, 2, NT, W), in_specs=[VM...]
    all_to_all x10 -> x0, waiting for transfers between devices: 70.1 us -> none  [the longest x5 70.1 us: shards(): lax.all_to_all(applied, 'tm', split_axis=0, concat_axis=2, tiled=True)]
    add x14 -> x0, other arithmetic: 12.8 us -> none  [the longest x5 7.34 us: residual(): speed_u * diff_i[:, 0] + diff_i[:, 1]]
    unnamed x75 -> x12, local copies, waits for them, and re-layouts: 9.53 us -> 3.07 us
  transfers between devices with their start and end apart: 10 -> 4, of which waited for: 5 -> 0; matrix products, arithmetic and copies ran while one was open for 31% -> 0% of each run, Pallas kernels for 0% -> 31%
where the time goes in v1:
time: 175 us; the launch traced here: 174 us
  blocking collectives  87.8 us (50%)
  Pallas kernels  78.2 us (45%)
  starting transfers between devices  5.07 us (3%)
  local copies, waits for them, and re-layouts  3.18 us (2%)
    pallas_call x1, Pallas kernels, shards(): pl.pallas_call(chain_kernel, out_shape=f32(5, NV, 2, NT, W), in_specs=[VM...  54.7 us
    all_to_all x1, blocking collectives, shards(): lines = lax.all_to_all(shares, 'tm', 0, 0, tiled=True).reshape(NT * NR, W)  35.5 us
    all_to_all x1, blocking collectives, shards(): lax.all_to_all(jnp.broadcast_to(offered, (BLOCKS, HALF_ZONE * NT, W)), 'b...  31.2 us
    pallas_call x1, Pallas kernels, shards(): pl.pallas_call(bulk_kernel, out_shape=f32(NT * NV * CHUNK, W), in_specs=[...  22 us
    all_to_all x1, blocking collectives, shards(): lax.all_to_all(done.reshape(NT, NV * CHUNK, W), 'tm', 0, 0, tiled=True)  21.1 us
    ppermute x1, starting transfers between devices, shards(): from_right = lax.ppermute(left, 'block', [(b, a) for a, b in rights])  3.56 us
  transfers between devices with their start and end apart: 4, of which 0 were waited for; matrix products, arithmetic and copies ran while one was open for 0% of the time, Pallas kernels for 31%

profile of v1, /device:TPU:1, one launch (start us, length us, event | category | flops | bytes accessed | tf_op | source)
XLA Modules:
  0.0 174.4 jit_solution(6145028765749019044)
XLA Ops:
  0.0 0.0 copy-start
  0.0 1.0 copy-done
  1.0 0.0 copy-start.3
  1.0 0.7 copy-done.3
  1.7 0.0 copy-start.4
  1.7 0.7 copy-done.4
  2.4 0.0 copy-start.5
  2.4 0.7 copy-done.5
  3.1 0.1 pack.1
  3.2 35.5 %all_to_all.15 = f32[16,112,128]{2,1,0:T(8,128)S(1)} all-to-all(f32[16,112,128]{2,1,0:T(8,128)S(1)} %pack.1), channel_id=1, replica_groups=mesh['tm'=16,'block'=16] {'tm'}, dimensions={0} | all-to-all | bytes 1835008 | tf_op jit(solution)/shard_map/all_to_all | solution.py:290
  38.7 0.6 zone.1
  39.3 0.7 collective-permute-start.2
  40.0 0.0 collective-permute-done.2
  40.0 0.1 broadcast_in_dim.6
  40.1 0.0 copy-start.1
  40.1 0.0 copy-start.2
  40.2 31.2 %all_to_all.16.high = f32[16,208,128]{2,1,0:T(8,128)S(1)} all-to-all(f32[16,208,128]{2,1,0:T(8,128)S(1)} %broadcast_in_dim.6), channel_id=1, replica_groups=mesh['tm'=16,'block'=16] {'block'}, dimensions={0} | all-to-all | bytes 3407872 | tf_op jit(solution)/shard_map/all_to_all | solution.py:305
  71.3 0.8 collective-permute-start.3
  72.1 0.1 collective-permute-start
  72.2 3.6 %collective-permute-start.1 = (f32[112,128]{1,0:T(8,128)S(1)}, f32[112,128]{1,0:T(8,128)S(1)}, u32[]{:S(2)}, u32[]{:S(2)}) collective-permute-start(f32[112,128]{1,0:T(8,128)S(1)} %get-tuple-element.10), channel_id=1, source_target_pairs={{1,0},{2,1},{3,2},{4,3},{5,4},{6,5},{7,6},{0,7},{9,8},{10,9},{11,1... | collective-permute-start | bytes 172040 | tf_op jit(solution)/shard_map/ppermute | solution.py:304
  75.7 0.0 collective-permute-done.3.low
  75.7 0.0 copy-done.1
  75.7 0.0 copy-done.2
  75.7 54.7 %chain.1.ghosts = f32[5,4,2,16,128]{4,3,2,1,0:T(8,128)S(1)} custom-call(f32[16,208,128]{2,1,0:T(8,128)S(1)} %collective-permute-done.3.low, f32[16,208,128]{2,1,0:T(8,128)S(1)} %all_to_all.16.high, f32[64,64]{1,0:T(8,128)S(1)} %copy-done.1, f32[2,2]{1,0:T(2,128)S(1)} %copy-done.2), custom_call_target="tpu_custom_call" | custom-call | tf_op jit(solution)/shard_map/chain/pallas_call | solution.py:307
  130.5 0.0 collective-permute-done.from_left
  130.5 0.0 collective-permute-done.1.from_right
  130.5 22.0 %bulk.1 = f32[1024,128]{1,0:T(8,128)S(1)} custom-call(f32[1792,128]{1,0:T(8,128)S(1)} %bitcast.7, f32[112,128]{1,0:T(8,128)S(1)} %collective-permute-done.from_left, f32[112,128]{1,0:T(8,128)S(1)} %collective-permute-done.1.from_right, f32[5,4,2,16,128]{4,3,2,1,0:T(8,128)S(1)} %chain.1.ghosts, f32[64,64]{1,0:T(8,128)S(1)} %copy-done.1, f32[2,2]{1,0:T(2,128)S(1)} %copy-done.2), custom_call_target="tpu_custom_call" | custom-call | tf_op jit(solution)/shard_map/bulk/pallas_call | solution.py:317
  152.5 21.1 %all_to_all.17.shares = f32[16,64,128]{2,1,0:T(8,128)S(1)} all-to-all(f32[16,64,128]{2,1,0:T(8,128)S(1)} %bitcast.8), channel_id=1, replica_groups=mesh['tm'=16,'block'=16] {'tm'}, dimensions={0} | all-to-all | bytes 1048576 | tf_op jit(solution)/shard_map/all_to_all | solution.py:326
  173.6 0.8 unpack.1
  (1 shorter events, 0.0 us)
Async XLA Ops:
  0.0 1.0 copy-start
  1.0 0.7 copy-start.3
  1.7 0.7 copy-start.4
  2.4 0.7 copy-start.5
  39.3 0.7 collective-permute-start.2
  40.1 35.6 %copy-start.1 = (f32[64,64]{1,0:T(8,128)S(1)}, f32[64,64]{1,0:T(8,128)}, u32[]{:S(2)}) copy-start(f32[64,64]{1,0:T(8,128)} %constant.9.clone.matrix) | copy-start | bytes 49156
  40.1 35.6 %copy-start.2 = (f32[2,2]{1,0:T(2,128)S(1)}, f32[2,2]{1,0:T(2,128)}, u32[]{:S(2)}) copy-start(f32[2,2]{1,0:T(2,128)} %flow.3) | copy-start | bytes 52
  71.3 4.4 %collective-permute-start.3 = (f32[16,208,128]{2,1,0:T(8,128)S(1)}, f32[16,208,128]{2,1,0:T(8,128)S(1)}, u32[]{:S(2)}, u32[]{:S(2)}) collective-permute-start(f32[16,208,128]{2,1,0:T(8,128)S(1)} %all_to_all.16.high), channel_id=1, source_target_pairs={{224,240},{225,241},{226,242},{227,243},{228,244},{229,245},{230,2... | collective-permute-start | bytes 5111816 | tf_op jit(solution)/shard_map/ppermute | solution.py:306
  72.1 58.4 %collective-permute-start = (f32[112,128]{1,0:T(8,128)S(1)}, f32[112,128]{1,0:T(8,128)S(1)}, u32[]{:S(2)}, u32[]{:S(2)}) collective-permute-start(f32[112,128]{1,0:T(8,128)S(1)} %get-tuple-element.9), channel_id=1, source_target_pairs={{0,1},{1,2},{2,3},{3,4},{4,5},{5,6},{6,7},{7,0},{8,9},{9,10},{10,1... | collective-permute-start | bytes 172040 | tf_op jit(solution)/shard_map/ppermute | solution.py:303
  72.2 58.3 %collective-permute-start.1 = (f32[112,128]{1,0:T(8,128)S(1)}, f32[112,128]{1,0:T(8,128)S(1)}, u32[]{:S(2)}, u32[]{:S(2)}) collective-permute-start(f32[112,128]{1,0:T(8,128)S(1)} %get-tuple-element.10), channel_id=1, source_target_pairs={{1,0},{2,1},{3,2},{4,3},{5,4},{6,5},{7,6},{0,7},{9,8},{10,9},{11,1... | collective-permute-start | bytes 172040 | tf_op jit(solution)/shard_map/ppermute | solution.py:304

commit v2 on v1

--- a/solution.py
+++ b/solution.py
@@ -1,7 +1,6 @@
-import functools
-
 import jax
 import jax.numpy as jnp
+import ml_dtypes
 import numpy as np
 from jax import lax
 from jax.experimental import pallas as pl
@@ -36,7 +35,10 @@
     cot = np.cos(safe) / np.sin(safe)
     matrix = np.where(offsets == 0, 0.0, 0.5 * (1.0 - 2.0 * (offsets % 2)) * cot)
     matrix = OMEGA * matrix + 4.0 * DISSIPATION * np.eye(NT)
-    return np.kron(np.eye(NV), matrix).astype(np.float32)
+    matrix = np.kron(np.eye(NV), matrix).astype(np.float32)
+    lead = matrix.astype(ml_dtypes.bfloat16)
+    rest = (matrix - lead.astype(np.float32)).astype(ml_dtypes.bfloat16)
+    return np.concatenate([lead, rest, lead], axis=1)
 
 
 def params(mib):
@@ -128,10 +130,16 @@
 
 
 def level_product(matrix, values):
-    return jnp.dot(matrix, values, precision=lax.Precision.HIGHEST, preferred_element_type=jnp.float32)
-
-
-def chain_kernel(low, high, matrix, flow, out, cur, ghosts):
+    lead = values.astype(jnp.bfloat16)
+    rest = (values - lead.astype(jnp.float32)).astype(jnp.bfloat16)
+    return jnp.dot(matrix, jnp.concatenate([lead, lead, rest], axis=0), preferred_element_type=jnp.float32)
+
+
+def split(lines):
+    return [lines[v * NT : (v + 1) * NT] for v in range(NV)]
+
+
+def chain_kernel(low, high, matrix, flow, out, cur, nexts, prevs, ghosts):
     _, block = place()
     own_side, own = block // HALF, block % HALF
     lane = lax.broadcasted_iota(jnp.int32, (NT, W), 1)
@@ -145,75 +153,82 @@
             return tile(side, j, line * NV + v)
         return cur[section % 2, side, line, v, j]
 
+    def keep_rolled(section, side, line, v, j, values):
+        nexts[section % 2, side, line, v, j] = pltpu.roll(values, W - 1, 1)
+        prevs[section % 2, side, line, v, j] = pltpu.roll(values, 1, 1)
+
     def interpolate(section, side, j):
         first = tile(side, j, 20).astype(jnp.int32)
-        totals = [jnp.zeros((NT, W), jnp.float32)] * NV
-        for k in range(4):
-            source = (first + k) & (HALF * W - 1)
-            within, which = source & (W - 1), source >> 7
-            weight = tile(side, j, 21 + k)
-            picked = [None] * NV
-            for m in range(HALF):
-                here = which == m
-                for v in range(NV):
-                    got = jnp.take_along_axis(value(section, 1 - side, 0, v, m), within, axis=1, mode="promise_in_bounds")
-                    picked[v] = got if m == 0 else jnp.where(here, got, picked[v])
-            totals = [totals[v] + weight * picked[v] for v in range(NV)]
-        return totals
-
-    for s in range(5):
-
-        def ghost_step(step, _, s=s):
-            side, j = step // HALF, step % HALF
-            got = interpolate(s, side, j)
+        parts = []
+        for h in range(2):
+            at = slice(8 * h, 8 * h + 8)
+            totals = [None] * NV
+            for k in range(4):
+                source = (first[at] + k) & (HALF * W - 1)
+                within, which = source & (W - 1), source >> 7
+                weight = tile(side, j, 21 + k)[at]
+                picked = [None] * NV
+                for m in range(HALF):
+                    here = which == m
+                    for v in range(NV):
+                        face = value(section, 1 - side, 0, v, m)[at]
+                        got = jnp.take_along_axis(face, within, axis=1, mode="promise_in_bounds")
+                        picked[v] = got if m == 0 else jnp.where(here, got, picked[v])
+                totals = [weight * picked[v] if k == 0 else totals[v] + weight * picked[v] for v in range(NV)]
+            parts.append(totals)
+        return [jnp.concatenate([parts[0][v], parts[1][v]], axis=0) for v in range(NV)]
+
+    def first_rolls(step, _):
+        side, j = step // HALF, step % HALF
+        for line in range(4):
             for v in range(NV):
-                ghosts[side, v, j] = got[v]
-            return 0
-
-        if s < 4:
-            lax.fori_loop(0, 2 * HALF, ghost_step, 0)
-            for v in range(NV):
-                out[s, v, 0] = ghosts[own_side, v, own]
-                after = ghosts[own_side, v, (own + 1) % HALF]
-                before = ghosts[own_side, v, (own + HALF - 1) % HALF]
-                out[s, v, 1] = jnp.where(lane < W // 2, after, before)
-        else:
-            got = interpolate(s, own_side, own)
-            for v in range(NV):
-                out[s, v, 0] = got[v]
-                out[s, v, 1] = got[v]
-            break
-
-        def line_step(step, _, s=s):
+                keep_rolled(0, side, line, v, j, value(0, side, line, v, j))
+        return 0
+
+    lax.fori_loop(0, 2 * HALF, first_rolls, 0)
+    for s in range(4):
+
+        def section_step(step, _, s=s):
             side, j = step // HALF, step % HALF
             after, before = (j + 1) % HALF, (j + HALF - 1) % HALF
             coefs = coefficients(flow, side)
-            for line in range(4 - s):
-                here = [value(s, side, line, v, j) for v in range(NV)]
-                up = [ghosts[side, v, j] if line == 0 else value(s, side, line - 1, v, j) for v in range(NV)]
-                down = [value(s, side, line + 1, v, j) for v in range(NV)]
+            ghost = interpolate(s, side, j)
+            for v in range(NV):
+                ghosts[side, v, j] = ghost[v]
+            lines = 4 - s
+            here = [[value(s, side, line, v, j) for v in range(NV)] for line in range(lines + 1)]
+            product = level_product(
+                matrix[...], jnp.concatenate([jnp.concatenate(here[line], axis=0) for line in range(lines)], axis=1)
+            )
+            for line in reversed(range(lines)):
+                up = ghost if line == 0 else here[line - 1]
                 nxt = [
-                    jnp.where(
-                        lane == W - 1,
-                        pltpu.roll(value(s, side, line, v, after), W - 1, 1),
-                        pltpu.roll(here[v], W - 1, 1),
-                    )
+                    jnp.where(lane == W - 1, nexts[s % 2, side, line, v, after], nexts[s % 2, side, line, v, j])
                     for v in range(NV)
                 ]
                 prv = [
-                    jnp.where(
-                        lane == 0, pltpu.roll(value(s, side, line, v, before), 1, 1), pltpu.roll(here[v], 1, 1)
-                    )
+                    jnp.where(lane == 0, prevs[s % 2, side, line, v, before], prevs[s % 2, side, line, v, j])
                     for v in range(NV)
                 ]
-                product = level_product(matrix[...], jnp.concatenate(here, axis=0))
-                timed = [product[v * NT : (v + 1) * NT] for v in range(NV)]
-                rate = rates(coefs, up, down, nxt, prv, timed)
+                timed = split(product[:, line * W : (line + 1) * W])
+                rate = rates(coefs, up, here[line + 1], nxt, prv, timed)
                 for v in range(NV):
-                    cur[(s + 1) % 2, side, line, v, j] = value(0, side, line, v, j) - SECTION_FACTORS[s] * rate[v]
+                    result = value(0, side, line, v, j) - SECTION_FACTORS[s] * rate[v]
+                    cur[(s + 1) % 2, side, line, v, j] = result
+                    if line < lines - 1:
+                        keep_rolled(s + 1, side, line, v, j, result)
             return 0
 
-        lax.fori_loop(0, 2 * HALF, line_step, 0)
+        lax.fori_loop(0, 2 * HALF, section_step, 0)
+        for v in range(NV):
+            out[s, v, 0] = ghosts[own_side, v, own]
+            after = ghosts[own_side, v, (own + 1) % HALF]
+            before = ghosts[own_side, v, (own + HALF - 1) % HALF]
+            out[s, v, 1] = jnp.where(lane < W // 2, after, before)
+    got = interpolate(4, own_side, own)
+    for v in range(NV):
+        out[4, v, 0] = got[v]
+        out[4, v, 1] = got[v]
 
 
 def bulk_kernel(lines, from_left, from_right, ghosts, matrix, flow, out, start, even, odd):
@@ -231,6 +246,7 @@
         before = before if k == 15 else pltpu.roll(before, 120 - 8 * k, 1)
         start[m // NV, at, W:] = jnp.where(lane < W // 2, after, before)
     coefs = coefficients(flow, side)
+    group = 4
     for s in range(5):
         now = start if s == 0 else (even if s % 2 == 0 else odd)
         new = odd if s % 2 == 0 else even
@@ -248,24 +264,29 @@
             def _(now=now):
                 now[HALO - 1] = start[HALO - 1]
 
-        def line_step(i, _, now=now, new=new, s=s):
-            here = now[i]
-            split = lambda x: [x[v * NT : (v + 1) * NT] for v in range(NV)]
-            nxt = pltpu.roll(here, 2 * W - 1, 1)
-            prv = pltpu.roll(here, 1, 1)
-            timed = level_product(matrix[...], here)
-            rate = rates(coefs, split(now[i + 1]), split(now[i - 1]), split(nxt), split(prv), split(timed))
-            base = split(start[i])
-            for v in range(NV):
-                result = base[v] - SECTION_FACTORS[s] * rate[v]
-                if s < 4:
-                    new[i, v * NT : (v + 1) * NT] = result
-                else:
-                    cell = jnp.where(side == 0, i - HALO, CHUNK - 1 + HALO - i)
-                    out[pl.ds(v * CHUNK + cell, NT, stride=NV * CHUNK), :] = result[:, :W]
+        first = (1, 1, 3, 3, 5)[s]
+
+        def line_step(step, _, now=now, new=new, s=s, first=first):
+            i = first + group * step
+            here = [now[i - 1 + g] for g in range(group + 2)]
+            product = level_product(matrix[...], jnp.concatenate(here[1:-1], axis=1))
+            for g in range(group):
+                line = here[g + 1]
+                nxt = pltpu.roll(line, 2 * W - 1, 1)
+                prv = pltpu.roll(line, 1, 1)
+                timed = split(product[:, 2 * W * g : 2 * W * (g + 1)])
+                rate = rates(coefs, split(here[g + 2]), split(here[g]), split(nxt), split(prv), timed)
+                base = split(start[i + g])
+                for v in range(NV):
+                    result = base[v] - SECTION_FACTORS[s] * rate[v]
+                    if s < 4:
+                        new[i + g, v * NT : (v + 1) * NT] = result
+                    else:
+                        cell = jnp.where(side == 0, i + g - HALO, CHUNK - 1 + HALO - i - g)
+                        out[pl.ds(v * CHUNK + cell, NT, stride=NV * CHUNK), :] = result[:, :W]
             return 0
 
-        lax.fori_loop(s + 1, LINES - 1 - s, line_step, 0)
+        lax.fori_loop(0, (LINES - 2 * first) // group, line_step, 0)
 
 
 def unpack_kernel(shares, out):
@@ -309,7 +330,8 @@
         out_shape=f32(5, NV, 2, NT, W),
         in_specs=[VMEM] * 3 + [SMEM],
         out_specs=VMEM,
-        scratch_shapes=[pltpu.VMEM((2, 2, 4, NV, HALF, NT, W), jnp.float32), pltpu.VMEM((2, NV, HALF, NT, W), jnp.float32)],
+        scratch_shapes=[pltpu.VMEM((2, 2, 4, NV, HALF, NT, W), jnp.float32)] * 3
+        + [pltpu.VMEM((2, NV, HALF, NT, W), jnp.float32)],
         compiler_params=params(32),
         name="chain",
     )(zone_low, zone_high, matrix, mean_flow)

time: 175 us -> 140 us (0.80)
  Pallas kernels: 78.2 us -> 43.1 us
    pallas_call x1, Pallas kernels: 54.7 us -> 33.6 us  [shards(): pl.pallas_call(chain_kernel, out_shape=f32(5, NV, 2, NT, W), in_specs=[VM...]
    pallas_call x1, Pallas kernels: 22 us -> 8 us  [shards(): pl.pallas_call(bulk_kernel, out_shape=f32(NT * NV * CHUNK, W), in_specs=[...]
  transfers between devices with their start and end apart: 4 -> 4, of which waited for: 0 -> 0; matrix products, arithmetic and copies ran while one was open for 0% -> 0% of each run, Pallas kernels for 31% -> 24%
where the time goes in v2:
time: 140 us; the launch traced here: 139 us
  blocking collectives  87.8 us (63%)
  Pallas kernels  43.1 us (31%)
  starting transfers between devices  5.07 us (4%)
  local copies, waits for them, and re-layouts  3.18 us (2%)
    all_to_all x1, blocking collectives, shards(): lines = lax.all_to_all(shares, 'tm', 0, 0, tiled=True).reshape(NT * NR, W)  35.5 us
    pallas_call x1, Pallas kernels, shards(): pl.pallas_call(chain_kernel, out_shape=f32(5, NV, 2, NT, W), in_specs=[VM...  33.6 us
    all_to_all x1, blocking collectives, shards(): lax.all_to_all(jnp.broadcast_to(offered, (BLOCKS, HALF_ZONE * NT, W)), 'b...  31.2 us
    all_to_all x1, blocking collectives, shards(): lax.all_to_all(done.reshape(NT, NV * CHUNK, W), 'tm', 0, 0, tiled=True)  21.1 us
    pallas_call x1, Pallas kernels, shards(): pl.pallas_call(bulk_kernel, out_shape=f32(NT * NV * CHUNK, W), in_specs=[...  8 us
    ppermute x1, starting transfers between devices, shards(): from_right = lax.ppermute(left, 'block', [(b, a) for a, b in rights])  3.56 us
    unnamed x12, local copies, waits for them, and re-layouts  3.07 us
  transfers between devices with their start and end apart: 4, of which 0 were waited for; matrix products, arithmetic and copies ran while one was open for 0% of the time, Pallas kernels for 24%

profile of v2, /device:TPU:1, one launch (start us, length us, event | category | flops | bytes accessed | tf_op | source)
XLA Modules:
  0.0 139.3 jit_solution(1938326435811186504)
XLA Ops:
  0.0 0.0 copy-start
  0.0 1.0 copy-done
  1.0 0.0 copy-start.3
  1.0 0.7 copy-done.3
  1.7 0.0 copy-start.4
  1.7 0.7 copy-done.4
  2.4 0.0 copy-start.5
  2.4 0.7 copy-done.5
  3.1 0.1 pack.1
  3.2 35.5 %all_to_all.15 = f32[16,112,128]{2,1,0:T(8,128)S(1)} all-to-all(f32[16,112,128]{2,1,0:T(8,128)S(1)} %pack.1), channel_id=1, replica_groups=mesh['tm'=16,'block'=16] {'tm'}, dimensions={0} | all-to-all | bytes 1835008 | tf_op jit(solution)/shard_map/all_to_all | solution.py:311
  38.7 0.6 zone.1
  39.3 0.7 collective-permute-start.2
  40.0 0.0 collective-permute-done.2
  40.0 0.1 broadcast_in_dim.6
  40.1 0.0 copy-start.1
  40.1 0.0 copy-start.2
  40.2 31.2 %all_to_all.16.high = f32[16,208,128]{2,1,0:T(8,128)S(1)} all-to-all(f32[16,208,128]{2,1,0:T(8,128)S(1)} %broadcast_in_dim.6), channel_id=1, replica_groups=mesh['tm'=16,'block'=16] {'block'}, dimensions={0} | all-to-all | bytes 3407872 | tf_op jit(solution)/shard_map/all_to_all | solution.py:326
  71.3 0.8 collective-permute-start.3
  72.1 0.1 collective-permute-start
  72.2 3.6 %collective-permute-start.1 = (f32[112,128]{1,0:T(8,128)S(1)}, f32[112,128]{1,0:T(8,128)S(1)}, u32[]{:S(2)}, u32[]{:S(2)}) collective-permute-start(f32[112,128]{1,0:T(8,128)S(1)} %get-tuple-element.10), channel_id=1, source_target_pairs={{1,0},{2,1},{3,2},{4,3},{5,4},{6,5},{7,6},{0,7},{9,8},{10,9},{11,1... | collective-permute-start | bytes 172040 | tf_op jit(solution)/shard_map/ppermute | solution.py:325
  75.7 0.0 collective-permute-done.3.low
  75.7 0.0 copy-done.1
  75.7 0.0 copy-done.2
  75.7 33.6 %chain.1.ghosts = f32[5,4,2,16,128]{4,3,2,1,0:T(8,128)S(1)} custom-call(f32[16,208,128]{2,1,0:T(8,128)S(1)} %collective-permute-done.3.low, f32[16,208,128]{2,1,0:T(8,128)S(1)} %all_to_all.16.high, bf16[64,192]{1,0:T(8,128)(2,1)S(1)} %copy-done.1, f32[2,2]{1,0:T(2,128)S(1)} %copy-done.2), custom_call_target="tpu_custom_call" | custom-call | tf_op jit(solution)/shard_map/chain/pallas_call | solution.py:328
  109.3 0.0 collective-permute-done.from_left
  109.3 0.0 collective-permute-done.1.from_right
  109.3 8.0 %bulk.1 = f32[1024,128]{1,0:T(8,128)S(1)} custom-call(f32[1792,128]{1,0:T(8,128)S(1)} %bitcast.7, f32[112,128]{1,0:T(8,128)S(1)} %collective-permute-done.from_left, f32[112,128]{1,0:T(8,128)S(1)} %collective-permute-done.1.from_right, f32[5,4,2,16,128]{4,3,2,1,0:T(8,128)S(1)} %chain.1.ghosts, bf16[64,192]{1,0:T(8,128)(2,1)S(1)} %copy-done.1, ...), custom_call_target="tpu_custom_call" | custom-call | tf_op jit(solution)/shard_map/bulk/pallas_call | solution.py:339
  117.4 21.1 %all_to_all.17.shares = f32[16,64,128]{2,1,0:T(8,128)S(1)} all-to-all(f32[16,64,128]{2,1,0:T(8,128)S(1)} %bitcast.8), channel_id=1, replica_groups=mesh['tm'=16,'block'=16] {'tm'}, dimensions={0} | all-to-all | bytes 1048576 | tf_op jit(solution)/shard_map/all_to_all | solution.py:348
  138.5 0.8 unpack.1
  (1 shorter events, 0.0 us)
Async XLA Ops:
  0.0 1.0 copy-start
  1.0 0.7 copy-start.3
  1.7 0.7 copy-start.4
  2.4 0.7 copy-start.5
  39.3 0.7 collective-permute-start.2
  40.1 35.6 %copy-start.1 = (bf16[64,192]{1,0:T(8,128)(2,1)S(1)}, bf16[64,192]{1,0:T(8,128)(2,1)}, u32[]{:S(2)}) copy-start(bf16[64,192]{1,0:T(8,128)(2,1)} %constant.9.clone.matrix) | copy-start | bytes 73732
  40.1 35.6 %copy-start.2 = (f32[2,2]{1,0:T(2,128)S(1)}, f32[2,2]{1,0:T(2,128)}, u32[]{:S(2)}) copy-start(f32[2,2]{1,0:T(2,128)} %flow.3) | copy-start | bytes 52
  71.3 4.4 %collective-permute-start.3 = (f32[16,208,128]{2,1,0:T(8,128)S(1)}, f32[16,208,128]{2,1,0:T(8,128)S(1)}, u32[]{:S(2)}, u32[]{:S(2)}) collective-permute-start(f32[16,208,128]{2,1,0:T(8,128)S(1)} %all_to_all.16.high), channel_id=1, source_target_pairs={{224,240},{225,241},{226,242},{227,243},{228,244},{229,245},{230,2... | collective-permute-start | bytes 5111816 | tf_op jit(solution)/shard_map/ppermute | solution.py:327
  72.1 37.3 %collective-permute-start = (f32[112,128]{1,0:T(8,128)S(1)}, f32[112,128]{1,0:T(8,128)S(1)}, u32[]{:S(2)}, u32[]{:S(2)}) collective-permute-start(f32[112,128]{1,0:T(8,128)S(1)} %get-tuple-element.9), channel_id=1, source_target_pairs={{0,1},{1,2},{2,3},{3,4},{4,5},{5,6},{6,7},{7,0},{8,9},{9,10},{10,1... | collective-permute-start | bytes 172040 | tf_op jit(solution)/shard_map/ppermute | solution.py:324
  72.2 37.2 %collective-permute-start.1 = (f32[112,128]{1,0:T(8,128)S(1)}, f32[112,128]{1,0:T(8,128)S(1)}, u32[]{:S(2)}, u32[]{:S(2)}) collective-permute-start(f32[112,128]{1,0:T(8,128)S(1)} %get-tuple-element.10), channel_id=1, source_target_pairs={{1,0},{2,1},{3,2},{4,3},{5,4},{6,5},{7,6},{0,7},{9,8},{10,9},{11,1... | collective-permute-start | bytes 172040 | tf_op jit(solution)/shard_map/ppermute | solution.py:325

commit v3 on v2

--- a/solution.py
+++ b/solution.py
@@ -59,10 +59,20 @@
     return jnp.where(side == 0, rotor, stator)
 
 
-def pack_kernel(state, far, index, weight, out):
+def pack_kernel(state_in, far_in, index_in, weight_in, out, state, far, index, weight, sems):
+    copies = [
+        pltpu.make_async_copy(source, target, sems.at[i])
+        for i, (source, target) in enumerate(
+            ((state_in, state), (far_in, far), (index_in, index), (weight_in, weight))
+        )
+    ]
+    for copy in copies:
+        copy.start()
     _, block = place()
     side = block // HALF
     rotor = side == 0
+    for copy in copies:
+        copy.wait()
     table = jnp.concatenate([index[...].astype(jnp.float32), weight[...], jnp.zeros((3, W), jnp.float32)], axis=0)
     for t in range(NT):
         chunk = jnp.where(rotor, t, NT - 1 - t)
@@ -139,10 +149,11 @@
     return [lines[v * NT : (v + 1) * NT] for v in range(NV)]
 
 
-def chain_kernel(low, high, matrix, flow, out, cur, nexts, prevs, ghosts):
-    _, block = place()
+def chain_kernel(low, high, table, matrix, flow, done, out, cur, nexts, prevs, shifted, ordered, weighed, ghosts, applied):
+    t, block = place()
     own_side, own = block // HALF, block % HALF
     lane = lax.broadcasted_iota(jnp.int32, (NT, W), 1)
+    out[...] = done[...]
 
     def tile(side, j, k):
         source, k = (low, k) if k < HALF_ZONE else (high, k - HALF_ZONE)
@@ -153,11 +164,14 @@
             return tile(side, j, line * NV + v)
         return cur[section % 2, side, line, v, j]
 
-    def keep_rolled(section, side, line, v, j, values):
+    def keep_rolled(section, side, line, v, j, values, shift=False):
         nexts[section % 2, side, line, v, j] = pltpu.roll(values, W - 1, 1)
         prevs[section % 2, side, line, v, j] = pltpu.roll(values, 1, 1)
-
-    def interpolate(section, side, j):
+        if shift:
+            shifted[0, side, v, j] = pltpu.roll(values, W - 2, 1)
+            shifted[1, side, v, j] = pltpu.roll(values, W - 3, 1)
+
+    def interpolate_first(side, j):
         first = tile(side, j, 20).astype(jnp.int32)
         parts = []
         for h in range(2):
@@ -171,11 +185,67 @@
                 for m in range(HALF):
                     here = which == m
                     for v in range(NV):
-                        face = value(section, 1 - side, 0, v, m)[at]
+                        face = value(0, 1 - side, 0, v, m)[at]
                         got = jnp.take_along_axis(face, within, axis=1, mode="promise_in_bounds")
                         picked[v] = got if m == 0 else jnp.where(here, got, picked[v])
                 totals = [weight * picked[v] if k == 0 else totals[v] + weight * picked[v] for v in range(NV)]
             parts.append(totals)
+        return [jnp.concatenate([parts[0][v], parts[1][v]], axis=0) for v in range(NV)]
+
+    def order_weights(side, level):
+        rows = lambda k: table[pl.ds(HALF * side * HALF_ZONE * NT + (7 + k) * NT + level, HALF, stride=HALF_ZONE * NT), :]
+        first = rows(0).astype(jnp.int32)
+        within, which = first & (W - 1), first >> 7
+        weight = [rows(1 + k) for k in range(4)]
+        eight = lax.broadcasted_iota(jnp.int32, (HALF, W), 0)
+        many = lax.broadcasted_iota(jnp.int32, (W, W), 0)
+        spread, chosen = [], []
+        for j in range(HALF):
+            here = jnp.broadcast_to(which[j : j + 1], (HALF, W)) == eight
+            spread.append(
+                jnp.concatenate(
+                    [jnp.where(here, jnp.broadcast_to(weight[k][j : j + 1], (HALF, W)), 0.0) for k in range(4)], axis=0
+                )
+            )
+            hit = jnp.broadcast_to(within[j : j + 1], (W, W)) == many
+            chosen.append(jnp.where(hit, 1.0, 0.0).astype(jnp.bfloat16))
+        spread = jnp.concatenate(spread, axis=1)
+        chosen = jnp.concatenate(chosen, axis=1)
+        lead = spread.astype(jnp.bfloat16)
+        rest = (spread - lead.astype(jnp.float32)).astype(jnp.bfloat16)
+        both = lax.dot_general(
+            jnp.concatenate([lead, rest], axis=0), chosen, (((1,), (1,)), ((), ())), preferred_element_type=jnp.float32
+        )
+        both = both[:32] + both[32:]
+        for k in range(4):
+            ordered[side, k, pl.ds(level, HALF, stride=NT), :] = both[8 * k : 8 * k + 8]
+
+    def weigh(section, side, m):
+        other, after = 1 - side, (m + 1) % HALF
+        weight = [ordered[side, k, pl.ds(pl.multiple_of(m * NT, NT), NT), :] for k in range(4)]
+        for v in range(NV):
+            total = weight[0] * value(section, other, 0, v, m)
+            for k in range(1, 4):
+                if k == 1:
+                    here, there = nexts[section % 2, other, 0, v, m], nexts[section % 2, other, 0, v, after]
+                else:
+                    here, there = shifted[k - 2, other, v, m], shifted[k - 2, other, v, after]
+                total = total + weight[k] * jnp.where(lane >= W - k, there, here)
+            weighed[side, v, m] = total
+
+    def interpolate(side, j):
+        first = tile(side, j, 20).astype(jnp.int32)
+        within, which = first & (W - 1), first >> 7
+        parts = []
+        for h in range(2):
+            at = slice(8 * h, 8 * h + 8)
+            picked = [None] * NV
+            for m in range(HALF):
+                here = which[at] == m
+                for v in range(NV):
+                    got = jnp.take_along_axis(weighed[side, v, m, at], within[at], axis=1, mode="promise_in_bounds")
+                    picked[v] = got if m == 0 else jnp.where(here, got, picked[v])
+            parts.append(picked)
         return [jnp.concatenate([parts[0][v], parts[1][v]], axis=0) for v in range(NV)]
 
     def first_rolls(step, _):
@@ -187,14 +257,19 @@
 
     lax.fori_loop(0, 2 * HALF, first_rolls, 0)
     for s in range(4):
-
-        def section_step(step, _, s=s):
-            side, j = step // HALF, step % HALF
+        first_side, steps = (0, 2 * HALF) if s < 3 else (1 - own_side, HALF)
+
+        def weigh_step(step, _, s=s):
+            weigh(s, step // HALF, step % HALF)
+            return 0
+
+        def section_step(step, _, s=s, first_side=first_side):
+            side, j = first_side + step // HALF, step % HALF
             after, before = (j + 1) % HALF, (j + HALF - 1) % HALF
             coefs = coefficients(flow, side)
-            ghost = interpolate(s, side, j)
+            ghost = interpolate_first(side, j) if s == 0 else interpolate(side, j)
             for v in range(NV):
-                ghosts[side, v, j] = ghost[v]
+                ghosts[s % 2, side, v, j] = ghost[v]
             lines = 4 - s
             here = [[value(s, side, line, v, j) for v in range(NV)] for line in range(lines + 1)]
             product = level_product(
@@ -215,23 +290,74 @@
                 for v in range(NV):
                     result = value(0, side, line, v, j) - SECTION_FACTORS[s] * rate[v]
                     cur[(s + 1) % 2, side, line, v, j] = result
-                    if line < lines - 1:
-                        keep_rolled(s + 1, side, line, v, j, result)
+                    if line < max(lines - 1, 1):
+                        keep_rolled(s + 1, side, line, v, j, result, line == 0)
+            if s == 0:
+                order_weights(side, 2 * j)
+                order_weights(side, 2 * j + 1)
             return 0
 
-        lax.fori_loop(0, 2 * HALF, section_step, 0)
+        if s > 0:
+            lax.fori_loop(0, 2 * HALF, weigh_step, 0)
+        lax.fori_loop(0, steps, section_step, 0)
+        if s == 3:
+
+            def own_step(step, _):
+                j = (own + HALF - 1 + step) % HALF
+                ghost = interpolate(own_side, j)
+                for v in range(NV):
+                    ghosts[1, own_side, v, j] = ghost[v]
+                return 0
+
+            lax.fori_loop(0, 3, own_step, 0)
         for v in range(NV):
-            out[s, v, 0] = ghosts[own_side, v, own]
-            after = ghosts[own_side, v, (own + 1) % HALF]
-            before = ghosts[own_side, v, (own + HALF - 1) % HALF]
-            out[s, v, 1] = jnp.where(lane < W // 2, after, before)
-    got = interpolate(4, own_side, own)
+            at = slice(v * NT, (v + 1) * NT)
+            applied[s, at, :W] = ghosts[s % 2, own_side, v, own]
+            after = ghosts[s % 2, own_side, v, (own + 1) % HALF]
+            before = ghosts[s % 2, own_side, v, (own + HALF - 1) % HALF]
+            applied[s, at, W:] = jnp.where(lane < W // 2, after, before)
+
+    def last_weigh(m, _):
+        weigh(4, own_side, m)
+        return 0
+
+    lax.fori_loop(0, HALF, last_weigh, 0)
+    got = interpolate(own_side, own)
     for v in range(NV):
-        out[4, v, 0] = got[v]
-        out[4, v, 1] = got[v]
-
-
-def bulk_kernel(lines, from_left, from_right, ghosts, matrix, flow, out, start, even, odd):
+        at = slice(v * NT, (v + 1) * NT)
+        applied[4, at, :W] = got[v]
+        applied[4, at, W:] = got[v]
+
+    coefs = coefficients(flow, own_side)
+    zero = jnp.zeros((NV * NT, 2 * W), jnp.float32)
+    response = []
+    for s in range(5):
+        product = None
+        if s:
+            product = level_product(matrix[...], jnp.concatenate(response, axis=1))
+        padded = [applied[s]] + response + [zero, zero]
+        new = []
+        for line in range(s + 1):
+            here = padded[line + 1]
+            if line < s:
+                nxt, prv = pltpu.roll(here, 2 * W - 1, 1), pltpu.roll(here, 1, 1)
+                timed = product[:, 2 * W * line : 2 * W * (line + 1)]
+            else:
+                nxt = prv = timed = zero
+            rate = rates(coefs, split(padded[line]), split(padded[line + 2]), split(nxt), split(prv), split(timed))
+            new.append(-SECTION_FACTORS[s] * jnp.concatenate(rate, axis=0))
+        response = new
+
+    @pl.when(t == NT - 1)
+    def _():
+        for line in range(HALO):
+            for v in range(NV):
+                cell = jnp.where(own_side == 0, CHUNK - 1 - line, line)
+                at = pl.ds(v * CHUNK + cell, NT, stride=NV * CHUNK)
+                out[at, :] = done[at, :] + response[line][v * NT : (v + 1) * NT, :W]
+
+
+def bulk_kernel(lines, from_left, from_right, matrix, flow, out, start, even, odd):
     t, block = place()
     side = block // HALF
     lane = lax.broadcasted_iota(jnp.int32, (NT, W), 1)
@@ -252,11 +378,8 @@
         new = odd if s % 2 == 0 else even
 
         @pl.when(t == NT - 1)
-        def _(now=now, s=s):
-            for v in range(NV):
-                at = slice(v * NT, (v + 1) * NT)
-                now[HALO + CHUNK, at, :W] = ghosts[s, v, 0]
-                now[HALO + CHUNK, at, W:] = ghosts[s, v, 1]
+        def _(now=now):
+            now[HALO + CHUNK] = jnp.zeros((NV * NT, 2 * W), jnp.float32)
 
         if s > 0:
 
@@ -302,11 +425,28 @@
     return jax.ShapeDtypeStruct(shape, jnp.float32)
 
 
+def cost(flops, nbytes):
+    return pl.CostEstimate(flops=flops, bytes_accessed=nbytes, transcendentals=0)
+
+
 def shards(state, far_field, face_index, face_weight, mean_flow):
     matrix = jnp.asarray(level_matrix())
     t = lax.axis_index("tm")
+    last = NT - 1
     shares = pl.pallas_call(
-        pack_kernel, out_shape=f32(NT, NR, W), in_specs=[VMEM] * 4, out_specs=VMEM, compiler_params=params(16), name="pack"
+        pack_kernel,
+        out_shape=f32(NT, NR, W),
+        in_specs=[pl.BlockSpec(memory_space=pltpu.HBM)] * 4,
+        out_specs=VMEM,
+        scratch_shapes=[
+            pltpu.VMEM((NV, NT * CHUNK, W), jnp.float32),
+            pltpu.VMEM((NV, W), jnp.float32),
+            pltpu.VMEM((1, W), jnp.int32),
+            pltpu.VMEM((NV, W), jnp.float32),
+            pltpu.SemaphoreType.DMA((4,)),
+        ],
+        compiler_params=params(16),
+        name="pack",
     )(state[0], far_field[0], face_index, face_weight[0])
     lines = lax.all_to_all(shares, "tm", 0, 0, tiled=True).reshape(NT * NR, W)
     low, high, left, right = pl.pallas_call(
@@ -317,37 +457,49 @@
         compiler_params=params(16),
         name="zone",
     )(lines)
-    last = NT - 1
-    given = lax.ppermute(low, "tm", [(last, last - 1)])
-    offered = jnp.where(t == last - 1, given, high)
     rights = [(b, b // HALF * HALF + (b + 1) % HALF) for b in range(BLOCKS)]
     from_left = lax.ppermute(right, "block", rights)
     from_right = lax.ppermute(left, "block", [(b, a) for a, b in rights])
+    given = lax.ppermute(low, "tm", [(last, last - 1)])
+    given, from_left, from_right = lax.optimization_barrier((given, from_left, from_right))
+    offered = jnp.where(t == last - 1, given, high)
     zone_high = lax.all_to_all(jnp.broadcast_to(offered, (BLOCKS, HALF_ZONE * NT, W)), "block", 0, 0, tiled=True)
-    zone_low = lax.ppermute(zone_high, "tm", [(last - 1, last)])
-    ghosts = pl.pallas_call(
-        chain_kernel,
-        out_shape=f32(5, NV, 2, NT, W),
-        in_specs=[VMEM] * 3 + [SMEM],
-        out_specs=VMEM,
-        scratch_shapes=[pltpu.VMEM((2, 2, 4, NV, HALF, NT, W), jnp.float32)] * 3
-        + [pltpu.VMEM((2, NV, HALF, NT, W), jnp.float32)],
-        compiler_params=params(32),
-        name="chain",
-    )(zone_low, zone_high, matrix, mean_flow)
     grid = pltpu.VMEM((LINES, NV * NT, 2 * W), jnp.float32)
     done = pl.pallas_call(
         bulk_kernel,
         out_shape=f32(NT * NV * CHUNK, W),
-        in_specs=[VMEM] * 5 + [SMEM],
+        in_specs=[VMEM] * 4 + [SMEM],
         out_specs=VMEM,
         scratch_shapes=[grid, grid, grid],
-        compiler_params=params(32),
+        compiler_params=params(24),
+        cost_estimate=cost(2 * 10**9, 16 << 20),
         name="bulk",
-    )(lines, from_left, from_right, ghosts, matrix, mean_flow)
+    )(lines, from_left, from_right, matrix, mean_flow)
+    zone_high, done = lax.optimization_barrier((zone_high, done))
+    zone_low = lax.ppermute(zone_high, "tm", [(last - 1, last)])
+    lines_of = pltpu.VMEM((2, 2, 4, NV, HALF, NT, W), jnp.float32)
+    faces_of = pltpu.VMEM((2, 2, NV, HALF, NT, W), jnp.float32)
+    done = pl.pallas_call(
+        chain_kernel,
+        out_shape=f32(NT * NV * CHUNK, W),
+        in_specs=[VMEM] * 4 + [SMEM, VMEM],
+        out_specs=VMEM,
+        scratch_shapes=[lines_of] * 3
+        + [faces_of]
+        + [pltpu.VMEM((2, 4, HALF * NT, W), jnp.float32), pltpu.VMEM((2, NV, HALF, NT, W), jnp.float32)]
+        + [faces_of, pltpu.VMEM((5, NV * NT, 2 * W), jnp.float32)],
+        compiler_params=params(40),
+        cost_estimate=cost(8 * 10**9, 64 << 20),
+        name="chain",
+    )(zone_low, zone_high, zone_high.reshape(BLOCKS * HALF_ZONE * NT, W), matrix, mean_flow, done)
     done = lax.all_to_all(done.reshape(NT, NV * CHUNK, W), "tm", 0, 0, tiled=True)
     result = pl.pallas_call(
-        unpack_kernel, out_shape=f32(NV, NT * CHUNK, W), in_specs=[VMEM], out_specs=VMEM, compiler_params=params(16), name="unpack"
+        unpack_kernel,
+        out_shape=f32(NV, NT * CHUNK, W),
+        in_specs=[VMEM],
+        out_specs=VMEM,
+        compiler_params=params(16),
+        name="unpack",
     )(done)
     return result[None]
 

time: 140 us -> 133 us (0.950)
  blocking collectives: 87.8 us -> 60.5 us
  waiting for transfers between devices: 0.01 us -> 17.7 us
  starting transfers between devices: 5.07 us -> 13.1 us
  Pallas kernels: 43.1 us -> 37.3 us
    all_to_all x1 -> x0, blocking collectives: 31.2 us -> none  [shards(): lax.all_to_all(jnp.broadcast_to(offered, (BLOCKS, HALF_ZONE * NT, W)), 'b...]
    all_to_all x0 -> x1, waiting for transfers between devices: none -> 15.9 us  [shards(): lax.all_to_all(jnp.broadcast_to(offered, (BLOCKS, HALF_ZONE * NT, W)), 'b...]
    all_to_all x0 -> x1, starting transfers between devices: none -> 7.83 us  [shards(): lax.all_to_all(jnp.broadcast_to(offered, (BLOCKS, HALF_ZONE * NT, W)), 'b...]
    pallas_call x2, Pallas kernels: 33.7 us -> 27.8 us  [the longest x1 27.6 us: shards(): pl.pallas_call(chain_kernel, out_shape=f32(NT * NV * CHUNK, W), in_specs=...]
    all_to_all x1, blocking collectives: 21.1 us -> 25 us  [shards(): lax.all_to_all(done.reshape(NT, NV * CHUNK, W), 'tm', 0, 0, tiled=True)]
    ppermute x1, waiting for transfers between devices: 0.01 us -> 1.74 us  [shards(): from_left = lax.ppermute(right, 'block', rights)]
  transfers between devices with their start and end apart: 4 -> 5, of which waited for: 0 -> 2; matrix products, arithmetic and copies ran while one was open for 0% -> 0% of each run, Pallas kernels for 24% -> 6%
where the time goes in v3:
time: 133 us
  blocking collectives  60.5 us (45%)
  Pallas kernels  37.3 us (28%)
  waiting for transfers between devices  17.7 us (13%)
  starting transfers between devices  13.1 us (10%)
  local copies, waits for them, and re-layouts  4.39 us (3%)
    all_to_all x1, blocking collectives, shards(): lines = lax.all_to_all(shares, 'tm', 0, 0, tiled=True).reshape(NT * NR, W)  35.5 us
    pallas_call x1, Pallas kernels, shards(): pl.pallas_call(chain_kernel, out_shape=f32(NT * NV * CHUNK, W), in_specs=...  27.6 us
    all_to_all x1, blocking collectives, shards(): lax.all_to_all(done.reshape(NT, NV * CHUNK, W), 'tm', 0, 0, tiled=True)  25 us
    all_to_all x1, waiting for transfers between devices, shards(): lax.all_to_all(jnp.broadcast_to(offered, (BLOCKS, HALF_ZONE * NT, W)), 'b...  15.9 us
    pallas_call x1, Pallas kernels, shards(): pl.pallas_call(bulk_kernel, out_shape=f32(NT * NV * CHUNK, W), in_specs=[...  8.03 us
    all_to_all x1, starting transfers between devices, shards(): lax.all_to_all(jnp.broadcast_to(offered, (BLOCKS, HALF_ZONE * NT, W)), 'b...  7.83 us
    unnamed x12, local copies, waits for them, and re-layouts  3.07 us
  transfers between devices with their start and end apart: 5, of which 2 were waited for; matrix products, arithmetic and copies ran while one was open for 0% of the time, Pallas kernels for 6%

profile of v3, /device:TPU:1, one launch (start us, length us, event | category | flops | bytes accessed | tf_op | source)
XLA Modules:
  0.0 133.0 jit_solution(10623880058326869210)
XLA Ops:
  0.0 0.0 copy-start
  0.0 1.0 copy-done
  1.0 0.0 copy-start.1
  1.0 0.7 copy-done.1
  1.7 0.0 copy-start.2
  1.7 0.7 copy-done.2
  2.4 0.0 copy-start.3
  2.4 0.7 copy-done.3
  3.1 0.2 pack.1
  3.2 35.5 %all_to_all.15 = f32[16,112,128]{2,1,0:T(8,128)S(1)} all-to-all(f32[16,112,128]{2,1,0:T(8,128)S(1)} %pack.1), channel_id=1, replica_groups=mesh['tm'=16,'block'=16] {'tm'}, dimensions={0} | all-to-all | bytes 1835008 | tf_op jit(solution)/shard_map/all_to_all | solution.py:451
  38.8 0.6 zone.1
  39.4 0.7 collective-permute-start
  40.0 1.4 %collective-permute-start.1 = (f32[112,128]{1,0:T(8,128)S(1)}, f32[112,128]{1,0:T(8,128)S(1)}, u32[]{:S(2)}, u32[]{:S(2)}) collective-permute-start(f32[112,128]{1,0:T(8,128)S(1)} %get-tuple-element.15), channel_id=1, source_target_pairs={{0,1},{1,2},{2,3},{3,4},{4,5},{5,6},{6,7},{7,0},{8,9},{9,10},{10,1... | collective-permute-start | bytes 172040 | tf_op jit(solution)/shard_map/ppermute | solution.py:461
  41.4 2.5 %collective-permute-start.2 = (f32[112,128]{1,0:T(8,128)S(1)}, f32[112,128]{1,0:T(8,128)S(1)}, u32[]{:S(2)}, u32[]{:S(2)}) collective-permute-start(f32[112,128]{1,0:T(8,128)S(1)} %get-tuple-element.16), channel_id=1, source_target_pairs={{1,0},{2,1},{3,2},{4,3},{5,4},{6,5},{7,6},{0,7},{9,8},{10,9},{11,1... | collective-permute-start | bytes 172040 | tf_op jit(solution)/shard_map/ppermute | solution.py:462
  43.9 1.7 %collective-permute-done.1.from_left = f32[112,128]{1,0:T(8,128)S(1)} collective-permute-done((f32[112,128]{1,0:T(8,128)S(1)}, f32[112,128]{1,0:T(8,128)S(1)}, u32[]{:S(2)}, u32[]{:S(2)}) %collective-permute-start.1) | collective-permute-done | bytes 57376 | tf_op jit(solution)/shard_map/ppermute | solution.py:461
  45.6 0.0 collective-permute-done.2.from_right
  45.6 0.0 collective-permute-done
  45.6 1.3 broadcast_in_dim.6
  47.0 0.0 copy-start.4
  47.0 0.0 copy-start.5
  47.0 7.8 %all-to-all-start.1 = ((f32[16,208,128]{2,1,0:T(8,128)}), f32[16,208,128]{2,1,0:T(8,128)S(1)}, u32[]{:S(2)}, u32[]{:S(2)}) async-start(f32[16,208,128]{2,1,0:T(8,128)} %broadcast_in_dim.6), calls=%async_computation.1 | async-start | bytes 3407872 | tf_op jit(solution)/shard_map/all_to_all | solution.py:466
  54.8 0.0 copy-done.4
  54.8 0.0 copy-done.5
  54.8 8.0 %bulk.1.done = f32[1024,128]{1,0:T(8,128)S(1)} custom-call(f32[1792,128]{1,0:T(8,128)S(1)} %bitcast.8, f32[112,128]{1,0:T(8,128)S(1)} %collective-permute-done.1.from_left, f32[112,128]{1,0:T(8,128)S(1)} %collective-permute-done.2.from_right, bf16[64,192]{1,0:T(8,128)(2,1)S(1)} %copy-done.5, f32[2,2]{1,0:T(2,128)S(1)} %copy-done.4), custom_call_target="tpu_custom_call" | custom-call | flops 2000000000 | bytes 16777216 | tf_op jit(solution)/shard_map/bulk/pallas_call | solution.py:468
  62.9 15.9 %all-to-all-done.1.high = f32[16,208,128]{2,1,0:T(8,128)S(1)} async-done(((f32[16,208,128]{2,1,0:T(8,128)}), f32[16,208,128]{2,1,0:T(8,128)S(1)}, u32[]{:S(2)}, u32[]{:S(2)}) %all-to-all-start.1) | async-done | bytes 1703968 | tf_op jit(solution)/shard_map/all_to_all | solution.py:466
  78.8 0.8 collective-permute-start.3
  79.6 0.0 collective-permute-done.3.low
  79.6 27.6 %chain.1 = f32[1024,128]{1,0:T(8,128)S(1)} custom-call(f32[16,208,128]{2,1,0:T(8,128)S(1)} %collective-permute-done.3.low, f32[16,208,128]{2,1,0:T(8,128)S(1)} %all-to-all-done.1.high, f32[3328,128]{1,0:T(8,128)S(1)} %bitcast.9, bf16[64,192]{1,0:T(8,128)(2,1)S(1)} %copy-done.5, f32[2,2]{1,0:T(2,128)S(1)} %copy-done.4, f32[1024,128]{1,0:T(8,128)S(1)} %bulk.1.done), custom_call_target="tpu_custom_call" | custom-call | flops 8000000000 | bytes 67108864 | tf_op jit(solution)/shard_map/chain/pallas_call | solution.py:482
  107.2 25.0 %all_to_all.16.shares = f32[16,64,128]{2,1,0:T(8,128)S(1)} all-to-all(f32[16,64,128]{2,1,0:T(8,128)S(1)} %bitcast.11), channel_id=1, replica_groups=mesh['tm'=16,'block'=16] {'tm'}, dimensions={0} | all-to-all | bytes 1048576 | tf_op jit(solution)/shard_map/all_to_all | solution.py:495
  132.2 0.8 unpack.1
  (1 shorter events, 0.0 us)
Async XLA Ops:
  0.0 1.0 copy-start
  1.0 0.7 copy-start.1
  1.7 0.7 copy-start.2
  2.4 0.7 copy-start.3
  39.4 6.2 %collective-permute-start = (f32[208,128]{1,0:T(8,128)S(1)}, f32[208,128]{1,0:T(8,128)S(1)}, u32[]{:S(2)}, u32[]{:S(2)}) collective-permute-start(f32[208,128]{1,0:T(8,128)S(1)} %get-tuple-element.14), channel_id=1, source_target_pairs={{240,224},{241,225},{242,226},{243,227},{244,228},{245,229},{246,2... | collective-permute-start | bytes 319496 | tf_op jit(solution)/shard_map/ppermute | solution.py:463
  40.0 5.6 %collective-permute-start.1 = (f32[112,128]{1,0:T(8,128)S(1)}, f32[112,128]{1,0:T(8,128)S(1)}, u32[]{:S(2)}, u32[]{:S(2)}) collective-permute-start(f32[112,128]{1,0:T(8,128)S(1)} %get-tuple-element.15), channel_id=1, source_target_pairs={{0,1},{1,2},{2,3},{3,4},{4,5},{5,6},{6,7},{7,0},{8,9},{9,10},{10,1... | collective-permute-start | bytes 172040 | tf_op jit(solution)/shard_map/ppermute | solution.py:461
  41.4 4.2 %collective-permute-start.2 = (f32[112,128]{1,0:T(8,128)S(1)}, f32[112,128]{1,0:T(8,128)S(1)}, u32[]{:S(2)}, u32[]{:S(2)}) collective-permute-start(f32[112,128]{1,0:T(8,128)S(1)} %get-tuple-element.16), channel_id=1, source_target_pairs={{1,0},{2,1},{3,2},{4,3},{5,4},{6,5},{7,6},{0,7},{9,8},{10,9},{11,1... | collective-permute-start | bytes 172040 | tf_op jit(solution)/shard_map/ppermute | solution.py:462
  47.0 7.8 %copy-start.4 = (f32[2,2]{1,0:T(2,128)S(1)}, f32[2,2]{1,0:T(2,128)}, u32[]{:S(2)}) copy-start(f32[2,2]{1,0:T(2,128)} %flow.3) | copy-start | bytes 52
  47.0 7.8 %copy-start.5 = (bf16[64,192]{1,0:T(8,128)(2,1)S(1)}, bf16[64,192]{1,0:T(8,128)(2,1)}, u32[]{:S(2)}) copy-start(bf16[64,192]{1,0:T(8,128)(2,1)} %constant.9.clone.matrix) | copy-start | bytes 73732
  47.0 31.8 %all-to-all-start.1 = ((f32[16,208,128]{2,1,0:T(8,128)}), f32[16,208,128]{2,1,0:T(8,128)S(1)}, u32[]{:S(2)}, u32[]{:S(2)}) async-start(f32[16,208,128]{2,1,0:T(8,128)} %broadcast_in_dim.6), calls=%async_computation.1 | async-start | bytes 3407872 | tf_op jit(solution)/shard_map/all_to_all | solution.py:466
  78.8 0.8 collective-permute-start.3

commit v4 on v3

v4 whole, which is shorter than its diff:
```python
import jax
import jax.numpy as jnp
import ml_dtypes
import numpy as np
from jax import lax
from jax.experimental import pallas as pl
from jax.experimental.pallas import tpu as pltpu
from jax.sharding import PartitionSpec as P

SECTION_FACTORS = (0.075, 0.05, 0.1125, 0.15, 0.3)
OMEGA = 1.0
DISSIPATION = 0.2

NT = 16
NV = 4
PARTS = 14
CHUNK = 19
HALO = 5
LINES = CHUNK + 2 * HALO
TAIL = 256 - (PARTS - 1) * CHUNK
W = 128
HALF = 8
BLOCKS = 16
NR = 80
ROW = 20
HALF_ZONE = 13
ENDS = HALO * NV
EDGE_PACKS = 8
FIRST_HALF = tuple(range(4, 17))
SECOND_HALF = (20, 21, 22, 23, 24, 0, 1, 2, 3, 17, 18, 19)
SU = (1, 2, 2, 4)
VMEM = pl.BlockSpec(memory_space=pltpu.VMEM)
SMEM = pl.BlockSpec(memory_space=pltpu.SMEM)


def level_matrix():
    offsets = np.arange(NT)[:, None] - np.arange(NT)[None, :]
    angle = np.pi * offsets / NT
    safe = np.where(offsets == 0, 0.5 * np.pi, angle)
    cot = np.cos(safe) / np.sin(safe)
    matrix = np.where(offsets == 0, 0.0, 0.5 * (1.0 - 2.0 * (offsets % 2)) * cot)
    matrix = OMEGA * matrix + 4.0 * DISSIPATION * np.eye(NT)
    matrix = np.kron(np.eye(NV), matrix).astype(np.float32)
    lead = matrix.astype(ml_dtypes.bfloat16)
    rest = (matrix - lead.astype(np.float32)).astype(ml_dtypes.bfloat16)
    return np.concatenate([lead, rest, lead], axis=1)


def params(mib):
    return pltpu.CompilerParams(vmem_limit_bytes=mib << 20)


def place():
    return lax.axis_index("tm"), lax.axis_index("block")


def pack_kernel(state_in, far_in, index_in, weight_in, out, state, far, index, weight, sems):
    copies = [
        pltpu.make_async_copy(source, target, sems.at[i])
        for i, (source, target) in enumerate(
            ((state_in, state), (far_in, far), (index_in, index), (weight_in, weight))
        )
    ]
    for copy in copies:
        copy.start()
    for copy in copies:
        copy.wait()
    _, block = place()

    def fill(rotor):
        for t in range(PARTS):
            first = t * CHUNK if rotor else 256 - (t + 1) * CHUNK
            skip = max(-first, 0)
            count = min(CHUNK, 256 - first) - skip
            for v in range(NV):
                at = v * ROW + skip
                out[t, at : at + count] = state[v, first + skip : first + skip + count]
                out[t, v * ROW + CHUNK : (v + 1) * ROW] = far[v : v + 1]
        lines = []
        for line in range(HALO):
            cell = 255 - line if rotor else line
            lines += [state[v, cell : cell + 1] for v in range(NV)]
        lines += [index[...].astype(jnp.float32)] + [weight[k : k + 1] for k in range(4)]
        for t, half in ((PARTS, FIRST_HALF), (PARTS + 1, SECOND_HALF)):
            for i, k in enumerate(half):
                out[t, i : i + 1] = lines[k]

    @pl.when(block < HALF)
    def _():
        fill(True)

    @pl.when(block >= HALF)
    def _():
        fill(False)


def line_address(side, r, v):
    return v * ROW + jnp.where(side == 0, r, CHUNK - 1 - r)


def zone_kernel(lines, zone, ends_up, ends_down):
    _, block = place()
    side = block // HALF
    for i in range(HALF_ZONE):
        tile = lines[pl.ds(i, NT, stride=NR), :]
        for b in range(BLOCKS):
            zone[b, i * NT : (i + 1) * NT] = tile
    for i in range(ENDS):
        r, v = i // NV, i % NV
        at = slice(i * NT, (i + 1) * NT)
        ends_up[at] = lines[pl.ds(line_address(side, CHUNK - HALO + r, v), NT, stride=NR), :]
        ends_down[at] = lines[pl.ds(line_address(side, r, v), NT, stride=NR), :]


def line_tile(lines, below, above, t, side, r, v):
    if r < 0:
        at = (r + HALO) * NV + v
        tile = below[at * NT : (at + 1) * NT]
        if r == -1:
            tile = jnp.where(t == 0, lines[pl.ds(v * ROW + CHUNK, NT, stride=NR), :], tile)
        return tile
    if r < CHUNK:
        return lines[pl.ds(line_address(side, r, v), NT, stride=NR), :]
    at = (r - CHUNK) * NV + v
    return above[at * NT : (at + 1) * NT]


def edge_kernel(lines, below, above, left, right):
    t, block = place()
    side = block // HALF
    part = lax.broadcasted_iota(jnp.int32, (NT, W), 1) // 8
    for p in range(EDGE_PACKS):
        left_pack = jnp.zeros((NT, W), jnp.float32)
        right_pack = jnp.zeros((NT, W), jnp.float32)
        for k in range(16):
            m = p * 16 + k
            if m >= LINES * NV:
                break
            tile = line_tile(lines, below, above, t, side, m // NV - HALO, m % NV)
            moved = tile if k == 0 else pltpu.roll(tile, 8 * k, 1)
            left_pack = jnp.where(part == k, moved, left_pack)
            moved = tile if k == 15 else pltpu.roll(tile, 8 * k + 8, 1)
            right_pack = jnp.where(part == k, moved, right_pack)
        left[p * NT : (p + 1) * NT] = left_pack
        right[p * NT : (p + 1) * NT] = right_pack


def coefficients(flow, side):
    sign = (0.5, -0.5)[side] if isinstance(side, int) else jnp.where(side == 0, 0.5, -0.5)
    along = sign * flow[side, 0]
    across = 0.5 * flow[side, 1]
    return sign, along - DISSIPATION, -along - DISSIPATION, across - DISSIPATION, -across - DISSIPATION


def rates(coefs, up, down, nxt, prv, timed):
    sign, cu, cd, cn, cp = coefs
    plain = [timed[v] + (cu * up[v] + cd * down[v]) + (cn * nxt[v] + cp * prv[v]) for v in range(NV)]
    mixed = sign * (up[1] - down[1]) + 0.5 * (nxt[2] - prv[2])
    pressure_up = sign * (up[3] - down[3])
    pressure_next = 0.5 * (nxt[3] - prv[3])
    return [plain[0] + mixed, plain[1] + pressure_up, plain[2] + pressure_next, plain[3] + mixed]


def level_product(matrix, values):
    lead = values.astype(jnp.bfloat16)
    rest = (values - lead.astype(jnp.float32)).astype(jnp.bfloat16)
    return jnp.dot(matrix, jnp.concatenate([lead, lead, rest], axis=0), preferred_element_type=jnp.float32)


def split(lines):
    return [lines[v * NT : (v + 1) * NT] for v in range(NV)]


def zone_tile(first_half, second_half, side, j, k):
    source, at = (first_half, FIRST_HALF.index(k)) if k in FIRST_HALF else (second_half, SECOND_HALF.index(k))
    return source[HALF * side + j, at * NT : (at + 1) * NT, :]


def start_kernel(high, table, ghosts, ordered):
    def tile(side, j, k):
        return zone_tile(None, high, side, j, k)

    def interpolate_first(side, j):
        first = tile(side, j, 20).astype(jnp.int32)
        parts = []
        for h in range(2):
            at = slice(8 * h, 8 * h + 8)
            totals = [None] * NV
            for k in range(4):
                source = (first[at] + k) & (HALF * W - 1)
                within, which = source & (W - 1), source >> 7
                weight = tile(side, j, 21 + k)[at]
                picked = [None] * NV
                for m in range(HALF):
                    here = which == m
                    for v in range(NV):
                        face = tile(1 - side, m, v)[at]
                        got = jnp.take_along_axis(face, within, axis=1, mode="promise_in_bounds")
                        picked[v] = got if m == 0 else jnp.where(here, got, picked[v])
                totals = [weight * picked[v] if k == 0 else totals[v] + weight * picked[v] for v in range(NV)]
            parts.append(totals)
        return [jnp.concatenate([parts[0][v], parts[1][v]], axis=0) for v in range(NV)]

    def order_weights(side, level):
        rows = lambda k: table[pl.ds(HALF * side * HALF_ZONE * NT + k * NT + level, HALF, stride=HALF_ZONE * NT), :]
        first = rows(0).astype(jnp.int32)
        within, which = first & (W - 1), first >> 7
        weight = [rows(1 + k) for k in range(4)]
        eight = lax.broadcasted_iota(jnp.int32, (HALF, W), 0)
        many = lax.broadcasted_iota(jnp.int32, (W, W), 0)
        spread, chosen = [], []
        for j in range(HALF):
            here = jnp.broadcast_to(which[j : j + 1], (HALF, W)) == eight
            spread.append(
                jnp.concatenate(
                    [jnp.where(here, jnp.broadcast_to(weight[k][j : j + 1], (HALF, W)), 0.0) for k in range(4)], axis=0
                )
            )
            hit = jnp.broadcast_to(within[j : j + 1], (W, W)) == many
            chosen.append(jnp.where(hit, 1.0, 0.0).astype(jnp.bfloat16))
        spread = jnp.concatenate(spread, axis=1)
        chosen = jnp.concatenate(chosen, axis=1)
        lead = spread.astype(jnp.bfloat16)
        rest = (spread - lead.astype(jnp.float32)).astype(jnp.bfloat16)
        both = lax.dot_general(
            jnp.concatenate([lead, rest], axis=0), chosen, (((1,), (1,)), ((), ())), preferred_element_type=jnp.float32
        )
        both = both[:32] + both[32:]
        for k in range(4):
            ordered[side, k, pl.ds(level, HALF, stride=NT), :] = both[8 * k : 8 * k + 8]

    def step(j, _):
        for side in range(2):
            ghost = interpolate_first(side, j)
            for v in range(NV):
                ghosts[side, v, j] = ghost[v]
            order_weights(side, 2 * j)
            order_weights(side, 2 * j + 1)
        return 0

    lax.fori_loop(0, HALF, step, 0)


def chain(
    low, high, given_ghosts, ordered, matrix, flow, out,
    cur0, cur1, nexts0, nexts1, prevs0, prevs1, shifted, weighed, ghosts, applied,
):
    _, block = place()
    own_side, own = block // HALF, block % HALF
    lane = lax.broadcasted_iota(jnp.int32, (NT, W), 1)
    cur, nexts, prevs = (cur0, cur1), (nexts0, nexts1), (prevs0, prevs1)

    def tile(side, j, k):
        return zone_tile(low, high, side, j, k)

    def value(section, side, line, v, j):
        if section == 0:
            return tile(side, j, line * NV + v)
        return cur[section % 2][side, line, v, j]

    def keep_rolled(section, side, line, v, j, values, shift=False):
        nexts[section % 2][side, line, v, j] = pltpu.roll(values, W - 1, 1)
        prevs[section % 2][side, line, v, j] = pltpu.roll(values, 1, 1)
        if shift:
            shifted[0, side, v, j] = pltpu.roll(values, W - 2, 1)
            shifted[1, side, v, j] = pltpu.roll(values, W - 3, 1)

    def weigh(section, side, m):
        other, after = 1 - side, (m + 1) % HALF
        weight = [ordered[side, k, pl.ds(pl.multiple_of(m * NT, NT), NT), :] for k in range(4)]
        for v in range(NV):
            total = weight[0] * value(section, other, 0, v, m)
            for k in range(1, 4):
                if k == 1:
                    here, there = nexts[section % 2][other, 0, v, m], nexts[section % 2][other, 0, v, after]
                else:
                    here, there = shifted[k - 2, other, v, m], shifted[k - 2, other, v, after]
                total = total + weight[k] * jnp.where(lane >= W - k, there, here)
            weighed[side, v, m] = total

    def interpolate(side, j):
        first = tile(side, j, 20).astype(jnp.int32)
        within, which = first & (W - 1), first >> 7
        parts = []
        for h in range(2):
            at = slice(8 * h, 8 * h + 8)
            picked = [None] * NV
            for m in range(HALF):
                here = which[at] == m
                for v in range(NV):
                    got = jnp.take_along_axis(weighed[side, v, m, at], within[at], axis=1, mode="promise_in_bounds")
                    picked[v] = got if m == 0 else jnp.where(here, got, picked[v])
            parts.append(picked)
        return [jnp.concatenate([parts[0][v], parts[1][v]], axis=0) for v in range(NV)]

    def first_rolls(j, _):
        for side in range(2):
            for line in range(4):
                for v in range(NV):
                    keep_rolled(0, side, line, v, j, value(0, side, line, v, j))
        return 0

    lax.fori_loop(0, HALF, first_rolls, 0)
    for s in range(4):
        sides = (0, 1) if s < 3 else (1 - own_side,)

        def weigh_step(m, _, s=s):
            weigh(s, 0, m)
            weigh(s, 1, m)
            return 0

        def advance(side, j, s=s):
            after, before = (j + 1) % HALF, (j + HALF - 1) % HALF
            coefs = coefficients(flow, side)
            if s == 0:
                ghost = [given_ghosts[side, v, j] for v in range(NV)]
            else:
                ghost = interpolate(side, j)
                for v in range(NV):
                    ghosts[s % 2, side, v, j] = ghost[v]
            lines = 4 - s
            here = [[value(s, side, line, v, j) for v in range(NV)] for line in range(lines + 1)]
            product = level_product(
                matrix[...], jnp.concatenate([jnp.concatenate(here[line], axis=0) for line in range(lines)], axis=1)
            )
            for line in reversed(range(lines)):
                up = ghost if line == 0 else here[line - 1]
                nxt = [
                    jnp.where(lane == W - 1, nexts[s % 2][side, line, v, after], nexts[s % 2][side, line, v, j])
                    for v in range(NV)
                ]
                prv = [
                    jnp.where(lane == 0, prevs[s % 2][side, line, v, before], prevs[s % 2][side, line, v, j])
                    for v in range(NV)
                ]
                timed = split(product[:, line * W : (line + 1) * W])
                rate = rates(coefs, up, here[line + 1], nxt, prv, timed)
                for v in range(NV):
                    result = value(0, side, line, v, j) - SECTION_FACTORS[s] * rate[v]
                    cur[(s + 1) % 2][side, line, v, j] = result
                    if line < max(lines - 1, 1):
                        keep_rolled(s + 1, side, line, v, j, result, line == 0)
        def section_step(j, _, advance=advance, sides=sides):
            for side in sides:
                advance(side, j)
            return 0

        if s > 0:
            lax.fori_loop(0, HALF, weigh_step, 0, unroll=2)
        lax.fori_loop(0, HALF, section_step, 0, unroll=SU[s])
        if s == 3:

            def own_step(step, _):
                j = (own + HALF - 1 + step) % HALF
                ghost = interpolate(own_side, j)
                for v in range(NV):
                    ghosts[1, own_side, v, j] = ghost[v]
                return 0

            lax.fori_loop(0, 3, own_step, 0)
        kept = given_ghosts if s == 0 else ghosts.at[s % 2]
        for v in range(NV):
            at = slice(v * NT, (v + 1) * NT)
            applied[s, at, :W] = kept[own_side, v, own]
            after = kept[own_side, v, (own + 1) % HALF]
            before = kept[own_side, v, (own + HALF - 1) % HALF]
            applied[s, at, W:] = jnp.where(lane < W // 2, after, before)

    def last_weigh(m, _):
        weigh(4, own_side, m)
        return 0

    lax.fori_loop(0, HALF, last_weigh, 0, unroll=4)
    got = interpolate(own_side, own)
    for v in range(NV):
        at = slice(v * NT, (v + 1) * NT)
        applied[4, at, :W] = got[v]
        applied[4, at, W:] = got[v]

    coefs = coefficients(flow, own_side)
    zero = jnp.zeros((NV * NT, 2 * W), jnp.float32)
    response = []
    for s in range(5):
        product = None
        if s:
            product = level_product(matrix[...], jnp.concatenate(response, axis=1))
        padded = [applied[s]] + response + [zero, zero]
        new = []
        for line in range(s + 1):
            here = padded[line + 1]
            if line < s:
                nxt, prv = pltpu.roll(here, 2 * W - 1, 1), pltpu.roll(here, 1, 1)
                timed = product[:, 2 * W * line : 2 * W * (line + 1)]
            else:
                nxt = prv = timed = zero
            rate = rates(coefs, split(padded[line]), split(padded[line + 2]), split(nxt), split(prv), split(timed))
            new.append(-SECTION_FACTORS[s] * jnp.concatenate(rate, axis=0))
        response = new

    for line in range(HALO):
        for v in range(NV):
            cell = jnp.where(own_side == 0, HALO - 1 - line, line)
            out[pl.ds(v * ROW + cell, NT, stride=NR), :] = response[line][v * NT : (v + 1) * NT, :W]


def bulk(lines, below, above, from_left, from_right, matrix, flow, out, start, even, odd):
    t, block = place()
    side = block // HALF
    lane = lax.broadcasted_iota(jnp.int32, (NT, W), 1)
    for m in range(LINES * NV):
        r, v = m // NV - HALO, m % NV
        at = slice(v * NT, (v + 1) * NT)
        start[m // NV, at, :W] = line_tile(lines, below, above, t, side, r, v)
        p, k = m // 16, m % 16
        after = from_right[p * NT : (p + 1) * NT]
        after = after if k == 0 else pltpu.roll(after, W - 8 * k, 1)
        before = from_left[p * NT : (p + 1) * NT]
        before = before if k == 15 else pltpu.roll(before, 120 - 8 * k, 1)
        start[m // NV, at, W:] = jnp.where(lane < W // 2, after, before)
    coefs = coefficients(flow, side)
    group = 4
    for s in range(5):
        now = start if s == 0 else (even if s % 2 == 0 else odd)
        new = odd if s % 2 == 0 else even

        @pl.when(t == PARTS - 1)
        def _(now=now):
            now[HALO + TAIL] = jnp.zeros((NV * NT, 2 * W), jnp.float32)

        if s > 0:

            @pl.when(t == 0)
            def _(now=now):
                now[HALO - 1] = start[HALO - 1]

        first = (1, 1, 3, 3, 5)[s]

        def line_step(step, _, now=now, new=new, s=s, first=first):
            i = first + group * step
            here = [now[i - 1 + g] for g in range(group + 2)]
            product = level_product(matrix[...], jnp.concatenate(here[1:-1], axis=1))
            for g in range(group):
                line = here[g + 1]
                nxt = pltpu.roll(line, 2 * W - 1, 1)
                prv = pltpu.roll(line, 1, 1)
                timed = split(product[:, 2 * W * g : 2 * W * (g + 1)])
                rate = rates(coefs, split(here[g + 2]), split(here[g]), split(nxt), split(prv), timed)
                base = split(start[i + g])
                for v in range(NV):
                    result = base[v] - SECTION_FACTORS[s] * rate[v]
                    if s < 4:
                        new[i + g, v * NT : (v + 1) * NT] = result
                    else:
                        cell = jnp.where(side == 0, i + g - HALO, CHUNK + HALO - i - g)
                        out[pl.ds(v * ROW + cell, NT, stride=NR), :] = result[:, :W]
            return 0

        lax.fori_loop(0, (LINES - 2 * first + group - 1) // group, line_step, 0)


def main_kernel(
    low, high, given_ghosts, ordered, lines, below, above, from_left, from_right, matrix, flow, out, *scratch
):
    t, _ = place()

    @pl.when(t < PARTS)
    def _():
        bulk(lines, below, above, from_left, from_right, matrix, flow, out, *scratch[:3])

    @pl.when(t >= PARTS)
    def _():
        chain(low, high, given_ghosts, ordered, matrix, flow, out, *scratch[3:])


def unpack_kernel(shares, out):
    _, block = place()

    def fill(rotor):
        for t in range(PARTS):
            first = t * CHUNK if rotor else 256 - (t + 1) * CHUNK
            skip = max(-first, 0)
            count = min(CHUNK, 256 - first) - skip
            for v in range(NV):
                at = v * ROW + skip + (0 if rotor else 1)
                share = shares[t, at : at + count]
                if t == PARTS - 1:
                    added = shares[NT - 1, v * ROW : v * ROW + HALO]
                    none = jnp.zeros((count - HALO, W), jnp.float32)
                    share = share + jnp.concatenate([none, added] if rotor else [added, none], axis=0)
                out[v, first + skip : first + skip + count] = share

    @pl.when(block < HALF)
    def _():
        fill(True)

    @pl.when(block >= HALF)
    def _():
        fill(False)


def f32(*shape):
    return jax.ShapeDtypeStruct(shape, jnp.float32)


def cost(flops, nbytes):
    return pl.CostEstimate(flops=flops, bytes_accessed=nbytes, transcendentals=0)


def shards(state, far_field, face_index, face_weight, mean_flow):
    matrix = jnp.asarray(level_matrix())
    shares = pl.pallas_call(
        pack_kernel,
        out_shape=f32(NT, NR, W),
        in_specs=[pl.BlockSpec(memory_space=pltpu.HBM)] * 4,
        out_specs=VMEM,
        scratch_shapes=[
            pltpu.VMEM((NV, 256, W), jnp.float32),
            pltpu.VMEM((NV, W), jnp.float32),
            pltpu.VMEM((1, W), jnp.int32),
            pltpu.VMEM((NV, W), jnp.float32),
            pltpu.SemaphoreType.DMA((4,)),
        ],
        compiler_params=params(16),
        name="pack",
    )(state[0], far_field[0], face_index, face_weight[0])
    lines = lax.all_to_all(shares, "tm", 0, 0, tiled=True).reshape(NT * NR, W)
    zone, ends_up, ends_down = pl.pallas_call(
        zone_kernel,
        out_shape=[f32(BLOCKS, HALF_ZONE * NT, W)] + [f32(ENDS * NT, W)] * 2,
        in_specs=[VMEM],
        out_specs=[VMEM] * 3,
        compiler_params=params(16),
        name="zone",
    )(lines)
    high = lax.all_to_all(zone, "block", 0, 0, tiled=True)
    below = lax.ppermute(ends_up, "tm", [(i, i + 1) for i in range(PARTS - 1)])
    above = lax.ppermute(ends_down, "tm", [(i + 1, i) for i in range(PARTS - 1)])
    left, right = pl.pallas_call(
        edge_kernel,
        out_shape=[f32(EDGE_PACKS * NT, W)] * 2,
        in_specs=[VMEM] * 3,
        out_specs=[VMEM] * 2,
        compiler_params=params(16),
        name="edges",
    )(lines, below, above)
    rights = [
        (i * BLOCKS + b, i * BLOCKS + b // HALF * HALF + (b + 1) % HALF) for i in range(PARTS) for b in range(BLOCKS)
    ]
    from_left = lax.ppermute(right, ("tm", "block"), rights)
    from_right = lax.ppermute(left, ("tm", "block"), [(b, a) for a, b in rights])
    high, from_left, from_right = lax.optimization_barrier((high, from_left, from_right))
    low = lax.ppermute(high, "tm", [(PARTS, PARTS + 1)])
    given_ghosts, ordered = pl.pallas_call(
        start_kernel,
        out_shape=[f32(2, NV, HALF, NT, W), f32(2, 4, HALF * NT, W)],
        in_specs=[VMEM] * 2,
        out_specs=[VMEM] * 2,
        compiler_params=params(16),
        cost_estimate=cost(4 * 10**9, 16 << 20),
        name="start",
    )(high, high.reshape(BLOCKS * HALF_ZONE * NT, W))
    grid = pltpu.VMEM((LINES + 3, NV * NT, 2 * W), jnp.float32)
    lines_of = pltpu.VMEM((2, 4, NV, HALF, NT, W), jnp.float32)
    faces_of = pltpu.VMEM((2, 2, NV, HALF, NT, W), jnp.float32)
    done = pl.pallas_call(
        main_kernel,
        out_shape=f32(NT * NR, W),
        in_specs=[VMEM] * 10 + [SMEM],
        out_specs=VMEM,
        scratch_shapes=[grid] * 3
        + [lines_of] * 6
        + [faces_of, pltpu.VMEM((2, NV, HALF, NT, W), jnp.float32)]
        + [faces_of, pltpu.VMEM((5, NV * NT, 2 * W), jnp.float32)],
        compiler_params=params(32),
        cost_estimate=cost(8 * 10**9, 64 << 20),
        name="main",
    )(low, high, given_ghosts, ordered, lines, below, above, from_left, from_right, matrix, mean_flow)
    done = lax.all_to_all(done.reshape(NT, NR, W), "tm", 0, 0, tiled=True)
    result = pl.pallas_call(
        unpack_kernel,
        out_shape=f32(NV, 256, W),
        in_specs=[VMEM],
        out_specs=VMEM,
        compiler_params=params(16),
        name="unpack",
    )(done)
    return result[None]


def solution(mesh):
    in_specs = (
        P("tm", None, None, "block"),
        P("tm", None, "block"),
        P("tm", "block"),
        P("tm", None, "block"),
        P(),
    )
    out_specs = P("tm", None, None, "block")
    return jax.shard_map(shards, mesh=mesh, in_specs=in_specs, out_specs=out_specs, check_vma=False)
```

time: 133 us -> 113 us (0.85)
  Pallas kernels: 37.3 us -> 16.5 us
  starting transfers between devices: 13.1 us -> 19.4 us
  waiting for transfers between devices: 17.7 us -> 14.6 us
  blocking collectives: 60.5 us -> 57.8 us
    pallas_call x4 -> x5, Pallas kernels: 37.1 us -> 16.4 us  [the longest x1 8.83 us: shards(): pl.pallas_call(main_kernel, out_shape=f32(NT * NR, W), in_specs=[VMEM] *...]
    all_to_all x1, waiting for transfers between devices: 15.9 us -> 0.01 us  [shards(): high = lax.all_to_all(zone, 'block', 0, 0, tiled=True)]
    ppermute x4 -> x5, waiting for transfers between devices: 1.75 us -> 14.6 us  [the longest x1 9.81 us: shards(): from_left = lax.ppermute(right, ('tm', 'block'), rights)]
    ppermute x4 -> x5, starting transfers between devices: 5.26 us -> 12.7 us  [the longest x1 4.03 us: shards(): lax.ppermute(left, ('tm', 'block'), [(b, a) for a, b in rights])]
    all_to_all x1, blocking collectives: 35.5 us -> 30 us  [shards(): lines = lax.all_to_all(shares, 'tm', 0, 0, tiled=True).reshape(NT * NR, W)]
    all_to_all x1, blocking collectives: 25 us -> 27.8 us  [shards(): done = lax.all_to_all(done.reshape(NT, NR, W), 'tm', 0, 0, tiled=True)]
    unnamed x12 -> x14, local copies, waits for them, and re-layouts: 3.07 us -> 4.26 us
  transfers between devices with their start and end apart: 5 -> 6, of which waited for: 2 -> 3; matrix products, arithmetic and copies ran while one was open for 0% -> 0% of each run, Pallas kernels for 6% -> 6%
where the time goes in v4:
time: 113 us
  blocking collectives  57.8 us (51%)
  starting transfers between devices  19.4 us (17%)
  Pallas kernels  16.5 us (15%)
  waiting for transfers between devices  14.6 us (13%)
  local copies, waits for them, and re-layouts  4.26 us (4%)
    all_to_all x1, blocking collectives, shards(): lines = lax.all_to_all(shares, 'tm', 0, 0, tiled=True).reshape(NT * NR, W)  30 us
    all_to_all x1, blocking collectives, shards(): done = lax.all_to_all(done.reshape(NT, NR, W), 'tm', 0, 0, tiled=True)  27.8 us
    ppermute x1, waiting for transfers between devices, shards(): from_left = lax.ppermute(right, ('tm', 'block'), rights)  9.81 us
    pallas_call x1, Pallas kernels, shards(): pl.pallas_call(main_kernel, out_shape=f32(NT * NR, W), in_specs=[VMEM] *...  8.83 us
    all_to_all x1, starting transfers between devices, shards(): high = lax.all_to_all(zone, 'block', 0, 0, tiled=True)  6.75 us
    pallas_call x1, Pallas kernels, shards(): pl.pallas_call(start_kernel, out_shape=[f32(2, NV, HALF, NT, W), f32(2, 4...  5.96 us
    ppermute x1, waiting for transfers between devices, shards(): lax.ppermute(ends_down, 'tm', [(i + 1, i) for i in range(PARTS - 1)])  4.69 us
    unnamed x14, local copies, waits for them, and re-layouts  4.26 us
  transfers between devices with their start and end apart: 6, of which 3 were waited for; matrix products, arithmetic and copies ran while one was open for 0% of the time, Pallas kernels for 6%

profile of v4, /device:TPU:1, one launch (start us, length us, event | category | flops | bytes accessed | tf_op | source)
XLA Modules:
  0.0 112.7 jit_solution(17371277684342867712)
XLA Ops:
  0.0 0.0 copy-start.1
  0.0 1.0 copy-done.1
  1.0 0.0 copy-start.2
  1.0 0.7 copy-done.2
  1.7 0.7 copy-done.3
  2.4 0.7 copy-done.4
  3.1 0.1 pack.1
  3.2 30.0 %all_to_all.15 = f32[16,80,128]{2,1,0:T(8,128)S(1)} all-to-all(f32[16,80,128]{2,1,0:T(8,128)S(1)} %pack.1), channel_id=1, replica_groups=mesh['tm'=16,'block'=16] {'tm'}, dimensions={0} | all-to-all | bytes 1310720 | tf_op jit(solution)/shard_map/all_to_all | solution.py:526
  33.2 0.2 zone.1
  33.4 0.0 copy-start
  33.5 1.2 %copy-done = f32[16,208,128]{2,1,0:T(8,128)} copy-done((f32[16,208,128]{2,1,0:T(8,128)}, f32[16,208,128]{2,1,0:T(8,128)S(1)}, u32[]{:S(2)}) %copy-start) | copy-done | bytes 1703960
  34.6 6.8 %all-to-all-start.1 = ((f32[16,208,128]{2,1,0:T(8,128)}), f32[16,208,128]{2,1,0:T(8,128)S(1)}, u32[]{:S(2)}, u32[]{:S(2)}) async-start(f32[16,208,128]{2,1,0:T(8,128)} %copy-done), calls=%async_computation.1 | async-start | bytes 3407872 | tf_op jit(solution)/shard_map/all_to_all | solution.py:535
  41.4 2.2 %collective-permute-start = (f32[320,128]{1,0:T(8,128)S(1)}, f32[320,128]{1,0:T(8,128)S(1)}, u32[]{:S(2)}, u32[]{:S(2)}) collective-permute-start(f32[320,128]{1,0:T(8,128)S(1)} %get-tuple-element.16), channel_id=1, source_target_pairs={{0,16},{16,32},{32,48},{48,64},{64,80},{80,96},{96,112},{112,128},... | collective-permute-start | bytes 491528 | tf_op jit(solution)/shard_map/ppermute | solution.py:536
  43.6 2.1 %collective-permute-start.1 = (f32[320,128]{1,0:T(8,128)S(1)}, f32[320,128]{1,0:T(8,128)S(1)}, u32[]{:S(2)}, u32[]{:S(2)}) collective-permute-start(f32[320,128]{1,0:T(8,128)S(1)} %get-tuple-element.17), channel_id=1, source_target_pairs={{16,0},{32,16},{48,32},{64,48},{80,64},{96,80},{112,96},{128,112},... | collective-permute-start | bytes 491528 | tf_op jit(solution)/shard_map/ppermute | solution.py:537
  45.7 0.1 collective-permute-done.below
  45.9 4.7 %collective-permute-done.1.above = f32[320,128]{1,0:T(8,128)S(1)} collective-permute-done((f32[320,128]{1,0:T(8,128)S(1)}, f32[320,128]{1,0:T(8,128)S(1)}, u32[]{:S(2)}, u32[]{:S(2)}) %collective-permute-start.1) | collective-permute-done | bytes 163872 | tf_op jit(solution)/shard_map/ppermute | solution.py:537
  50.6 0.5 edges.1
  51.1 3.6 %collective-permute-start.2 = (f32[128,128]{1,0:T(8,128)S(1)}, f32[128,128]{1,0:T(8,128)S(1)}, u32[]{:S(2)}, u32[]{:S(2)}) collective-permute-start(f32[128,128]{1,0:T(8,128)S(1)} %get-tuple-element.18), channel_id=1, source_target_pairs={{0,1},{1,2},{2,3},{3,4},{4,5},{5,6},{6,7},{7,0},{8,9},{9,10},{10,1... | collective-permute-start | bytes 196616 | tf_op jit(solution)/shard_map/ppermute | solution.py:549
  54.7 4.0 %collective-permute-start.3 = (f32[128,128]{1,0:T(8,128)S(1)}, f32[128,128]{1,0:T(8,128)S(1)}, u32[]{:S(2)}, u32[]{:S(2)}) collective-permute-start(f32[128,128]{1,0:T(8,128)S(1)} %get-tuple-element.19), channel_id=1, source_target_pairs={{1,0},{2,1},{3,2},{4,3},{5,4},{6,5},{7,6},{0,7},{9,8},{10,9},{11,1... | collective-permute-start | bytes 196616 | tf_op jit(solution)/shard_map/ppermute | solution.py:550
  58.7 9.8 %collective-permute-done.2.from_left = f32[128,128]{1,0:T(8,128)S(1)} collective-permute-done((f32[128,128]{1,0:T(8,128)S(1)}, f32[128,128]{1,0:T(8,128)S(1)}, u32[]{:S(2)}, u32[]{:S(2)}) %collective-permute-start.2) | collective-permute-done | bytes 65568 | tf_op jit(solution)/shard_map/ppermute | solution.py:549
  68.5 0.0 collective-permute-done.3.from_right
  68.5 0.0 all-to-all-done.1.high
  68.5 0.8 collective-permute-start.4
  69.3 0.0 copy-start.5
  69.3 0.0 copy-start.6
  69.3 6.0 %start.1 = (f32[2,4,8,16,128]{4,3,2,1,0:T(8,128)S(1)}, f32[2,4,128,128]{3,2,1,0:T(8,128)S(1)}) custom-call(f32[16,208,128]{2,1,0:T(8,128)S(1)} %all-to-all-done.1.high, f32[3328,128]{1,0:T(8,128)S(1)} %bitcast.10), custom_call_target="tpu_custom_call" | custom-call | flops 4000000000 | bytes 16777216 | tf_op jit(solution)/shard_map/start/pallas_call | solution.py:553
  75.3 0.0 collective-permute-done.4.low
  75.3 0.0 copy-done.5
  75.3 0.0 copy-done.6
  75.3 8.8 %main.1 = f32[1280,128]{1,0:T(8,128)S(1)} custom-call(f32[16,208,128]{2,1,0:T(8,128)S(1)} %collective-permute-done.4.low, f32[16,208,128]{2,1,0:T(8,128)S(1)} %all-to-all-done.1.high, f32[2,4,8,16,128]{4,3,2,1,0:T(8,128)S(1)} %get-tuple-element.21.given_ghosts, f32[2,4,128,128]{3,2,1,0:T(8,128)S(1)} %get-tuple-element.22.ordered, f32[1280,128]{1,0:T(8,128)S(1)} %bitcast.9, ...), custom_call_target="tpu_custom_call" | custom-call | flops 8000000000 | bytes 67108864 | tf_op jit(solution)/shard_map/main/pallas_call | solution.py:565
  84.1 27.8 %all_to_all.16.shares = f32[16,80,128]{2,1,0:T(8,128)S(1)} all-to-all(f32[16,80,128]{2,1,0:T(8,128)S(1)} %bitcast.11), channel_id=1, replica_groups=mesh['tm'=16,'block'=16] {'tm'}, dimensions={0} | all-to-all | bytes 1310720 | tf_op jit(solution)/shard_map/all_to_all | solution.py:578
  111.9 0.8 unpack.1
  (2 shorter events, 0.0 us)
Async XLA Ops:
  0.0 1.0 copy-start.1
  1.0 0.7 copy-start.2
  1.7 0.7 copy-start.3
  2.4 0.7 copy-start.4
  33.4 1.2 %copy-start = (f32[16,208,128]{2,1,0:T(8,128)}, f32[16,208,128]{2,1,0:T(8,128)S(1)}, u32[]{:S(2)}) copy-start(f32[16,208,128]{2,1,0:T(8,128)S(1)} %get-tuple-element.15) | copy-start | bytes 5111812
  34.6 33.9 %all-to-all-start.1 = ((f32[16,208,128]{2,1,0:T(8,128)}), f32[16,208,128]{2,1,0:T(8,128)S(1)}, u32[]{:S(2)}, u32[]{:S(2)}) async-start(f32[16,208,128]{2,1,0:T(8,128)} %copy-done), calls=%async_computation.1 | async-start | bytes 3407872 | tf_op jit(solution)/shard_map/all_to_all | solution.py:535
  41.4 4.5 %collective-permute-start = (f32[320,128]{1,0:T(8,128)S(1)}, f32[320,128]{1,0:T(8,128)S(1)}, u32[]{:S(2)}, u32[]{:S(2)}) collective-permute-start(f32[320,128]{1,0:T(8,128)S(1)} %get-tuple-element.16), channel_id=1, source_target_pairs={{0,16},{16,32},{32,48},{48,64},{64,80},{80,96},{96,112},{112,128},... | collective-permute-start | bytes 491528 | tf_op jit(solution)/shard_map/ppermute | solution.py:536
  43.6 6.9 %collective-permute-start.1 = (f32[320,128]{1,0:T(8,128)S(1)}, f32[320,128]{1,0:T(8,128)S(1)}, u32[]{:S(2)}, u32[]{:S(2)}) collective-permute-start(f32[320,128]{1,0:T(8,128)S(1)} %get-tuple-element.17), channel_id=1, source_target_pairs={{16,0},{32,16},{48,32},{64,48},{80,64},{96,80},{112,96},{128,112},... | collective-permute-start | bytes 491528 | tf_op jit(solution)/shard_map/ppermute | solution.py:537
  51.1 17.4 %collective-permute-start.2 = (f32[128,128]{1,0:T(8,128)S(1)}, f32[128,128]{1,0:T(8,128)S(1)}, u32[]{:S(2)}, u32[]{:S(2)}) collective-permute-start(f32[128,128]{1,0:T(8,128)S(1)} %get-tuple-element.18), channel_id=1, source_target_pairs={{0,1},{1,2},{2,3},{3,4},{4,5},{5,6},{6,7},{7,0},{8,9},{9,10},{10,1... | collective-permute-start | bytes 196616 | tf_op jit(solution)/shard_map/ppermute | solution.py:549
  54.7 13.9 %collective-permute-start.3 = (f32[128,128]{1,0:T(8,128)S(1)}, f32[128,128]{1,0:T(8,128)S(1)}, u32[]{:S(2)}, u32[]{:S(2)}) collective-permute-start(f32[128,128]{1,0:T(8,128)S(1)} %get-tuple-element.19), channel_id=1, source_target_pairs={{1,0},{2,1},{3,2},{4,3},{5,4},{6,5},{7,6},{0,7},{9,8},{10,9},{11,1... | collective-permute-start | bytes 196616 | tf_op jit(solution)/shard_map/ppermute | solution.py:550
  68.5 6.8 %collective-permute-start.4 = (f32[16,208,128]{2,1,0:T(8,128)S(1)}, f32[16,208,128]{2,1,0:T(8,128)S(1)}, u32[]{:S(2)}, u32[]{:S(2)}) collective-permute-start(f32[16,208,128]{2,1,0:T(8,128)S(1)} %all-to-all-done.1.high), channel_id=1, source_target_pairs={{224,240},{225,241},{226,242},{227,243},{228,244},{229,245},{230,2... | collective-permute-start | bytes 5111816 | tf_op jit(solution)/shard_map/ppermute | solution.py:552
  69.3 6.0 %copy-start.5 = (f32[2,2]{1,0:T(2,128)S(1)}, f32[2,2]{1,0:T(2,128)}, u32[]{:S(2)}) copy-start(f32[2,2]{1,0:T(2,128)} %flow.1) | copy-start | bytes 52
  69.3 6.0 %copy-start.6 = (bf16[64,192]{1,0:T(8,128)(2,1)S(1)}, bf16[64,192]{1,0:T(8,128)(2,1)}, u32[]{:S(2)}) copy-start(bf16[64,192]{1,0:T(8,128)(2,1)} %constant.2.clone.matrix) | copy-start | bytes 73732

commit v5 on v4

--- a/solution.py
+++ b/solution.py
@@ -30,6 +30,7 @@
 SECOND_HALF = (20, 21, 22, 23, 24, 0, 1, 2, 3, 17, 18, 19)
 SU = (1, 2, 2, 4)
 VMEM = pl.BlockSpec(memory_space=pltpu.VMEM)
+HBM = pl.BlockSpec(memory_space=pltpu.HBM)
 SMEM = pl.BlockSpec(memory_space=pltpu.SMEM)
 
 
@@ -238,7 +239,9 @@
             order_weights(side, 2 * j + 1)
         return 0
 
-    lax.fori_loop(0, HALF, step, 0)
+    @pl.when(place()[0] >= PARTS)
+    def _():
+        lax.fori_loop(0, HALF, step, 0)
 
 
 def chain(
@@ -293,14 +296,6 @@
             parts.append(picked)
         return [jnp.concatenate([parts[0][v], parts[1][v]], axis=0) for v in range(NV)]
 
-    def first_rolls(j, _):
-        for side in range(2):
-            for line in range(4):
-                for v in range(NV):
-                    keep_rolled(0, side, line, v, j, value(0, side, line, v, j))
-        return 0
-
-    lax.fori_loop(0, HALF, first_rolls, 0)
     for s in range(4):
         sides = (0, 1) if s < 3 else (1 - own_side,)
 
@@ -325,14 +320,17 @@
             )
             for line in reversed(range(lines)):
                 up = ghost if line == 0 else here[line - 1]
-                nxt = [
-                    jnp.where(lane == W - 1, nexts[s % 2][side, line, v, after], nexts[s % 2][side, line, v, j])
-                    for v in range(NV)
-                ]
-                prv = [
-                    jnp.where(lane == 0, prevs[s % 2][side, line, v, before], prevs[s % 2][side, line, v, j])
-                    for v in range(NV)
-                ]
+                nxt, prv = [], []
+                for v in range(NV):
+                    if s == 0:
+                        ahead = jnp.where(lane == 0, value(0, side, line, v, after), here[line][v])
+                        behind = jnp.where(lane == W - 1, value(0, side, line, v, before), here[line][v])
+                        nxt.append(pltpu.roll(ahead, W - 1, 1))
+                        prv.append(pltpu.roll(behind, 1, 1))
+                    else:
+                        ahead, behind = nexts[s % 2], prevs[s % 2]
+                        nxt.append(jnp.where(lane == W - 1, ahead[side, line, v, after], ahead[side, line, v, j]))
+                        prv.append(jnp.where(lane == 0, behind[side, line, v, before], behind[side, line, v, j]))
                 timed = split(product[:, line * W : (line + 1) * W])
                 rate = rates(coefs, up, here[line + 1], nxt, prv, timed)
                 for v in range(NV):
@@ -511,7 +509,7 @@
     shares = pl.pallas_call(
         pack_kernel,
         out_shape=f32(NT, NR, W),
-        in_specs=[pl.BlockSpec(memory_space=pltpu.HBM)] * 4,
+        in_specs=[HBM] * 4,
         out_specs=VMEM,
         scratch_shapes=[
             pltpu.VMEM((NV, 256, W), jnp.float32),
@@ -520,7 +518,7 @@
             pltpu.VMEM((NV, W), jnp.float32),
             pltpu.SemaphoreType.DMA((4,)),
         ],
-        compiler_params=params(16),
+        compiler_params=params(60),
         name="pack",
     )(state[0], far_field[0], face_index, face_weight[0])
     lines = lax.all_to_all(shares, "tm", 0, 0, tiled=True).reshape(NT * NR, W)

time: 113 us -> 112 us (level)
  blocking collectives: 57.8 us -> 62.7 us
  Pallas kernels: 16.5 us -> 12.4 us
  local copies, waits for them, and re-layouts: 4.26 us -> 1.93 us
    pallas_call x1, Pallas kernels: 5.96 us -> 0.02 us  [shards(): pl.pallas_call(start_kernel, out_shape=[f32(2, NV, HALF, NT, W), f32(2, 4...]
    all_to_all x1, blocking collectives: 27.8 us -> 32.5 us  [shards(): done = lax.all_to_all(done.reshape(NT, NR, W), 'tm', 0, 0, tiled=True)]
    unnamed x14 -> x6, local copies, waits for them, and re-layouts: 4.26 us -> 1.93 us
    pallas_call x1, Pallas kernels: 0.15 us -> 1.99 us  [shards(): pl.pallas_call(pack_kernel, out_shape=f32(NT, NR, W), in_specs=[HBM] * 4,...]
  transfers between devices with their start and end apart: 6 -> 6, of which waited for: 3 -> 3; matrix products, arithmetic and copies ran while one was open for 0% -> 0% of each run, Pallas kernels for 6% -> 0%
where the time goes in v5:
time: 112 us; the launch traced here: 111 us
  blocking collectives  62.7 us (56%)
  starting transfers between devices  19.4 us (17%)
  waiting for transfers between devices  14.6 us (13%)
  Pallas kernels  12.4 us (11%)
  local copies, waits for them, and re-layouts  1.93 us (2%)
    all_to_all x1, blocking collectives, shards(): done = lax.all_to_all(done.reshape(NT, NR, W), 'tm', 0, 0, tiled=True)  32.5 us
    all_to_all x1, blocking collectives, shards(): lines = lax.all_to_all(shares, 'tm', 0, 0, tiled=True).reshape(NT * NR, W)  30.2 us
    ppermute x1, waiting for transfers between devices, shards(): from_left = lax.ppermute(right, ('tm', 'block'), rights)  9.81 us
    pallas_call x1, Pallas kernels, shards(): pl.pallas_call(main_kernel, out_shape=f32(NT * NR, W), in_specs=[VMEM] *...  8.82 us
    all_to_all x1, starting transfers between devices, shards(): high = lax.all_to_all(zone, 'block', 0, 0, tiled=True)  6.75 us
    ppermute x1, waiting for transfers between devices, shards(): lax.ppermute(ends_down, 'tm', [(i + 1, i) for i in range(PARTS - 1)])  4.69 us
    ppermute x1, starting transfers between devices, shards(): lax.ppermute(left, ('tm', 'block'), [(b, a) for a, b in rights])  4.03 us
    ppermute x1, starting transfers between devices, shards(): from_left = lax.ppermute(right, ('tm', 'block'), rights)  3.56 us
  transfers between devices with their start and end apart: 6, of which 3 were waited for; matrix products, arithmetic and copies ran while one was open for 0% of the time, Pallas kernels for 0%

profile of v5, /device:TPU:1, one launch (start us, length us, event | category | flops | bytes accessed | tf_op | source)
XLA Modules:
  0.0 111.3 jit_solution(9725030274996436468)
XLA Ops:
  0.0 2.0 %pack.1 = f32[16,80,128]{2,1,0:T(8,128)} custom-call(f32[4,256,128]{2,1,0:T(8,128)} %bitcast.12, f32[4,128]{1,0:T(4,128)} %bitcast.13, s32[1,128]{1,0:T(1,128)} %index_in.1, f32[4,128]{1,0:T(4,128)} %bitcast.14), custom_call_target="tpu_custom_call" | custom-call | tf_op jit(solution)/shard_map/pack/pallas_call | solution.py:509
  2.0 30.2 %all_to_all.15 = f32[16,80,128]{2,1,0:T(8,128)S(1)} all-to-all(f32[16,80,128]{2,1,0:T(8,128)} %pack.1), channel_id=1, replica_groups=mesh['tm'=16,'block'=16] {'tm'}, dimensions={0} | all-to-all | bytes 1310720 | tf_op jit(solution)/shard_map/all_to_all | solution.py:524
  32.2 0.2 zone.1
  32.4 0.0 copy-start
  32.4 1.2 %copy-done = f32[16,208,128]{2,1,0:T(8,128)} copy-done((f32[16,208,128]{2,1,0:T(8,128)}, f32[16,208,128]{2,1,0:T(8,128)S(1)}, u32[]{:S(2)}) %copy-start) | copy-done | bytes 1703960
  33.6 6.8 %all-to-all-start.1 = ((f32[16,208,128]{2,1,0:T(8,128)}), f32[16,208,128]{2,1,0:T(8,128)S(1)}, u32[]{:S(2)}, u32[]{:S(2)}) async-start(f32[16,208,128]{2,1,0:T(8,128)} %copy-done), calls=%async_computation.1 | async-start | bytes 3407872 | tf_op jit(solution)/shard_map/all_to_all | solution.py:533
  40.4 2.2 %collective-permute-start = (f32[320,128]{1,0:T(8,128)S(1)}, f32[320,128]{1,0:T(8,128)S(1)}, u32[]{:S(2)}, u32[]{:S(2)}) collective-permute-start(f32[320,128]{1,0:T(8,128)S(1)} %get-tuple-element.16), channel_id=1, source_target_pairs={{0,16},{16,32},{32,48},{48,64},{64,80},{80,96},{96,112},{112,128},... | collective-permute-start | bytes 491528 | tf_op jit(solution)/shard_map/ppermute | solution.py:534
  42.6 2.1 %collective-permute-start.1 = (f32[320,128]{1,0:T(8,128)S(1)}, f32[320,128]{1,0:T(8,128)S(1)}, u32[]{:S(2)}, u32[]{:S(2)}) collective-permute-start(f32[320,128]{1,0:T(8,128)S(1)} %get-tuple-element.17), channel_id=1, source_target_pairs={{16,0},{32,16},{48,32},{64,48},{80,64},{96,80},{112,96},{128,112},... | collective-permute-start | bytes 491528 | tf_op jit(solution)/shard_map/ppermute | solution.py:535
  44.7 0.1 collective-permute-done.below
  44.9 4.7 %collective-permute-done.1.above = f32[320,128]{1,0:T(8,128)S(1)} collective-permute-done((f32[320,128]{1,0:T(8,128)S(1)}, f32[320,128]{1,0:T(8,128)S(1)}, u32[]{:S(2)}, u32[]{:S(2)}) %collective-permute-start.1) | collective-permute-done | bytes 163872 | tf_op jit(solution)/shard_map/ppermute | solution.py:535
  49.6 0.5 edges.1
  50.1 3.6 %collective-permute-start.2 = (f32[128,128]{1,0:T(8,128)S(1)}, f32[128,128]{1,0:T(8,128)S(1)}, u32[]{:S(2)}, u32[]{:S(2)}) collective-permute-start(f32[128,128]{1,0:T(8,128)S(1)} %get-tuple-element.18), channel_id=1, source_target_pairs={{0,1},{1,2},{2,3},{3,4},{4,5},{5,6},{6,7},{7,0},{8,9},{9,10},{10,1... | collective-permute-start | bytes 196616 | tf_op jit(solution)/shard_map/ppermute | solution.py:547
  53.7 4.0 %collective-permute-start.3 = (f32[128,128]{1,0:T(8,128)S(1)}, f32[128,128]{1,0:T(8,128)S(1)}, u32[]{:S(2)}, u32[]{:S(2)}) collective-permute-start(f32[128,128]{1,0:T(8,128)S(1)} %get-tuple-element.19), channel_id=1, source_target_pairs={{1,0},{2,1},{3,2},{4,3},{5,4},{6,5},{7,6},{0,7},{9,8},{10,9},{11,1... | collective-permute-start | bytes 196616 | tf_op jit(solution)/shard_map/ppermute | solution.py:548
  57.7 9.8 %collective-permute-done.2.from_left = f32[128,128]{1,0:T(8,128)S(1)} collective-permute-done((f32[128,128]{1,0:T(8,128)S(1)}, f32[128,128]{1,0:T(8,128)S(1)}, u32[]{:S(2)}, u32[]{:S(2)}) %collective-permute-start.2) | collective-permute-done | bytes 65568 | tf_op jit(solution)/shard_map/ppermute | solution.py:547
  67.5 0.0 collective-permute-done.3.from_right
  67.5 0.0 all-to-all-done.1.high
  67.5 0.8 collective-permute-start.4
  68.3 0.0 copy-start.1
  68.3 0.0 copy-start.2
  68.3 0.0 collective-permute-done.4.low
  68.3 0.6 copy-done.1
  69.0 0.1 copy-done.2
  69.1 8.8 %main.1 = f32[1280,128]{1,0:T(8,128)S(1)} custom-call(f32[16,208,128]{2,1,0:T(8,128)S(1)} %collective-permute-done.4.low, f32[16,208,128]{2,1,0:T(8,128)S(1)} %all-to-all-done.1.high, f32[2,4,8,16,128]{4,3,2,1,0:T(8,128)S(1)} %get-tuple-element.21.given_ghosts, f32[2,4,128,128]{3,2,1,0:T(8,128)S(1)} %get-tuple-element.22.ordered, f32[1280,128]{1,0:T(8,128)S(1)} %bitcast.9, ...), custom_call_target="tpu_custom_call" | custom-call | flops 8000000000 | bytes 67108864 | tf_op jit(solution)/shard_map/main/pallas_call | solution.py:563
  77.9 32.5 %all_to_all.16.shares = f32[16,80,128]{2,1,0:T(8,128)S(1)} all-to-all(f32[16,80,128]{2,1,0:T(8,128)S(1)} %bitcast.11), channel_id=1, replica_groups=mesh['tm'=16,'block'=16] {'tm'}, dimensions={0} | all-to-all | bytes 1310720 | tf_op jit(solution)/shard_map/all_to_all | solution.py:576
  110.4 0.8 unpack.1
  (1 shorter events, 0.0 us)
Async XLA Ops:
  32.4 1.2 %copy-start = (f32[16,208,128]{2,1,0:T(8,128)}, f32[16,208,128]{2,1,0:T(8,128)S(1)}, u32[]{:S(2)}) copy-start(f32[16,208,128]{2,1,0:T(8,128)S(1)} %get-tuple-element.15) | copy-start | bytes 5111812
  33.6 33.9 %all-to-all-start.1 = ((f32[16,208,128]{2,1,0:T(8,128)}), f32[16,208,128]{2,1,0:T(8,128)S(1)}, u32[]{:S(2)}, u32[]{:S(2)}) async-start(f32[16,208,128]{2,1,0:T(8,128)} %copy-done), calls=%async_computation.1 | async-start | bytes 3407872 | tf_op jit(solution)/shard_map/all_to_all | solution.py:533
  40.4 4.5 %collective-permute-start = (f32[320,128]{1,0:T(8,128)S(1)}, f32[320,128]{1,0:T(8,128)S(1)}, u32[]{:S(2)}, u32[]{:S(2)}) collective-permute-start(f32[320,128]{1,0:T(8,128)S(1)} %get-tuple-element.16), channel_id=1, source_target_pairs={{0,16},{16,32},{32,48},{48,64},{64,80},{80,96},{96,112},{112,128},... | collective-permute-start | bytes 491528 | tf_op jit(solution)/shard_map/ppermute | solution.py:534
  42.6 6.9 %collective-permute-start.1 = (f32[320,128]{1,0:T(8,128)S(1)}, f32[320,128]{1,0:T(8,128)S(1)}, u32[]{:S(2)}, u32[]{:S(2)}) collective-permute-start(f32[320,128]{1,0:T(8,128)S(1)} %get-tuple-element.17), channel_id=1, source_target_pairs={{16,0},{32,16},{48,32},{64,48},{80,64},{96,80},{112,96},{128,112},... | collective-permute-start | bytes 491528 | tf_op jit(solution)/shard_map/ppermute | solution.py:535
  50.1 17.4 %collective-permute-start.2 = (f32[128,128]{1,0:T(8,128)S(1)}, f32[128,128]{1,0:T(8,128)S(1)}, u32[]{:S(2)}, u32[]{:S(2)}) collective-permute-start(f32[128,128]{1,0:T(8,128)S(1)} %get-tuple-element.18), channel_id=1, source_target_pairs={{0,1},{1,2},{2,3},{3,4},{4,5},{5,6},{6,7},{7,0},{8,9},{9,10},{10,1... | collective-permute-start | bytes 196616 | tf_op jit(solution)/shard_map/ppermute | solution.py:547
  53.7 13.9 %collective-permute-start.3 = (f32[128,128]{1,0:T(8,128)S(1)}, f32[128,128]{1,0:T(8,128)S(1)}, u32[]{:S(2)}, u32[]{:S(2)}) collective-permute-start(f32[128,128]{1,0:T(8,128)S(1)} %get-tuple-element.19), channel_id=1, source_target_pairs={{1,0},{2,1},{3,2},{4,3},{5,4},{6,5},{7,6},{0,7},{9,8},{10,9},{11,1... | collective-permute-start | bytes 196616 | tf_op jit(solution)/shard_map/ppermute | solution.py:548
  67.5 0.8 collective-permute-start.4
  68.3 0.7 copy-start.1
  68.3 0.8 copy-start.2

commit v6 on v5

--- a/solution.py
+++ b/solution.py
@@ -28,7 +28,7 @@
 EDGE_PACKS = 8
 FIRST_HALF = tuple(range(4, 17))
 SECOND_HALF = (20, 21, 22, 23, 24, 0, 1, 2, 3, 17, 18, 19)
-SU = (1, 2, 2, 4)
+SU = (2, 4, 4, 8)
 VMEM = pl.BlockSpec(memory_space=pltpu.VMEM)
 HBM = pl.BlockSpec(memory_space=pltpu.HBM)
 SMEM = pl.BlockSpec(memory_space=pltpu.SMEM)
@@ -41,10 +41,11 @@
     cot = np.cos(safe) / np.sin(safe)
     matrix = np.where(offsets == 0, 0.0, 0.5 * (1.0 - 2.0 * (offsets % 2)) * cot)
     matrix = OMEGA * matrix + 4.0 * DISSIPATION * np.eye(NT)
-    matrix = np.kron(np.eye(NV), matrix).astype(np.float32)
+    matrix = np.asarray(SECTION_FACTORS)[:, None, None] * np.kron(np.eye(NV), matrix)
+    matrix = matrix.astype(np.float32)
     lead = matrix.astype(ml_dtypes.bfloat16)
     rest = (matrix - lead.astype(np.float32)).astype(ml_dtypes.bfloat16)
-    return np.concatenate([lead, rest, lead], axis=1)
+    return np.concatenate([lead, rest, lead], axis=2)
 
 
 def params(mib):
@@ -146,19 +147,26 @@
         right[p * NT : (p + 1) * NT] = right_pack
 
 
-def coefficients(flow, side):
+def coefficients(flow, side, factor):
     sign = (0.5, -0.5)[side] if isinstance(side, int) else jnp.where(side == 0, 0.5, -0.5)
     along = sign * flow[side, 0]
     across = 0.5 * flow[side, 1]
-    return sign, along - DISSIPATION, -along - DISSIPATION, across - DISSIPATION, -across - DISSIPATION
+    return (
+        factor * sign,
+        0.5 * factor,
+        factor * (along - DISSIPATION),
+        factor * (-along - DISSIPATION),
+        factor * (across - DISSIPATION),
+        factor * (-across - DISSIPATION),
+    )
 
 
 def rates(coefs, up, down, nxt, prv, timed):
-    sign, cu, cd, cn, cp = coefs
+    ci, cj, cu, cd, cn, cp = coefs
     plain = [timed[v] + (cu * up[v] + cd * down[v]) + (cn * nxt[v] + cp * prv[v]) for v in range(NV)]
-    mixed = sign * (up[1] - down[1]) + 0.5 * (nxt[2] - prv[2])
-    pressure_up = sign * (up[3] - down[3])
-    pressure_next = 0.5 * (nxt[3] - prv[3])
+    mixed = ci * (up[1] - down[1]) + cj * (nxt[2] - prv[2])
+    pressure_up = ci * (up[3] - down[3])
+    pressure_next = cj * (nxt[3] - prv[3])
     return [plain[0] + mixed, plain[1] + pressure_up, plain[2] + pressure_next, plain[3] + mixed]
 
 
@@ -246,12 +254,12 @@
 
 def chain(
     low, high, given_ghosts, ordered, matrix, flow, out,
-    cur0, cur1, nexts0, nexts1, prevs0, prevs1, shifted, weighed, ghosts, applied,
+    cur0, cur1, weighed, ghosts, applied,
 ):
     _, block = place()
     own_side, own = block // HALF, block % HALF
     lane = lax.broadcasted_iota(jnp.int32, (NT, W), 1)
-    cur, nexts, prevs = (cur0, cur1), (nexts0, nexts1), (prevs0, prevs1)
+    cur = (cur0, cur1)
 
     def tile(side, j, k):
         return zone_tile(low, high, side, j, k)
@@ -260,13 +268,6 @@
         if section == 0:
             return tile(side, j, line * NV + v)
         return cur[section % 2][side, line, v, j]
-
-    def keep_rolled(section, side, line, v, j, values, shift=False):
-        nexts[section % 2][side, line, v, j] = pltpu.roll(values, W - 1, 1)
-        prevs[section % 2][side, line, v, j] = pltpu.roll(values, 1, 1)
-        if shift:
-            shifted[0, side, v, j] = pltpu.roll(values, W - 2, 1)
-            shifted[1, side, v, j] = pltpu.roll(values, W - 3, 1)
 
     def weigh(section, side, m):
         other, after = 1 - side, (m + 1) % HALF
@@ -274,11 +275,8 @@
         for v in range(NV):
             total = weight[0] * value(section, other, 0, v, m)
             for k in range(1, 4):
-                if k == 1:
-                    here, there = nexts[section % 2][other, 0, v, m], nexts[section % 2][other, 0, v, after]
-                else:
-                    here, there = shifted[k - 2, other, v, m], shifted[k - 2, other, v, after]
-                total = total + weight[k] * jnp.where(lane >= W - k, there, here)
+                ahead = jnp.where(lane < k, value(section, other, 0, v, after), value(section, other, 0, v, m))
+                total = total + weight[k] * pltpu.roll(ahead, W - k, 1)
             weighed[side, v, m] = total
 
     def interpolate(side, j):
@@ -306,7 +304,7 @@
 
         def advance(side, j, s=s):
             after, before = (j + 1) % HALF, (j + HALF - 1) % HALF
-            coefs = coefficients(flow, side)
+            coefs = coefficients(flow, side, SECTION_FACTORS[s])
             if s == 0:
                 ghost = [given_ghosts[side, v, j] for v in range(NV)]
             else:
@@ -316,35 +314,28 @@
             lines = 4 - s
             here = [[value(s, side, line, v, j) for v in range(NV)] for line in range(lines + 1)]
             product = level_product(
-                matrix[...], jnp.concatenate([jnp.concatenate(here[line], axis=0) for line in range(lines)], axis=1)
+                matrix[s], jnp.concatenate([jnp.concatenate(here[line], axis=0) for line in range(lines)], axis=1)
             )
             for line in reversed(range(lines)):
                 up = ghost if line == 0 else here[line - 1]
                 nxt, prv = [], []
                 for v in range(NV):
-                    if s == 0:
-                        ahead = jnp.where(lane == 0, value(0, side, line, v, after), here[line][v])
-                        behind = jnp.where(lane == W - 1, value(0, side, line, v, before), here[line][v])
-                        nxt.append(pltpu.roll(ahead, W - 1, 1))
-                        prv.append(pltpu.roll(behind, 1, 1))
-                    else:
-                        ahead, behind = nexts[s % 2], prevs[s % 2]
-                        nxt.append(jnp.where(lane == W - 1, ahead[side, line, v, after], ahead[side, line, v, j]))
-                        prv.append(jnp.where(lane == 0, behind[side, line, v, before], behind[side, line, v, j]))
+                    ahead = jnp.where(lane == 0, value(s, side, line, v, after), here[line][v])
+                    behind = jnp.where(lane == W - 1, value(s, side, line, v, before), here[line][v])
+                    nxt.append(pltpu.roll(ahead, W - 1, 1))
+                    prv.append(pltpu.roll(behind, 1, 1))
                 timed = split(product[:, line * W : (line + 1) * W])
                 rate = rates(coefs, up, here[line + 1], nxt, prv, timed)
                 for v in range(NV):
-                    result = value(0, side, line, v, j) - SECTION_FACTORS[s] * rate[v]
+                    result = value(0, side, line, v, j) - rate[v]
                     cur[(s + 1) % 2][side, line, v, j] = result
-                    if line < max(lines - 1, 1):
-                        keep_rolled(s + 1, side, line, v, j, result, line == 0)
         def section_step(j, _, advance=advance, sides=sides):
             for side in sides:
                 advance(side, j)
             return 0
 
         if s > 0:
-            lax.fori_loop(0, HALF, weigh_step, 0, unroll=2)
+            lax.fori_loop(0, HALF, weigh_step, 0, unroll=8)
         lax.fori_loop(0, HALF, section_step, 0, unroll=SU[s])
         if s == 3:
 
@@ -355,7 +346,7 @@
                     ghosts[1, own_side, v, j] = ghost[v]
                 return 0
 
-            lax.fori_loop(0, 3, own_step, 0)
+            lax.fori_loop(0, 3, own_step, 0, unroll=3)
         kept = given_ghosts if s == 0 else ghosts.at[s % 2]
         for v in range(NV):
             at = slice(v * NT, (v + 1) * NT)
@@ -368,20 +359,20 @@
         weigh(4, own_side, m)
         return 0
 
-    lax.fori_loop(0, HALF, last_weigh, 0, unroll=4)
+    lax.fori_loop(0, HALF, last_weigh, 0, unroll=8)
     got = interpolate(own_side, own)
     for v in range(NV):
         at = slice(v * NT, (v + 1) * NT)
         applied[4, at, :W] = got[v]
         applied[4, at, W:] = got[v]
 
-    coefs = coefficients(flow, own_side)
     zero = jnp.zeros((NV * NT, 2 * W), jnp.float32)
     response = []
     for s in range(5):
+        coefs = coefficients(flow, own_side, SECTION_FACTORS[s])
         product = None
         if s:
-            product = level_product(matrix[...], jnp.concatenate(response, axis=1))
+            product = level_product(matrix[s], jnp.concatenate(response, axis=1))
         padded = [applied[s]] + response + [zero, zero]
         new = []
         for line in range(s + 1):
@@ -392,7 +383,7 @@
             else:
                 nxt = prv = timed = zero
             rate = rates(coefs, split(padded[line]), split(padded[line + 2]), split(nxt), split(prv), split(timed))
-            new.append(-SECTION_FACTORS[s] * jnp.concatenate(rate, axis=0))
+            new.append(-jnp.concatenate(rate, axis=0))
         response = new
 
     for line in range(HALO):
@@ -415,9 +406,9 @@
         before = from_left[p * NT : (p + 1) * NT]
         before = before if k == 15 else pltpu.roll(before, 120 - 8 * k, 1)
         start[m // NV, at, W:] = jnp.where(lane < W // 2, after, before)
-    coefs = coefficients(flow, side)
     group = 4
     for s in range(5):
+        coefs = coefficients(flow, side, SECTION_FACTORS[s])
         now = start if s == 0 else (even if s % 2 == 0 else odd)
         new = odd if s % 2 == 0 else even
 
@@ -433,10 +424,10 @@
 
         first = (1, 1, 3, 3, 5)[s]
 
-        def line_step(step, _, now=now, new=new, s=s, first=first):
+        def line_step(step, _, now=now, new=new, s=s, first=first, coefs=coefs):
             i = first + group * step
             here = [now[i - 1 + g] for g in range(group + 2)]
-            product = level_product(matrix[...], jnp.concatenate(here[1:-1], axis=1))
+            product = level_product(matrix[s], jnp.concatenate(here[1:-1], axis=1))
             for g in range(group):
                 line = here[g + 1]
                 nxt = pltpu.roll(line, 2 * W - 1, 1)
@@ -445,7 +436,7 @@
                 rate = rates(coefs, split(here[g + 2]), split(here[g]), split(nxt), split(prv), timed)
                 base = split(start[i + g])
                 for v in range(NV):
-                    result = base[v] - SECTION_FACTORS[s] * rate[v]
+                    result = base[v] - rate[v]
                     if s < 4:
                         new[i + g, v * NT : (v + 1) * NT] = result
                     else:
@@ -566,8 +557,8 @@
         in_specs=[VMEM] * 10 + [SMEM],
         out_specs=VMEM,
         scratch_shapes=[grid] * 3
-        + [lines_of] * 6
-        + [faces_of, pltpu.VMEM((2, NV, HALF, NT, W), jnp.float32)]
+        + [lines_of] * 2
+        + [pltpu.VMEM((2, NV, HALF, NT, W), jnp.float32)]
         + [faces_of, pltpu.VMEM((5, NV * NT, 2 * W), jnp.float32)],
         compiler_params=params(32),
         cost_estimate=cost(8 * 10**9, 64 << 20),

time: 112 us -> 107 us (0.955)
  blocking collectives: 62.7 us -> 57.9 us
    all_to_all x1, blocking collectives: 32.5 us -> 27.6 us  [shards(): done = lax.all_to_all(done.reshape(NT, NR, W), 'tm', 0, 0, tiled=True)]
  transfers between devices with their start and end apart: 6 -> 6, of which waited for: 3 -> 3; matrix products, arithmetic and copies ran while one was open for 0% -> 0% of each run, Pallas kernels for 0% -> 1%
where the time goes in v6:
time: 107 us; the launch traced here: 106 us
  blocking collectives  57.9 us (54%)
  starting transfers between devices  19.4 us (18%)
  waiting for transfers between devices  14.6 us (14%)
  Pallas kernels  12.3 us (11%)
  local copies, waits for them, and re-layouts  2.09 us (2%)
    all_to_all x1, blocking collectives, shards(): lines = lax.all_to_all(shares, 'tm', 0, 0, tiled=True).reshape(NT * NR, W)  30.2 us
    all_to_all x1, blocking collectives, shards(): done = lax.all_to_all(done.reshape(NT, NR, W), 'tm', 0, 0, tiled=True)  27.6 us
    ppermute x1, waiting for transfers between devices, shards(): from_left = lax.ppermute(right, ('tm', 'block'), rights)  9.81 us
    pallas_call x1, Pallas kernels, shards(): pl.pallas_call(main_kernel, out_shape=f32(NT * NR, W), in_specs=[VMEM] *...  8.72 us
    all_to_all x1, starting transfers between devices, shards(): high = lax.all_to_all(zone, 'block', 0, 0, tiled=True)  6.75 us
    ppermute x1, waiting for transfers between devices, shards(): lax.ppermute(ends_down, 'tm', [(i + 1, i) for i in range(PARTS - 1)])  4.69 us
    ppermute x1, starting transfers between devices, shards(): lax.ppermute(left, ('tm', 'block'), [(b, a) for a, b in rights])  4.03 us
    ppermute x1, starting transfers between devices, shards(): from_left = lax.ppermute(right, ('tm', 'block'), rights)  3.56 us
  transfers between devices with their start and end apart: 6, of which 3 were waited for; matrix products, arithmetic and copies ran while one was open for 0% of the time, Pallas kernels for 1%

profile of v6, /device:TPU:1, one launch (start us, length us, event | category | flops | bytes accessed | tf_op | source)
XLA Modules:
  0.0 106.4 jit_solution(11123385270796772025)
XLA Ops:
  0.0 2.0 %pack.1 = f32[16,80,128]{2,1,0:T(8,128)} custom-call(f32[4,256,128]{2,1,0:T(8,128)} %bitcast.12, f32[4,128]{1,0:T(4,128)} %bitcast.13, s32[1,128]{1,0:T(1,128)} %index_in.1, f32[4,128]{1,0:T(4,128)} %bitcast.14), custom_call_target="tpu_custom_call" | custom-call | tf_op jit(solution)/shard_map/pack/pallas_call | solution.py:500
  2.0 30.2 %all_to_all.15 = f32[16,80,128]{2,1,0:T(8,128)S(1)} all-to-all(f32[16,80,128]{2,1,0:T(8,128)} %pack.1), channel_id=1, replica_groups=mesh['tm'=16,'block'=16] {'tm'}, dimensions={0} | all-to-all | bytes 1310720 | tf_op jit(solution)/shard_map/all_to_all | solution.py:515
  32.2 0.2 zone.1
  32.4 0.0 copy-start
  32.4 1.2 %copy-done = f32[16,208,128]{2,1,0:T(8,128)} copy-done((f32[16,208,128]{2,1,0:T(8,128)}, f32[16,208,128]{2,1,0:T(8,128)S(1)}, u32[]{:S(2)}) %copy-start) | copy-done | bytes 1703960
  33.6 6.8 %all-to-all-start.1 = ((f32[16,208,128]{2,1,0:T(8,128)}), f32[16,208,128]{2,1,0:T(8,128)S(1)}, u32[]{:S(2)}, u32[]{:S(2)}) async-start(f32[16,208,128]{2,1,0:T(8,128)} %copy-done), calls=%async_computation.1 | async-start | bytes 3407872 | tf_op jit(solution)/shard_map/all_to_all | solution.py:524
  40.4 2.2 %collective-permute-start = (f32[320,128]{1,0:T(8,128)S(1)}, f32[320,128]{1,0:T(8,128)S(1)}, u32[]{:S(2)}, u32[]{:S(2)}) collective-permute-start(f32[320,128]{1,0:T(8,128)S(1)} %get-tuple-element.16), channel_id=1, source_target_pairs={{0,16},{16,32},{32,48},{48,64},{64,80},{80,96},{96,112},{112,128},... | collective-permute-start | bytes 491528 | tf_op jit(solution)/shard_map/ppermute | solution.py:525
  42.6 2.1 %collective-permute-start.1 = (f32[320,128]{1,0:T(8,128)S(1)}, f32[320,128]{1,0:T(8,128)S(1)}, u32[]{:S(2)}, u32[]{:S(2)}) collective-permute-start(f32[320,128]{1,0:T(8,128)S(1)} %get-tuple-element.17), channel_id=1, source_target_pairs={{16,0},{32,16},{48,32},{64,48},{80,64},{96,80},{112,96},{128,112},... | collective-permute-start | bytes 491528 | tf_op jit(solution)/shard_map/ppermute | solution.py:526
  44.7 0.1 collective-permute-done.below
  44.9 4.7 %collective-permute-done.1.above = f32[320,128]{1,0:T(8,128)S(1)} collective-permute-done((f32[320,128]{1,0:T(8,128)S(1)}, f32[320,128]{1,0:T(8,128)S(1)}, u32[]{:S(2)}, u32[]{:S(2)}) %collective-permute-start.1) | collective-permute-done | bytes 163872 | tf_op jit(solution)/shard_map/ppermute | solution.py:526
  49.6 0.5 edges.1
  50.1 3.6 %collective-permute-start.2 = (f32[128,128]{1,0:T(8,128)S(1)}, f32[128,128]{1,0:T(8,128)S(1)}, u32[]{:S(2)}, u32[]{:S(2)}) collective-permute-start(f32[128,128]{1,0:T(8,128)S(1)} %get-tuple-element.18), channel_id=1, source_target_pairs={{0,1},{1,2},{2,3},{3,4},{4,5},{5,6},{6,7},{7,0},{8,9},{9,10},{10,1... | collective-permute-start | bytes 196616 | tf_op jit(solution)/shard_map/ppermute | solution.py:538
  53.7 4.0 %collective-permute-start.3 = (f32[128,128]{1,0:T(8,128)S(1)}, f32[128,128]{1,0:T(8,128)S(1)}, u32[]{:S(2)}, u32[]{:S(2)}) collective-permute-start(f32[128,128]{1,0:T(8,128)S(1)} %get-tuple-element.19), channel_id=1, source_target_pairs={{1,0},{2,1},{3,2},{4,3},{5,4},{6,5},{7,6},{0,7},{9,8},{10,9},{11,1... | collective-permute-start | bytes 196616 | tf_op jit(solution)/shard_map/ppermute | solution.py:539
  57.7 9.8 %collective-permute-done.2.from_left = f32[128,128]{1,0:T(8,128)S(1)} collective-permute-done((f32[128,128]{1,0:T(8,128)S(1)}, f32[128,128]{1,0:T(8,128)S(1)}, u32[]{:S(2)}, u32[]{:S(2)}) %collective-permute-start.2) | collective-permute-done | bytes 65568 | tf_op jit(solution)/shard_map/ppermute | solution.py:538
  67.5 0.0 collective-permute-done.3.from_right
  67.5 0.0 all-to-all-done.1.high
  67.5 0.8 collective-permute-start.4
  68.3 0.0 copy-start.1
  68.3 0.0 copy-start.2
  68.3 0.0 collective-permute-done.4.low
  68.3 0.6 copy-done.1
  69.0 0.3 copy-done.2
  69.2 8.7 %main.1 = f32[1280,128]{1,0:T(8,128)S(1)} custom-call(f32[16,208,128]{2,1,0:T(8,128)S(1)} %collective-permute-done.4.low, f32[16,208,128]{2,1,0:T(8,128)S(1)} %all-to-all-done.1.high, f32[2,4,8,16,128]{4,3,2,1,0:T(8,128)S(1)} %get-tuple-element.21.given_ghosts, f32[2,4,128,128]{3,2,1,0:T(8,128)S(1)} %get-tuple-element.22.ordered, f32[1280,128]{1,0:T(8,128)S(1)} %bitcast.9, ...), custom_call_target="tpu_custom_call" | custom-call | flops 8000000000 | bytes 67108864 | tf_op jit(solution)/shard_map/main/pallas_call | solution.py:554
  78.0 27.6 %all_to_all.16.shares = f32[16,80,128]{2,1,0:T(8,128)S(1)} all-to-all(f32[16,80,128]{2,1,0:T(8,128)S(1)} %bitcast.11), channel_id=1, replica_groups=mesh['tm'=16,'block'=16] {'tm'}, dimensions={0} | all-to-all | bytes 1310720 | tf_op jit(solution)/shard_map/all_to_all | solution.py:567
  105.6 0.8 unpack.1
  (1 shorter events, 0.0 us)
Async XLA Ops:
  32.4 1.2 %copy-start = (f32[16,208,128]{2,1,0:T(8,128)}, f32[16,208,128]{2,1,0:T(8,128)S(1)}, u32[]{:S(2)}) copy-start(f32[16,208,128]{2,1,0:T(8,128)S(1)} %get-tuple-element.15) | copy-start | bytes 5111812
  33.6 33.9 %all-to-all-start.1 = ((f32[16,208,128]{2,1,0:T(8,128)}), f32[16,208,128]{2,1,0:T(8,128)S(1)}, u32[]{:S(2)}, u32[]{:S(2)}) async-start(f32[16,208,128]{2,1,0:T(8,128)} %copy-done), calls=%async_computation.1 | async-start | bytes 3407872 | tf_op jit(solution)/shard_map/all_to_all | solution.py:524
  40.4 4.5 %collective-permute-start = (f32[320,128]{1,0:T(8,128)S(1)}, f32[320,128]{1,0:T(8,128)S(1)}, u32[]{:S(2)}, u32[]{:S(2)}) collective-permute-start(f32[320,128]{1,0:T(8,128)S(1)} %get-tuple-element.16), channel_id=1, source_target_pairs={{0,16},{16,32},{32,48},{48,64},{64,80},{80,96},{96,112},{112,128},... | collective-permute-start | bytes 491528 | tf_op jit(solution)/shard_map/ppermute | solution.py:525
  42.6 6.9 %collective-permute-start.1 = (f32[320,128]{1,0:T(8,128)S(1)}, f32[320,128]{1,0:T(8,128)S(1)}, u32[]{:S(2)}, u32[]{:S(2)}) collective-permute-start(f32[320,128]{1,0:T(8,128)S(1)} %get-tuple-element.17), channel_id=1, source_target_pairs={{16,0},{32,16},{48,32},{64,48},{80,64},{96,80},{112,96},{128,112},... | collective-permute-start | bytes 491528 | tf_op jit(solution)/shard_map/ppermute | solution.py:526
  50.1 17.4 %collective-permute-start.2 = (f32[128,128]{1,0:T(8,128)S(1)}, f32[128,128]{1,0:T(8,128)S(1)}, u32[]{:S(2)}, u32[]{:S(2)}) collective-permute-start(f32[128,128]{1,0:T(8,128)S(1)} %get-tuple-element.18), channel_id=1, source_target_pairs={{0,1},{1,2},{2,3},{3,4},{4,5},{5,6},{6,7},{7,0},{8,9},{9,10},{10,1... | collective-permute-start | bytes 196616 | tf_op jit(solution)/shard_map/ppermute | solution.py:538
  53.7 13.9 %collective-permute-start.3 = (f32[128,128]{1,0:T(8,128)S(1)}, f32[128,128]{1,0:T(8,128)S(1)}, u32[]{:S(2)}, u32[]{:S(2)}) collective-permute-start(f32[128,128]{1,0:T(8,128)S(1)} %get-tuple-element.19), channel_id=1, source_target_pairs={{1,0},{2,1},{3,2},{4,3},{5,4},{6,5},{7,6},{0,7},{9,8},{10,9},{11,1... | collective-permute-start | bytes 196616 | tf_op jit(solution)/shard_map/ppermute | solution.py:539
  67.5 0.8 collective-permute-start.4
  68.3 0.7 copy-start.1
  68.3 0.9 copy-start.2

commit v7 on v6

--- a/solution.py
+++ b/solution.py
@@ -100,51 +100,67 @@
     return v * ROW + jnp.where(side == 0, r, CHUNK - 1 - r)
 
 
-def zone_kernel(lines, zone, ends_up, ends_down):
-    _, block = place()
+def ends_kernel(lines, to_partner, to_chip):
+    t, block = place()
     side = block // HALF
-    for i in range(HALF_ZONE):
-        tile = lines[pl.ds(i, NT, stride=NR), :]
-        for b in range(BLOCKS):
-            zone[b, i * NT : (i + 1) * NT] = tile
+    even = t % 2 == 0
     for i in range(ENDS):
         r, v = i // NV, i % NV
         at = slice(i * NT, (i + 1) * NT)
-        ends_up[at] = lines[pl.ds(line_address(side, CHUNK - HALO + r, v), NT, stride=NR), :]
-        ends_down[at] = lines[pl.ds(line_address(side, r, v), NT, stride=NR), :]
-
-
-def line_tile(lines, below, above, t, side, r, v):
-    if r < 0:
-        at = (r + HALO) * NV + v
-        tile = below[at * NT : (at + 1) * NT]
-        if r == -1:
-            tile = jnp.where(t == 0, lines[pl.ds(v * ROW + CHUNK, NT, stride=NR), :], tile)
-        return tile
-    if r < CHUNK:
+        up = lines[pl.ds(line_address(side, CHUNK - HALO + r, v), NT, stride=NR), :]
+        down = lines[pl.ds(line_address(side, r, v), NT, stride=NR), :]
+        to_partner[at] = jnp.where(even, up, down)
+        to_chip[at] = jnp.where(even, down, up)
+
+
+def neighbours(block):
+    row = block // HALF * HALF
+    return row + (block + HALF - 1) % HALF, row + (block + 1) % HALF
+
+
+def line_tile(lines, partner, chip, t, side, r, v):
+    even = t % 2 == 0
+    if 0 <= r < CHUNK:
         return lines[pl.ds(line_address(side, r, v), NT, stride=NR), :]
-    at = (r - CHUNK) * NV + v
-    return above[at * NT : (at + 1) * NT]
-
-
-def edge_kernel(lines, below, above, left, right):
+    at = (r + HALO if r < 0 else r - CHUNK) * NV + v
+    at = slice(at * NT, (at + 1) * NT)
+    if r >= CHUNK:
+        return jnp.where(even, partner[at], chip[at])
+    tile = jnp.where(even, chip[at], partner[at])
+    if r == -1:
+        tile = jnp.where(t == 0, lines[pl.ds(v * ROW + CHUNK, NT, stride=NR), :], tile)
+    return tile
+
+
+def zone_kernel(lines, from_partner, from_chip, zone):
     t, block = place()
     side = block // HALF
+    before, after = neighbours(block)
     part = lax.broadcasted_iota(jnp.int32, (NT, W), 1) // 8
-    for p in range(EDGE_PACKS):
-        left_pack = jnp.zeros((NT, W), jnp.float32)
-        right_pack = jnp.zeros((NT, W), jnp.float32)
-        for k in range(16):
-            m = p * 16 + k
-            if m >= LINES * NV:
-                break
-            tile = line_tile(lines, below, above, t, side, m // NV - HALO, m % NV)
-            moved = tile if k == 0 else pltpu.roll(tile, 8 * k, 1)
-            left_pack = jnp.where(part == k, moved, left_pack)
-            moved = tile if k == 15 else pltpu.roll(tile, 8 * k + 8, 1)
-            right_pack = jnp.where(part == k, moved, right_pack)
-        left[p * NT : (p + 1) * NT] = left_pack
-        right[p * NT : (p + 1) * NT] = right_pack
+
+    @pl.when(t >= PARTS)
+    def _():
+        for i in range(HALF_ZONE):
+            tile = lines[pl.ds(i, NT, stride=NR), :]
+            for b in range(BLOCKS):
+                zone[b, i * NT : (i + 1) * NT] = tile
+
+    @pl.when(t < PARTS)
+    def _():
+        for p in range(EDGE_PACKS):
+            left_pack = jnp.zeros((NT, W), jnp.float32)
+            right_pack = jnp.zeros((NT, W), jnp.float32)
+            for k in range(16):
+                m = p * 16 + k
+                if m >= LINES * NV:
+                    break
+                tile = line_tile(lines, from_partner, from_chip, t, side, m // NV - HALO, m % NV)
+                moved = tile if k == 0 else pltpu.roll(tile, 8 * k, 1)
+                left_pack = jnp.where(part == k, moved, left_pack)
+                moved = tile if k == 15 else pltpu.roll(tile, 8 * k + 8, 1)
+                right_pack = jnp.where(part == k, moved, right_pack)
+            zone[before, p * NT : (p + 1) * NT] = left_pack
+            zone[after, p * NT : (p + 1) * NT] = right_pack
 
 
 def coefficients(flow, side, factor):
@@ -392,18 +408,19 @@
             out[pl.ds(v * ROW + cell, NT, stride=NR), :] = response[line][v * NT : (v + 1) * NT, :W]
 
 
-def bulk(lines, below, above, from_left, from_right, matrix, flow, out, start, even, odd):
+def bulk(lines, from_partner, from_chip, edges, matrix, flow, out, start, even, odd):
     t, block = place()
     side = block // HALF
+    left, right = neighbours(block)
     lane = lax.broadcasted_iota(jnp.int32, (NT, W), 1)
     for m in range(LINES * NV):
         r, v = m // NV - HALO, m % NV
         at = slice(v * NT, (v + 1) * NT)
-        start[m // NV, at, :W] = line_tile(lines, below, above, t, side, r, v)
+        start[m // NV, at, :W] = line_tile(lines, from_partner, from_chip, t, side, r, v)
         p, k = m // 16, m % 16
-        after = from_right[p * NT : (p + 1) * NT]
+        after = edges[right, p * NT : (p + 1) * NT]
         after = after if k == 0 else pltpu.roll(after, W - 8 * k, 1)
-        before = from_left[p * NT : (p + 1) * NT]
+        before = edges[left, p * NT : (p + 1) * NT]
         before = before if k == 15 else pltpu.roll(before, 120 - 8 * k, 1)
         start[m // NV, at, W:] = jnp.where(lane < W // 2, after, before)
     group = 4
@@ -444,17 +461,15 @@
                         out[pl.ds(v * ROW + cell, NT, stride=NR), :] = result[:, :W]
             return 0
 
-        lax.fori_loop(0, (LINES - 2 * first + group - 1) // group, line_step, 0)
-
-
-def main_kernel(
-    low, high, given_ghosts, ordered, lines, below, above, from_left, from_right, matrix, flow, out, *scratch
-):
+        lax.fori_loop(0, (LINES - 2 * first + group - 1) // group, line_step, 0, unroll=True)
+
+
+def main_kernel(low, high, given_ghosts, ordered, lines, from_partner, from_chip, matrix, flow, out, *scratch):
     t, _ = place()
 
     @pl.when(t < PARTS)
     def _():
-        bulk(lines, below, above, from_left, from_right, matrix, flow, out, *scratch[:3])
+        bulk(lines, from_partner, from_chip, high, matrix, flow, out, *scratch[:3])
 
     @pl.when(t >= PARTS)
     def _():
@@ -513,31 +528,26 @@
         name="pack",
     )(state[0], far_field[0], face_index, face_weight[0])
     lines = lax.all_to_all(shares, "tm", 0, 0, tiled=True).reshape(NT * NR, W)
-    zone, ends_up, ends_down = pl.pallas_call(
+    to_partner, to_chip = pl.pallas_call(
+        ends_kernel,
+        out_shape=[f32(ENDS * NT, W)] * 2,
+        in_specs=[VMEM],
+        out_specs=[VMEM] * 2,
+        compiler_params=params(16),
+        name="ends",
+    )(lines)
+    pairs = [(i, i + 1) for i in range(1, PARTS - 1, 2)]
+    from_chip = lax.ppermute(to_chip, "tm", pairs + [(b, a) for a, b in pairs])
+    from_partner = lax.ppermute(to_partner, "tm", [(i, i ^ 1) for i in range(PARTS)])
+    zone = pl.pallas_call(
         zone_kernel,
-        out_shape=[f32(BLOCKS, HALF_ZONE * NT, W)] + [f32(ENDS * NT, W)] * 2,
-        in_specs=[VMEM],
-        out_specs=[VMEM] * 3,
+        out_shape=f32(BLOCKS, HALF_ZONE * NT, W),
+        in_specs=[VMEM] * 3,
+        out_specs=VMEM,
         compiler_params=params(16),
         name="zone",
-    )(lines)
+    )(lines, from_partner, from_chip)
     high = lax.all_to_all(zone, "block", 0, 0, tiled=True)
-    below = lax.ppermute(ends_up, "tm", [(i, i + 1) for i in range(PARTS - 1)])
-    above = lax.ppermute(ends_down, "tm", [(i + 1, i) for i in range(PARTS - 1)])
-    left, right = pl.pallas_call(
-        edge_kernel,
-        out_shape=[f32(EDGE_PACKS * NT, W)] * 2,
-        in_specs=[VMEM] * 3,
-        out_specs=[VMEM] * 2,
-        compiler_params=params(16),
-        name="edges",
-    )(lines, below, above)
-    rights = [
-        (i * BLOCKS + b, i * BLOCKS + b // HALF * HALF + (b + 1) % HALF) for i in range(PARTS) for b in range(BLOCKS)
-    ]
-    from_left = lax.ppermute(right, ("tm", "block"), rights)
-    from_right = lax.ppermute(left, ("tm", "block"), [(b, a) for a, b in rights])
-    high, from_left, from_right = lax.optimization_barrier((high, from_left, from_right))
     low = lax.ppermute(high, "tm", [(PARTS, PARTS + 1)])
     given_ghosts, ordered = pl.pallas_call(
         start_kernel,
@@ -554,7 +564,7 @@
     done = pl.pallas_call(
         main_kernel,
         out_shape=f32(NT * NR, W),
-        in_specs=[VMEM] * 10 + [SMEM],
+        in_specs=[VMEM] * 8 + [SMEM],
         out_specs=VMEM,
         scratch_shapes=[grid] * 3
         + [lines_of] * 2
@@ -563,7 +573,7 @@
         compiler_params=params(32),
         cost_estimate=cost(8 * 10**9, 64 << 20),
         name="main",
-    )(low, high, given_ghosts, ordered, lines, below, above, from_left, from_right, matrix, mean_flow)
+    )(low, high, given_ghosts, ordered, lines, from_partner, from_chip, matrix, mean_flow)
     done = lax.all_to_all(done.reshape(NT, NR, W), "tm", 0, 0, tiled=True)
     result = pl.pallas_call(
         unpack_kernel,

time: 107 us -> 106 us (level)
  blocking collectives: 57.9 us -> 84.8 us
  starting transfers between devices: 19.4 us -> 5.27 us
  waiting for transfers between devices: 14.6 us -> 4.04 us
  Pallas kernels: 12.3 us -> 10.4 us
  local copies, waits for them, and re-layouts: 2.09 us -> 0.88 us
    all_to_all x0 -> x1, blocking collectives: none -> 26.4 us  [shards(): high = lax.all_to_all(zone, 'block', 0, 0, tiled=True)]
    ppermute x4 -> x2, waiting for transfers between devices: 14.6 us -> 4.03 us  [the longest x1 4.03 us: shards(): from_chip = lax.ppermute(to_chip, 'tm', pairs + [(b, a) for a, b in pairs])]
    ppermute x4 -> x2, starting transfers between devices: 11.9 us -> 4.51 us  [the longest x1 2.59 us: shards(): from_chip = lax.ppermute(to_chip, 'tm', pairs + [(b, a) for a, b in pairs])]
    all_to_all x1 -> x0, starting transfers between devices: 6.75 us -> none  [shards(): high = lax.all_to_all(zone, 'block', 0, 0, tiled=True)]
    pallas_call x1, Pallas kernels: 8.72 us -> 6.93 us  [shards(): pl.pallas_call(main_kernel, out_shape=f32(NT * NR, W), in_specs=[VMEM] *...]
    unnamed x6 -> x4, local copies, waits for them, and re-layouts: 2.09 us -> 0.88 us
  transfers between devices with their start and end apart: 6 -> 3, of which waited for: 3 -> 1; matrix products, arithmetic and copies ran while one was open for 0% -> 0% of each run, Pallas kernels for 1% -> 0%
where the time goes in v7:
time: 106 us
  blocking collectives  84.8 us (80%)
  Pallas kernels  10.4 us (10%)
  starting transfers between devices  5.27 us (5%)
  waiting for transfers between devices  4.04 us (4%)
    all_to_all x1, blocking collectives, shards(): lines = lax.all_to_all(shares, 'tm', 0, 0, tiled=True).reshape(NT * NR, W)  30.2 us
    all_to_all x1, blocking collectives, shards(): done = lax.all_to_all(done.reshape(NT, NR, W), 'tm', 0, 0, tiled=True)  28.2 us
    all_to_all x1, blocking collectives, shards(): high = lax.all_to_all(zone, 'block', 0, 0, tiled=True)  26.4 us
    pallas_call x1, Pallas kernels, shards(): pl.pallas_call(main_kernel, out_shape=f32(NT * NR, W), in_specs=[VMEM] *...  6.93 us
    ppermute x1, waiting for transfers between devices, shards(): from_chip = lax.ppermute(to_chip, 'tm', pairs + [(b, a) for a, b in pairs])  4.03 us
    ppermute x1, starting transfers between devices, shards(): from_chip = lax.ppermute(to_chip, 'tm', pairs + [(b, a) for a, b in pairs])  2.59 us
  transfers between devices with their start and end apart: 3, of which 1 were waited for; matrix products, arithmetic and copies ran while one was open for 0% of the time, Pallas kernels for 0%

profile of v7, /device:TPU:1, one launch (start us, length us, event | category | flops | bytes accessed | tf_op | source)
XLA Modules:
  0.0 105.5 jit_solution(6824454661476990543)
XLA Ops:
  0.0 2.0 %pack.1 = f32[16,80,128]{2,1,0:T(8,128)} custom-call(f32[4,256,128]{2,1,0:T(8,128)} %bitcast.12, f32[4,128]{1,0:T(4,128)} %bitcast.13, s32[1,128]{1,0:T(1,128)} %index_in.1, f32[4,128]{1,0:T(4,128)} %bitcast.14), custom_call_target="tpu_custom_call" | custom-call | tf_op jit(solution)/shard_map/pack/pallas_call | solution.py:515
  2.0 30.2 %all_to_all.15 = f32[16,80,128]{2,1,0:T(8,128)S(1)} all-to-all(f32[16,80,128]{2,1,0:T(8,128)} %pack.1), channel_id=1, replica_groups=mesh['tm'=16,'block'=16] {'tm'}, dimensions={0} | all-to-all | bytes 1310720 | tf_op jit(solution)/shard_map/all_to_all | solution.py:530
  32.2 0.1 ends.1
  32.3 1.9 %collective-permute-start = (f32[320,128]{1,0:T(8,128)S(1)}, f32[320,128]{1,0:T(8,128)S(1)}, u32[]{:S(2)}, u32[]{:S(2)}) collective-permute-start(f32[320,128]{1,0:T(8,128)S(1)} %get-tuple-element.9), channel_id=1, source_target_pairs={{0,16},{16,0},{32,48},{48,32},{64,80},{80,64},{96,112},{112,96},{1... | collective-permute-start | bytes 491528 | tf_op jit(solution)/shard_map/ppermute | solution.py:541
  34.2 2.6 %collective-permute-start.1 = (f32[320,128]{1,0:T(8,128)S(1)}, f32[320,128]{1,0:T(8,128)S(1)}, u32[]{:S(2)}, u32[]{:S(2)}) collective-permute-start(f32[320,128]{1,0:T(8,128)S(1)} %get-tuple-element.10), channel_id=1, source_target_pairs={{16,32},{48,64},{80,96},{112,128},{144,160},{176,192},{32,16},{64,... | collective-permute-start | bytes 491528 | tf_op jit(solution)/shard_map/ppermute | solution.py:540
  36.8 0.0 collective-permute-done.from_partner
  36.8 4.0 %collective-permute-done.1.from_chip = f32[320,128]{1,0:T(8,128)S(1)} collective-permute-done((f32[320,128]{1,0:T(8,128)S(1)}, f32[320,128]{1,0:T(8,128)S(1)}, u32[]{:S(2)}, u32[]{:S(2)}) %collective-permute-start.1) | collective-permute-done | bytes 163872 | tf_op jit(solution)/shard_map/ppermute | solution.py:540
  40.9 0.5 zone.1
  41.4 26.4 %all_to_all.16.high = f32[16,208,128]{2,1,0:T(8,128)S(1)} all-to-all(f32[16,208,128]{2,1,0:T(8,128)S(1)} %zone.1), channel_id=1, replica_groups=mesh['tm'=16,'block'=16] {'block'}, dimensions={0} | all-to-all | bytes 3407872 | tf_op jit(solution)/shard_map/all_to_all | solution.py:550
  67.8 0.8 collective-permute-start.2
  68.6 0.0 copy-start
  68.6 0.0 copy-start.1
  68.7 0.0 collective-permute-done.2.low
  68.7 0.6 copy-done
  69.3 0.3 copy-done.1
  69.5 6.9 %main.1 = f32[1280,128]{1,0:T(8,128)S(1)} custom-call(f32[16,208,128]{2,1,0:T(8,128)S(1)} %collective-permute-done.2.low, f32[16,208,128]{2,1,0:T(8,128)S(1)} %all_to_all.16.high, f32[2,4,8,16,128]{4,3,2,1,0:T(8,128)S(1)} %get-tuple-element.11.given_ghosts, f32[2,4,128,128]{3,2,1,0:T(8,128)S(1)} %get-tuple-element.12.ordered, f32[1280,128]{1,0:T(8,128)S(1)} %bitcast.9, ...), custom_call_target="tpu_custom_call" | custom-call | flops 8000000000 | bytes 67108864 | tf_op jit(solution)/shard_map/main/pallas_call | solution.py:564
  76.5 28.2 %all_to_all.17.shares = f32[16,80,128]{2,1,0:T(8,128)S(1)} all-to-all(f32[16,80,128]{2,1,0:T(8,128)S(1)} %bitcast.11), channel_id=1, replica_groups=mesh['tm'=16,'block'=16] {'tm'}, dimensions={0} | all-to-all | bytes 1310720 | tf_op jit(solution)/shard_map/all_to_all | solution.py:577
  104.7 0.8 unpack.1
  (1 shorter events, 0.0 us)
Async XLA Ops:
  32.3 4.5 %collective-permute-start = (f32[320,128]{1,0:T(8,128)S(1)}, f32[320,128]{1,0:T(8,128)S(1)}, u32[]{:S(2)}, u32[]{:S(2)}) collective-permute-start(f32[320,128]{1,0:T(8,128)S(1)} %get-tuple-element.9), channel_id=1, source_target_pairs={{0,16},{16,0},{32,48},{48,32},{64,80},{80,64},{96,112},{112,96},{1... | collective-permute-start | bytes 491528 | tf_op jit(solution)/shard_map/ppermute | solution.py:541
  34.2 6.6 %collective-permute-start.1 = (f32[320,128]{1,0:T(8,128)S(1)}, f32[320,128]{1,0:T(8,128)S(1)}, u32[]{:S(2)}, u32[]{:S(2)}) collective-permute-start(f32[320,128]{1,0:T(8,128)S(1)} %get-tuple-element.10), channel_id=1, source_target_pairs={{16,32},{48,64},{80,96},{112,128},{144,160},{176,192},{32,16},{64,... | collective-permute-start | bytes 491528 | tf_op jit(solution)/shard_map/ppermute | solution.py:540
  67.8 0.8 collective-permute-start.2
  68.6 0.7 copy-start
  68.6 0.9 copy-start.1
